TPU v7x, 512 devices: a whole 4x4x16 slice. The times are simulated.
512 devices in a mesh: seq: 64 (over z_hi, y, x, core), chan: 8 (over z_lo).
Axes of the slice: x: 4, y: 4, z: 16 (z_hi: 2, z_lo: 8; z = z_hi * 8 + z_lo), core: 2. Of those that a mesh axis runs over, the one named last changes fastest.
Arguments:
- query_in: bfloat16 [2048, 8192], P('chan', 'seq'), may hold values from -6 to 6
- key_in: bfloat16 [2048, 8192], P('chan', 'seq'), may hold values from -6 to 6
- value_in: bfloat16 [2048, 8192], P('chan', 'seq'), may hold values from -6 to 6
- short_weight: float32 [3, 7, 2048], P(None, None, 'chan'), may hold values from -2 to 2
- residue: float32 [2048, 16], P(('chan', 'seq')), may hold values from -1.5 to 1.5
- log_rate: float32 [2048, 16], P(('chan', 'seq')), may hold values from -13 to -3.2
- grad_out: bfloat16 [2048, 8192], P('chan', 'seq'), may hold values from -6 to 6
Outputs:
- output: bfloat16 [2048, 8192], P('chan', 'seq')
- grad_query: bfloat16 [2048, 8192], P('chan', 'seq')
- grad_key: bfloat16 [2048, 8192], P('chan', 'seq')
- grad_value: bfloat16 [2048, 8192], P('chan', 'seq')
- grad_short: float32 [3, 7, 2048], P(None, None, 'chan')
- grad_residue: float32 [2048, 16], P(('chan', 'seq'))
- grad_log_rate: float32 [2048, 16], P(('chan', 'seq'))
All inputs are finite; a program needn't handle non-finite values.
Results may differ from a plain program's by a relative error of at most 0.008.
Values may be sent and summed in bfloat16 or wider, within the bound.
No kernel may reach another device: no remote copies, remote signals or barrier semaphores. Data moves between devices by JAX's collectives and lax.ppermute only.
A program may use at most 64 MiB of HBM per device.

v0:
```python
import math

import jax
import jax.numpy as jnp
from jax import lax
from jax.sharding import PartitionSpec as P


def shifted(shard, axis, by):
    count = lax.axis_size(axis)
    pairs = [(i, i + by) for i in range(count) if 0 <= i + by < count]
    return lax.ppermute(shard, axis, pairs)


def dft_table(length, sign):
    counter = jnp.arange(length, dtype=jnp.int32)
    product = counter[:, None] * counter[None, :] % length
    angle = product.astype(jnp.float32) * (sign * 2.0 * math.pi / length)
    return (jnp.cos(angle), jnp.sin(angle))


def complex_dot(real_part, imag_part, table_real, table_imag):
    highest = lax.Precision.HIGHEST
    out_real = jnp.matmul(real_part, table_real, precision=highest) - jnp.matmul(
        imag_part, table_imag, precision=highest
    )
    out_imag = jnp.matmul(real_part, table_imag, precision=highest) + jnp.matmul(
        imag_part, table_real, precision=highest
    )
    return (out_real, out_imag)


def transform(real_part, imag_part, sign):
    length = real_part.shape[-1]
    if length <= 256 or length % 128 != 0:
        table_real, table_imag = dft_table(length, sign)
        return complex_dot(real_part, imag_part, table_real, table_imag)
    outer = 128
    inner = length // outer
    leading = real_part.shape[:-1]
    split_real = jnp.swapaxes(real_part.reshape(leading + (inner, outer)), -1, -2)
    split_imag = jnp.swapaxes(imag_part.reshape(leading + (inner, outer)), -1, -2)
    part_real, part_imag = transform(split_real, split_imag, sign)
    first_index = jnp.arange(outer, dtype=jnp.int32)[:, None]
    second_index = jnp.arange(inner, dtype=jnp.int32)[None, :]
    angle = (first_index * second_index % length).astype(jnp.float32) * (
        sign * 2.0 * math.pi / length
    )
    twist_real = jnp.cos(angle)
    twist_imag = jnp.sin(angle)
    turned_real = part_real * twist_real - part_imag * twist_imag
    turned_imag = part_real * twist_imag + part_imag * twist_real
    table_real, table_imag = dft_table(outer, sign)
    highest = lax.Precision.HIGHEST
    out_real = jnp.einsum(
        "...nk,nl->...lk", turned_real, table_real, precision=highest
    ) - jnp.einsum("...nk,nl->...lk", turned_imag, table_imag, precision=highest)
    out_imag = jnp.einsum(
        "...nk,nl->...lk", turned_real, table_imag, precision=highest
    ) + jnp.einsum("...nk,nl->...lk", turned_imag, table_real, precision=highest)
    return (out_real.reshape(leading + (length,)), out_imag.reshape(leading + (length,)))


def spectrum(signal):
    length = signal.shape[1]
    padded = jnp.pad(signal.astype(jnp.float32), ((0, 0), (0, length)))
    return transform(padded, jnp.zeros_like(padded), -1.0)


def mirrored(values):
    return jnp.roll(jnp.flip(values, -1), 1, -1)


def paired_spectra(first, second):
    length = first.shape[1]
    first_pad = jnp.pad(first, ((0, 0), (0, length)))
    second_pad = jnp.pad(second.astype(jnp.float32), ((0, 0), (0, length)))
    joint_real, joint_imag = transform(first_pad, second_pad, -1.0)
    mirror_real = mirrored(joint_real)
    mirror_imag = mirrored(joint_imag)
    first_spec = (0.5 * (joint_real + mirror_real), 0.5 * (joint_imag - mirror_imag))
    second_spec = (0.5 * (joint_imag + mirror_imag), -0.5 * (joint_real - mirror_real))
    return (first_spec, second_spec)


def to_time(spec_pair, length):
    real_part, imag_part = spec_pair
    back_real, back_imag = transform(real_part, imag_part, 1.0)
    return back_real[:, :length] / real_part.shape[-1]


def paired_time(first_spec, second_spec, length):
    joint_real = first_spec[0] - second_spec[1]
    joint_imag = first_spec[1] + second_spec[0]
    back_real, back_imag = transform(joint_real, joint_imag, 1.0)
    total_len = joint_real.shape[-1]
    return (back_real[:, :length] / total_len, back_imag[:, :length] / total_len)


def spectral_product(first, second, conjugate):
    first_real, first_imag = first
    second_real, second_imag = second
    if conjugate:
        second_imag = -second_imag
    return (
        first_real * second_real - first_imag * second_imag,
        first_real * second_imag + first_imag * second_real,
    )


def modal_filter(residue, log_rate, length):
    decay_rate = jnp.exp(log_rate)
    offsets = jnp.arange(length).astype(jnp.float32)
    filt = jnp.zeros((residue.shape[0], length), jnp.float32)
    for mode_index in range(residue.shape[1]):
        factor = residue[:, mode_index] * jnp.sqrt(2.0 * decay_rate[:, mode_index])
        filt = filt + factor[:, None] * jnp.exp(-decay_rate[:, mode_index][:, None] * offsets)
    return filt


def modal_grads(filt_grad, residue, log_rate):
    decay_rate = jnp.exp(log_rate)
    offsets = jnp.arange(filt_grad.shape[1]).astype(jnp.float32)
    res_terms = []
    log_terms = []
    for mode_index in range(residue.shape[1]):
        rate_col = decay_rate[:, mode_index][:, None]
        basis = jnp.sqrt(2.0 * rate_col) * jnp.exp(-rate_col * offsets)
        weighted = filt_grad * basis
        res_terms.append(jnp.sum(weighted, axis=1))
        log_terms.append(
            residue[:, mode_index] * jnp.sum(weighted * (0.5 - rate_col * offsets), axis=1)
        )
    return (jnp.stack(res_terms, axis=1), jnp.stack(log_terms, axis=1))


def apply_taps(widened, taps, tok_rows):
    total = jnp.zeros((widened.shape[0], tok_rows), jnp.float32)
    for offset in range(7):
        total = total + taps[offset][:, None] * widened[:, 6 - offset : 6 - offset + tok_rows]
    return total


def taps_back(gradient, following, taps):
    tok_rows = gradient.shape[1]
    widened = jnp.concatenate([gradient, following], axis=1)
    total = jnp.zeros_like(gradient)
    for offset in range(7):
        total = total + taps[offset][:, None] * widened[:, offset : offset + tok_rows]
    return total


def taps_gradient(gradient, widened):
    tok_rows = gradient.shape[1]
    rows_out = [
        jnp.sum(gradient * widened[:, 6 - offset : 6 - offset + tok_rows], axis=1)
        for offset in range(7)
    ]
    return jnp.stack(rows_out, axis=0)


def to_channels(stream):
    return lax.all_to_all(stream, "seq", split_axis=0, concat_axis=1, tiled=True)


def to_tokens(stream):
    return lax.all_to_all(stream, "seq", split_axis=1, concat_axis=0, tiled=True)


def local(query_in, key_in, value_in, short_weight, residue, log_rate, grad_out):
    tok_rows = query_in.shape[1]
    length = tok_rows * lax.axis_size("seq")
    scale = 1.0 / math.sqrt(length)
    tails = shifted((query_in[:, -6:], key_in[:, -6:], value_in[:, -6:]), "seq", 1)
    query_wide = jnp.concatenate([tails[0], query_in], axis=1).astype(jnp.float32)
    key_wide = jnp.concatenate([tails[1], key_in], axis=1).astype(jnp.float32)
    value_wide = jnp.concatenate([tails[2], value_in], axis=1).astype(jnp.float32)
    query_hat = apply_taps(query_wide, short_weight[0], tok_rows)
    key_hat = apply_taps(key_wide, short_weight[1], tok_rows)
    value_hat = apply_taps(value_wide, short_weight[2], tok_rows)
    mixed = (key_hat * value_hat).astype(jnp.bfloat16)
    grad_up = grad_out.astype(jnp.float32)
    grad_mixed = (grad_up * query_hat).astype(jnp.bfloat16)
    mixed_cols = to_channels(mixed)
    filt = modal_filter(residue, log_rate, length)
    spec_filter, spec_mixed = paired_spectra(filt, mixed_cols)
    long_out = to_time(spectral_product(spec_mixed, spec_filter, False), length).astype(
        jnp.bfloat16
    )
    conv_out = to_tokens(long_out)
    grad_cols = to_channels(grad_mixed)
    spec_grad = spectrum(grad_cols)
    long_grad, filt_grad = paired_time(
        spectral_product(spec_grad, spec_filter, True),
        spectral_product(spec_grad, spec_mixed, True),
        length,
    )
    conv_grad = to_tokens(long_grad.astype(jnp.bfloat16))
    grad_res, grad_log = modal_grads(filt_grad, residue, log_rate)
    conv_wide = conv_out.astype(jnp.float32)
    conv_grad_wide = conv_grad.astype(jnp.float32)
    output = (query_hat * conv_wide).astype(jnp.bfloat16)
    grad_q = grad_up * conv_wide
    grad_k = conv_grad_wide * value_hat
    grad_v = conv_grad_wide * key_hat
    heads = shifted((grad_q[:, :6], grad_k[:, :6], grad_v[:, :6]), "seq", -1)
    grad_query = taps_back(grad_q, heads[0], short_weight[0]).astype(jnp.bfloat16)
    grad_key = taps_back(grad_k, heads[1], short_weight[1]).astype(jnp.bfloat16)
    grad_value = taps_back(grad_v, heads[2], short_weight[2]).astype(jnp.bfloat16)
    local_terms = jnp.stack(
        [
            taps_gradient(grad_q, query_wide),
            taps_gradient(grad_k, key_wide),
            taps_gradient(grad_v, value_wide),
        ],
        axis=0,
    )
    grad_short = lax.psum(local_terms, "seq") * scale
    return (
        output,
        grad_query,
        grad_key,
        grad_value,
        grad_short,
        grad_res * scale,
        grad_log * scale,
    )


def solution(mesh):
    return jax.shard_map(
        local,
        mesh=mesh,
        in_specs=(
            P("chan", "seq"),
            P("chan", "seq"),
            P("chan", "seq"),
            P(None, None, "chan"),
            P(("chan", "seq"), None),
            P(("chan", "seq"), None),
            P("chan", "seq"),
        ),
        out_specs=(
            P("chan", "seq"),
            P("chan", "seq"),
            P("chan", "seq"),
            P("chan", "seq"),
            P(None, None, "chan"),
            P(("chan", "seq"), None),
            P(("chan", "seq"), None),
        ),
        check_vma=False,
    )
```

profile of v0, /device:TPU:63, one launch (start us, length us, event | category | flops | bytes accessed | tf_op | source)
XLA Modules:
  0.0 777.7 jit_solution(15686201260251525525)
XLA Ops:
  0.6 1.0 slice.511
  1.6 14.8 %collective-permute-start.1 = (bf16[256,6]{1,0:T(8,128)(2,1)S(1)}, bf16[256,6]{1,0:T(8,128)(2,1)S(1)}, u32[]{:S(2)}, u32[]{:S(2)}) collective-permute-start(bf16[256,6]{1,0:T(8,128)(2,1)S(1)} %slice.511), channel_id=1, source_target_pairs={{0,8},{8,16},{16,24},{24,32},{32,40},{40,48},{48,56},{56,64},{64,7... | collective-permute-start | bytes 9224 | tf_op jit(solution)/shard_map/ppermute | solution.py:12
  16.5 1.9 collective-permute-start.2
  18.6 3.5 collective-permute-start
  28.4 1.4 multiply_add_fusion.6
  32.7 0.7 copy-done.4
  33.8 1.6 multiply_convert_fusion.1
  35.4 8.3 %all-to-all-start = ((bf16[64,4,128]{2,1,0:T(4,128)(2,1)}), bf16[64,4,128]{2,1,0:T(4,128)(2,1)S(1)}, u32[]{:S(2)}, u32[]{:S(2)}) async-start(bf16[64,4,128]{2,1,0:T(4,128)(2,1)} %bitcast.57), calls=%async_computation | async-start | bytes 131072 | tf_op jit(solution)/shard_map/all_to_all | solution.py:163
  44.5 1.2 fusion.32
  45.7 11.6 %all-to-all-done = bf16[64,4,128]{2,1,0:T(4,128)(2,1)S(1)} async-done(((bf16[64,4,128]{2,1,0:T(4,128)(2,1)}), bf16[64,4,128]{2,1,0:T(4,128)(2,1)S(1)}, u32[]{:S(2)}, u32[]{:S(2)}) %all-to-all-start) | async-done | bytes 65568 | tf_op jit(solution)/shard_map/all_to_all | solution.py:163
  57.3 8.1 %all-to-all-start.2 = ((bf16[64,4,128]{2,1,0:T(4,128)(2,1)}), bf16[64,4,128]{2,1,0:T(4,128)(2,1)S(1)}, u32[]{:S(2)}, u32[]{:S(2)}) async-start(bf16[64,4,128]{2,1,0:T(4,128)(2,1)} %bitcast.79), calls=%async_computation.2 | async-start | bytes 131072 | tf_op jit(solution)/shard_map/all_to_all | solution.py:163
  67.3 0.7 convolution_subtract_fusion.6
  68.0 0.7 fusion.147
  71.3 7.6 all-to-all-done.2
  82.1 1.4 fusion.143
  83.5 11.1 %reverse.4 = f32[4,16384]{1,0:T(4,128)S(1)} reverse(f32[4,16384]{1,0:T(4,128)S(1)} %bitcast.444), dimensions={1} | reverse | bytes 524288
  94.8 11.3 %reverse.5 = f32[4,16384]{1,0:T(4,128)S(1)} reverse(f32[4,16384]{1,0:T(4,128)S(1)} %bitcast.445), dimensions={1} | reverse | bytes 524288
  108.1 0.8 subtract_add_fusion
  109.0 0.7 fusion.13
  109.7 0.7 fusion.11
  110.5 0.7 fusion.19
  111.2 0.7 fusion.17
  111.9 0.7 convolution_subtract_fusion.1
  112.7 0.7 convolution_add_fusion.1
  116.4 1.4 multiply_reduce_fusion.5
  119.9 0.7 copy-done.59
  121.4 1.2 multiply_reduce_fusion.3
  122.7 0.7 copy-done.57
  125.6 1.2 multiply_reduce_fusion.2
  129.6 1.2 multiply_reduce_fusion.1
  137.2 1.0 convolution_subtract_fusion.5
  138.2 0.7 convolution_add_fusion.4
  138.9 0.7 fusion.28
  139.6 0.7 fusion.4
  141.1 10.0 %all-to-all-start.1 = ((bf16[4,64,128]{2,0,1:T(4,128)(2,1)}), bf16[4,64,128]{2,0,1:T(4,128)(2,1)S(1)}, u32[]{:S(2)}, u32[]{:S(2)}) async-start(bf16[4,64,128]{2,0,1:T(4,128)(2,1)} %fusion.119), calls=%async_computation.1 | async-start | bytes 131072 | tf_op jit(solution)/shard_map/all_to_all | solution.py:167
  154.3 10.5 %all-to-all-done.1 = bf16[4,64,128]{2,0,1:T(4,128)(2,1)S(1)} async-done(((bf16[4,64,128]{2,0,1:T(4,128)(2,1)}), bf16[4,64,128]{2,0,1:T(4,128)(2,1)S(1)}, u32[]{:S(2)}, u32[]{:S(2)}) %all-to-all-start.1) | async-done | bytes 65568 | tf_op jit(solution)/shard_map/all_to_all | solution.py:167
  164.8 7.8 %all-to-all-start.3 = ((bf16[4,64,128]{2,0,1:T(4,128)(2,1)}), bf16[4,64,128]{2,0,1:T(4,128)(2,1)S(1)}, u32[]{:S(2)}, u32[]{:S(2)}) async-start(bf16[4,64,128]{2,0,1:T(4,128)(2,1)} %fusion.120), calls=%async_computation.3 | async-start | bytes 131072 | tf_op jit(solution)/shard_map/all_to_all | solution.py:167
  174.0 1.1 multiply_reduce_fusion.30
  175.1 11.1 %all-to-all-done.3 = bf16[4,64,128]{2,0,1:T(4,128)(2,1)S(1)} async-done(((bf16[4,64,128]{2,0,1:T(4,128)(2,1)}), bf16[4,64,128]{2,0,1:T(4,128)(2,1)S(1)}, u32[]{:S(2)}, u32[]{:S(2)}) %all-to-all-start.3) | async-done | bytes 65568 | tf_op jit(solution)/shard_map/all_to_all | solution.py:167
  186.3 1.0 multiply_reduce_fusion.16
  187.4 553.3 %psum.7 = f32[3,7,256]{2,1,0:T(8,128)S(1)} all-reduce(f32[3,7,256]{2,1,0:T(8,128)S(1)} %pad_maximum_fusion.3), channel_id=1, replica_groups=mesh['seq'=64,'chan'=8] {'seq'}, use_global_device_ids=true, to_apply=%region_21.22 | all-reduce | flops 5376 | bytes 43008 | tf_op jit(solution)/shard_map/psum | solution.py:218
  740.6 1.9 collective-permute-start.5
  743.2 1.9 collective-permute-start.4
  745.1 1.9 collective-permute-start.3
  747.1 26.0 %collective-permute-done.5 = f32[256,6]{1,0:T(8,128)S(1)} collective-permute-done((f32[256,6]{1,0:T(8,128)S(1)}, f32[256,6]{1,0:T(8,128)S(1)}, u32[]{:S(2)}, u32[]{:S(2)}) %collective-permute-start.5) | collective-permute-done | bytes 6176 | tf_op jit(solution)/shard_map/ppermute | solution.py:12
  773.1 1.3 fusion.37
  774.5 1.3 fusion.54
  775.9 1.3 fusion.71
  (388 shorter events, 42.9 us)
Async XLA Ops:
  0.6 15.8 %copy-start.5 = (bf16[256,128]{1,0:T(8,128)(2,1)S(1)}, bf16[256,128]{1,0:T(8,128)(2,1)}, u32[]{:S(2)}) copy-start(bf16[256,128]{1,0:T(8,128)(2,1)} %param.9) | copy-start | bytes 196612
  1.6 16.9 %copy-start.6 = (bf16[256,128]{1,0:T(8,128)(2,1)S(1)}, bf16[256,128]{1,0:T(8,128)(2,1)}, u32[]{:S(2)}) copy-start(bf16[256,128]{1,0:T(8,128)(2,1)} %param.7) | copy-start | bytes 196612
  1.6 31.1 %collective-permute-start.1 = (bf16[256,6]{1,0:T(8,128)(2,1)S(1)}, bf16[256,6]{1,0:T(8,128)(2,1)S(1)}, u32[]{:S(2)}, u32[]{:S(2)}) collective-permute-start(bf16[256,6]{1,0:T(8,128)(2,1)S(1)} %slice.511), channel_id=1, source_target_pairs={{0,8},{8,16},{16,24},{24,32},{32,40},{40,48},{48,56},{56,64},{64,7... | collective-permute-start | bytes 9224 | tf_op jit(solution)/shard_map/ppermute | solution.py:12
  16.5 17.0 %collective-permute-start.2 = (bf16[256,6]{1,0:T(8,128)(2,1)S(1)}, bf16[256,6]{1,0:T(8,128)(2,1)S(1)}, u32[]{:S(2)}, u32[]{:S(2)}) collective-permute-start(bf16[256,6]{1,0:T(8,128)(2,1)S(1)} %slice.526), channel_id=1, source_target_pairs={{0,8},{8,16},{16,24},{24,32},{32,40},{40,48},{48,56},{56,64},{64,7... | collective-permute-start | bytes 9224 | tf_op jit(solution)/shard_map/ppermute | solution.py:12
  18.6 25.1 %collective-permute-start = (bf16[256,6]{1,0:T(8,128)(2,1)S(1)}, bf16[256,6]{1,0:T(8,128)(2,1)S(1)}, u32[]{:S(2)}, u32[]{:S(2)}) collective-permute-start(bf16[256,6]{1,0:T(8,128)(2,1)S(1)} %slice.464), channel_id=1, source_target_pairs={{0,8},{8,16},{16,24},{24,32},{32,40},{40,48},{48,56},{56,64},{64,7... | collective-permute-start | bytes 9224 | tf_op jit(solution)/shard_map/ppermute | solution.py:12
  23.6 10.0 %copy-start.12 = (f32[1,1,256]{2,1,0:T(1,128)}, f32[1,1,256]{2,1,0:T(1,128)S(1)}, u32[]{:S(2)}) copy-start(f32[1,1,256]{2,1,0:T(1,128)S(1)} %get-tuple-element.134) | copy-start | bytes 3076
  23.6 10.0 %copy-start.14 = (f32[1,1,256]{2,1,0:T(1,128)}, f32[1,1,256]{2,1,0:T(1,128)S(1)}, u32[]{:S(2)}) copy-start(f32[1,1,256]{2,1,0:T(1,128)S(1)} %get-tuple-element.135) | copy-start | bytes 3076
  23.6 10.0 %copy-start.16 = (f32[1,1,256]{2,1,0:T(1,128)}, f32[1,1,256]{2,1,0:T(1,128)S(1)}, u32[]{:S(2)}) copy-start(f32[1,1,256]{2,1,0:T(1,128)S(1)} %get-tuple-element.136) | copy-start | bytes 3076
  23.6 10.0 %copy-start.18 = (f32[1,1,256]{2,1,0:T(1,128)}, f32[1,1,256]{2,1,0:T(1,128)S(1)}, u32[]{:S(2)}) copy-start(f32[1,1,256]{2,1,0:T(1,128)S(1)} %get-tuple-element.126) | copy-start | bytes 3076
  23.7 10.0 %copy-start.20 = (f32[1,1,256]{2,1,0:T(1,128)}, f32[1,1,256]{2,1,0:T(1,128)S(1)}, u32[]{:S(2)}) copy-start(f32[1,1,256]{2,1,0:T(1,128)S(1)} %get-tuple-element.127) | copy-start | bytes 3076
  23.7 10.0 %copy-start.22 = (f32[1,1,256]{2,1,0:T(1,128)}, f32[1,1,256]{2,1,0:T(1,128)S(1)}, u32[]{:S(2)}) copy-start(f32[1,1,256]{2,1,0:T(1,128)S(1)} %get-tuple-element.128) | copy-start | bytes 3076
  23.7 10.0 %copy-start.24 = (f32[1,1,256]{2,1,0:T(1,128)}, f32[1,1,256]{2,1,0:T(1,128)S(1)}, u32[]{:S(2)}) copy-start(f32[1,1,256]{2,1,0:T(1,128)S(1)} %get-tuple-element.129) | copy-start | bytes 3076
  23.7 10.0 %copy-start.26 = (f32[1,1,256]{2,1,0:T(1,128)}, f32[1,1,256]{2,1,0:T(1,128)S(1)}, u32[]{:S(2)}) copy-start(f32[1,1,256]{2,1,0:T(1,128)S(1)} %get-tuple-element.130) | copy-start | bytes 3076
  23.7 20.1 %copy-start.32 = (f32[1,1,256]{2,1,0:T(1,128)}, f32[1,1,256]{2,1,0:T(1,128)S(1)}, u32[]{:S(2)}) copy-start(f32[1,1,256]{2,1,0:T(1,128)S(1)} %get-tuple-element.137) | copy-start | bytes 3076
  23.7 20.1 %copy-start.34 = (f32[1,1,256]{2,1,0:T(1,128)}, f32[1,1,256]{2,1,0:T(1,128)S(1)}, u32[]{:S(2)}) copy-start(f32[1,1,256]{2,1,0:T(1,128)S(1)} %get-tuple-element.138) | copy-start | bytes 3076
  23.7 20.1 %copy-start.36 = (f32[1,1,256]{2,1,0:T(1,128)}, f32[1,1,256]{2,1,0:T(1,128)S(1)}, u32[]{:S(2)}) copy-start(f32[1,1,256]{2,1,0:T(1,128)S(1)} %get-tuple-element.139) | copy-start | bytes 3076
  23.7 20.1 %copy-start.38 = (f32[1,1,256]{2,1,0:T(1,128)}, f32[1,1,256]{2,1,0:T(1,128)S(1)}, u32[]{:S(2)}) copy-start(f32[1,1,256]{2,1,0:T(1,128)S(1)} %get-tuple-element.140) | copy-start | bytes 3076
  23.7 20.1 %copy-start.40 = (f32[1,1,256]{2,1,0:T(1,128)}, f32[1,1,256]{2,1,0:T(1,128)S(1)}, u32[]{:S(2)}) copy-start(f32[1,1,256]{2,1,0:T(1,128)S(1)} %get-tuple-element.141) | copy-start | bytes 3076
  23.7 20.1 %copy-start.42 = (f32[1,1,256]{2,1,0:T(1,128)}, f32[1,1,256]{2,1,0:T(1,128)S(1)}, u32[]{:S(2)}) copy-start(f32[1,1,256]{2,1,0:T(1,128)S(1)} %get-tuple-element.142) | copy-start | bytes 3076
  23.8 20.1 %copy-start.44 = (f32[1,1,256]{2,1,0:T(1,128)}, f32[1,1,256]{2,1,0:T(1,128)S(1)}, u32[]{:S(2)}) copy-start(f32[1,1,256]{2,1,0:T(1,128)S(1)} %get-tuple-element.143) | copy-start | bytes 3076
  24.5 9.3 %copy-start.28 = (f32[1,1,256]{2,1,0:T(1,128)}, f32[1,1,256]{2,1,0:T(1,128)S(1)}, u32[]{:S(2)}) copy-start(f32[1,1,256]{2,1,0:T(1,128)S(1)} %get-tuple-element.144) | copy-start | bytes 3076
  24.5 9.3 %copy-start.30 = (f32[1,1,256]{2,1,0:T(1,128)}, f32[1,1,256]{2,1,0:T(1,128)S(1)}, u32[]{:S(2)}) copy-start(f32[1,1,256]{2,1,0:T(1,128)S(1)} %get-tuple-element.145) | copy-start | bytes 3076
  35.4 21.9 %all-to-all-start = ((bf16[64,4,128]{2,1,0:T(4,128)(2,1)}), bf16[64,4,128]{2,1,0:T(4,128)(2,1)S(1)}, u32[]{:S(2)}, u32[]{:S(2)}) async-start(bf16[64,4,128]{2,1,0:T(4,128)(2,1)} %bitcast.57), calls=%async_computation | async-start | bytes 131072 | tf_op jit(solution)/shard_map/all_to_all | solution.py:163
  57.3 21.7 %all-to-all-start.2 = ((bf16[64,4,128]{2,1,0:T(4,128)(2,1)}), bf16[64,4,128]{2,1,0:T(4,128)(2,1)S(1)}, u32[]{:S(2)}, u32[]{:S(2)}) async-start(bf16[64,4,128]{2,1,0:T(4,128)(2,1)} %bitcast.79), calls=%async_computation.2 | async-start | bytes 131072 | tf_op jit(solution)/shard_map/all_to_all | solution.py:163
  116.4 8.5 %copy-start.106 = (f32[4]{0:T(128)S(1)}, f32[4]{0:T(128)}, u32[]{:S(2)}) copy-start(f32[4]{0:T(128)} %get-tuple-element.160) | copy-start | bytes 52
  116.4 8.5 %copy-start.107 = (f32[4]{0:T(128)S(1)}, f32[4]{0:T(128)}, u32[]{:S(2)}) copy-start(f32[4]{0:T(128)} %get-tuple-element.161) | copy-start | bytes 52
  116.4 8.5 %copy-start.108 = (f32[4]{0:T(128)S(1)}, f32[4]{0:T(128)}, u32[]{:S(2)}) copy-start(f32[4]{0:T(128)} %get-tuple-element.163) | copy-start | bytes 52
  116.4 8.6 %copy-start.109 = (f32[4]{0:T(128)S(1)}, f32[4]{0:T(128)}, u32[]{:S(2)}) copy-start(f32[4]{0:T(128)} %get-tuple-element.164) | copy-start | bytes 52
  121.4 7.5 copy-start.102
  121.4 7.5 copy-start.103
  121.4 7.5 copy-start.104
  121.4 7.6 copy-start.105
  141.1 23.6 %all-to-all-start.1 = ((bf16[4,64,128]{2,0,1:T(4,128)(2,1)}), bf16[4,64,128]{2,0,1:T(4,128)(2,1)S(1)}, u32[]{:S(2)}, u32[]{:S(2)}) async-start(bf16[4,64,128]{2,0,1:T(4,128)(2,1)} %fusion.119), calls=%async_computation.1 | async-start | bytes 131072 | tf_op jit(solution)/shard_map/all_to_all | solution.py:167
  164.8 21.4 %all-to-all-start.3 = ((bf16[4,64,128]{2,0,1:T(4,128)(2,1)}), bf16[4,64,128]{2,0,1:T(4,128)(2,1)S(1)}, u32[]{:S(2)}, u32[]{:S(2)}) async-start(bf16[4,64,128]{2,0,1:T(4,128)(2,1)} %fusion.120), calls=%async_computation.3 | async-start | bytes 131072 | tf_op jit(solution)/shard_map/all_to_all | solution.py:167
  175.1 11.1 %copy-start.1 = (f32[256,128]{1,0:T(8,128)S(1)}, f32[256,128]{1,0:T(8,128)}, u32[]{:S(2)}) copy-start(f32[256,128]{1,0:T(8,128)} %get-tuple-element.106) | copy-start | bytes 393220
  186.2 586.8 %copy-start.21 = (f32[1,1,256]{2,1,0:T(1,128)S(1)}, f32[1,1,256]{2,1,0:T(1,128)}, u32[]{:S(2)}) copy-start(f32[1,1,256]{2,1,0:T(1,128)} %copy-done.20) | copy-start | bytes 3076
  186.2 586.8 %copy-start.23 = (f32[1,1,256]{2,1,0:T(1,128)S(1)}, f32[1,1,256]{2,1,0:T(1,128)}, u32[]{:S(2)}) copy-start(f32[1,1,256]{2,1,0:T(1,128)} %copy-done.22) | copy-start | bytes 3076
  186.3 586.8 %copy-start.25 = (f32[1,1,256]{2,1,0:T(1,128)S(1)}, f32[1,1,256]{2,1,0:T(1,128)}, u32[]{:S(2)}) copy-start(f32[1,1,256]{2,1,0:T(1,128)} %copy-done.24) | copy-start | bytes 3076
  186.3 586.8 %copy-start.27 = (f32[1,1,256]{2,1,0:T(1,128)S(1)}, f32[1,1,256]{2,1,0:T(1,128)}, u32[]{:S(2)}) copy-start(f32[1,1,256]{2,1,0:T(1,128)} %copy-done.26) | copy-start | bytes 3076
  186.3 586.8 %copy-start.29 = (f32[1,1,256]{2,1,0:T(1,128)S(1)}, f32[1,1,256]{2,1,0:T(1,128)}, u32[]{:S(2)}) copy-start(f32[1,1,256]{2,1,0:T(1,128)} %copy-done.28) | copy-start | bytes 3076
  186.3 586.8 %copy-start.31 = (f32[1,1,256]{2,1,0:T(1,128)S(1)}, f32[1,1,256]{2,1,0:T(1,128)}, u32[]{:S(2)}) copy-start(f32[1,1,256]{2,1,0:T(1,128)} %copy-done.30) | copy-start | bytes 3076
  740.6 32.4 %collective-permute-start.5 = (f32[256,6]{1,0:T(8,128)S(1)}, f32[256,6]{1,0:T(8,128)S(1)}, u32[]{:S(2)}, u32[]{:S(2)}) collective-permute-start(f32[256,6]{1,0:T(8,128)S(1)} %bitcast.453), channel_id=1, source_target_pairs={{8,0},{16,8},{24,16},{32,24},{40,32},{48,40},{56,48},{64,56},{72,6... | collective-permute-start | bytes 18440 | tf_op jit(solution)/shard_map/ppermute | solution.py:12
  743.2 31.3 %collective-permute-start.4 = (f32[256,6]{1,0:T(8,128)S(1)}, f32[256,6]{1,0:T(8,128)S(1)}, u32[]{:S(2)}, u32[]{:S(2)}) collective-permute-start(f32[256,6]{1,0:T(8,128)S(1)} %bitcast.452), channel_id=1, source_target_pairs={{8,0},{16,8},{24,16},{32,24},{40,32},{48,40},{56,48},{64,56},{72,6... | collective-permute-start | bytes 18440 | tf_op jit(solution)/shard_map/ppermute | solution.py:12
  745.1 28.0 %copy-start.19 = (f32[1,1,256]{2,1,0:T(1,128)S(1)}, f32[1,1,256]{2,1,0:T(1,128)}, u32[]{:S(2)}) copy-start(f32[1,1,256]{2,1,0:T(1,128)} %copy-done.18) | copy-start | bytes 3076
  745.1 29.4 %copy-start.13 = (f32[1,1,256]{2,1,0:T(1,128)S(1)}, f32[1,1,256]{2,1,0:T(1,128)}, u32[]{:S(2)}) copy-start(f32[1,1,256]{2,1,0:T(1,128)} %copy-done.12) | copy-start | bytes 3076
  745.1 29.4 %copy-start.15 = (f32[1,1,256]{2,1,0:T(1,128)S(1)}, f32[1,1,256]{2,1,0:T(1,128)}, u32[]{:S(2)}) copy-start(f32[1,1,256]{2,1,0:T(1,128)} %copy-done.14) | copy-start | bytes 3076
  745.1 29.4 %copy-start.17 = (f32[1,1,256]{2,1,0:T(1,128)S(1)}, f32[1,1,256]{2,1,0:T(1,128)}, u32[]{:S(2)}) copy-start(f32[1,1,256]{2,1,0:T(1,128)} %copy-done.16) | copy-start | bytes 3076
  745.1 30.7 %collective-permute-start.3 = (f32[256,6]{1,0:T(8,128)S(1)}, f32[256,6]{1,0:T(8,128)S(1)}, u32[]{:S(2)}, u32[]{:S(2)}) collective-permute-start(f32[256,6]{1,0:T(8,128)S(1)} %bitcast.451), channel_id=1, source_target_pairs={{8,0},{16,8},{24,16},{32,24},{40,32},{48,40},{56,48},{64,56},{72,6... | collective-permute-start | bytes 18440 | tf_op jit(solution)/shard_map/ppermute | solution.py:12
  (85 other events, 153.7 us)
where the time goes:
time: 785 us; the launch traced here: 778 us
  blocking collectives  553 us (70%)
  waiting for transfers between devices  66.8 us (9%)
  starting transfers between devices  60.2 us (8%)
  local copies, waits for them, and re-layouts  51 us (6%)
  other arithmetic  22.9 us (3%)
  matrix products  20.9 us (3%)
    psum x1, blocking collectives, local(): grad_short = lax.psum(local_terms, 'seq') * scale  553 us
    unnamed x278, local copies, waits for them, and re-layouts  44.1 us
    ppermute x6, waiting for transfers between devices, shifted(): return lax.ppermute(shard, axis, pairs)  26 us
    ppermute x6, starting transfers between devices, shifted(): return lax.ppermute(shard, axis, pairs)  26 us
    all_to_all x2, waiting for transfers between devices, to_tokens(): lax.all_to_all(stream, 'seq', split_axis=1, concat_axis=0, tiled=True)  21.6 us
    all_to_all x2, waiting for transfers between devices, to_channels(): lax.all_to_all(stream, 'seq', split_axis=0, concat_axis=1, tiled=True)  19.2 us
    all_to_all x2, starting transfers between devices, to_tokens(): lax.all_to_all(stream, 'seq', split_axis=1, concat_axis=0, tiled=True)  17.8 us
    all_to_all x2, starting transfers between devices, to_channels(): lax.all_to_all(stream, 'seq', split_axis=0, concat_axis=1, tiled=True)  16.4 us
  transfers between devices with their start and end apart: 10, of which 5 were waited for; matrix products, arithmetic and copies ran while one was open for 3% of the time, Pallas kernels for 0%

commit v1 on v0

v1 whole, which is shorter than its diff:
```python
import math

import jax
import jax.numpy as jnp
from jax import lax
from jax.experimental import pallas as pl
from jax.experimental.pallas import tpu as pltpu
from jax.sharding import PartitionSpec as P

TAPS = 7
MODES = 16
PAD = 8
ROWS_IN = 16
ROWS_OUT = 24
VMEM_LIMIT = 40 * 1024 * 1024


def pack_kernel(query_ref, key_ref, value_ref, grad_ref, send_ref, wide, mixed_rows):
    owners = send_ref.shape[0]
    for stream, ref in enumerate((query_ref, key_ref, value_ref, grad_ref)):
        wide[...] = ref[...].astype(jnp.float32)
        for chan in range(4):
            mixed_rows[pl.ds(stream * 4 + chan, owners, stride=ROWS_IN), :] = wide[
                pl.ds(chan, owners, stride=4), :
            ]
    send_ref[...] = mixed_rows[...].reshape(send_ref.shape).astype(jnp.bfloat16)


def unpack_kernel(recv_ref, out_ref, gq_ref, gk_ref, gv_ref, short_ref, rows, wide):
    owners = recv_ref.shape[0]
    rows[...] = recv_ref[...].reshape(rows.shape).astype(jnp.float32)
    for stream, ref in enumerate((out_ref, gq_ref, gk_ref, gv_ref)):
        for chan in range(4):
            wide[pl.ds(chan, owners, stride=4), :] = rows[
                pl.ds(stream * 4 + chan, owners, stride=ROWS_OUT), :
            ]
        ref[...] = wide[...].astype(jnp.bfloat16)
    for chan in range(4):
        wide[pl.ds(chan, owners, stride=4), :] = (
            rows[pl.ds(16 + chan, owners, stride=ROWS_OUT), :]
            + rows[pl.ds(20 + chan, owners, stride=ROWS_OUT), :]
        )
    short_ref[...] = wide[...].T[: short_ref.shape[0], :]


def main_kernel(
    recv_ref,
    prm_ref,
    send_ref,
    modal_ref,
    raw,
    xt,
    hat,
    mixed,
    gmixed,
    part_y,
    part_z,
    states,
    grads,
    sums,
    out_rows,
):
    chunks = recv_ref.shape[0]
    toks = recv_ref.shape[2]
    lanes = 4 * chunks
    scale = 1.0 / math.sqrt(chunks * toks)
    f32 = jnp.float32
    lane_chunk = lax.broadcasted_iota(jnp.int32, (8, lanes), 1) % chunks

    raw[...] = recv_ref[...].reshape(raw.shape).astype(f32)
    for stream in range(4):
        for pair in range(2):
            first = stream * 4 + 2 * pair
            tile = jnp.concatenate(
                [
                    raw[pl.ds(first, chunks, stride=ROWS_IN), :],
                    raw[pl.ds(first + 1, chunks, stride=ROWS_IN), :],
                ],
                axis=0,
            )
            xt[stream, PAD : PAD + toks, pair * 2 * chunks : (pair + 1) * 2 * chunks] = tile.T
    for stream in range(3):
        tail = pltpu.roll(xt[stream, toks : toks + PAD, :], 1, 1)
        xt[stream, 0:PAD, :] = jnp.where(lane_chunk >= 1, tail, 0.0)

    block = 32
    for start in range(0, toks, block):
        filtered = []
        for stream in range(3):
            total = None
            for tap in range(TAPS):
                row = prm_ref[stream * TAPS + tap : stream * TAPS + tap + 1, :]
                lo = PAD - tap + start
                term = row * xt[stream, lo : lo + block, :]
                total = term if total is None else total + term
            filtered.append(total)
            hat[stream, start : start + block, :] = total
        mixed[start : start + block, :] = (
            (filtered[1] * filtered[2]).astype(jnp.bfloat16).astype(f32)
        )
        gmixed[start : start + block, :] = (
            (xt[3, PAD + start : PAD + start + block, :] * filtered[0])
            .astype(jnp.bfloat16)
            .astype(f32)
        )

    rates = [jnp.exp(prm_ref[24 + 8 * i : 32 + 8 * i, :]) for i in range(2)]
    resid = [prm_ref[40 + 8 * i : 48 + 8 * i, :] for i in range(2)]
    decay = [jnp.exp(-r) for r in rates]
    root = [jnp.sqrt(2.0 * r) for r in rates]
    amp = [resid[i] * root[i] for i in range(2)]

    zero = jnp.zeros((8, lanes), f32)

    def row_of(ref, tok):
        return jnp.broadcast_to(ref[pl.ds(tok, 1), :], (8, lanes))

    def local_body(tok, carry):
        e0, e1, f0, f1 = carry
        xb = row_of(mixed, tok)
        gb = row_of(gmixed, toks - 1 - tok)
        return (
            decay[0] * e0 + xb,
            decay[1] * e1 + xb,
            decay[0] * f0 + gb,
            decay[1] * f1 + gb,
        )

    e0, e1, f0, f1 = lax.fori_loop(0, toks, local_body, (zero,) * 4, unroll=16)

    ends = [e0, e1]
    heads = [f0, f1]
    step = 1
    while step < chunks:
        for i in range(2):
            power = jnp.exp(rates[i] * (-1.0 * toks * step))
            moved = jnp.where(lane_chunk >= step, pltpu.roll(ends[i], step, 1), 0.0)
            ends[i] = ends[i] + power * moved
            moved = jnp.where(
                lane_chunk < chunks - step, pltpu.roll(heads[i], lanes - step, 1), 0.0
            )
            heads[i] = heads[i] + power * moved
        step *= 2
    start_h = [jnp.where(lane_chunk >= 1, pltpu.roll(e, 1, 1), 0.0) for e in ends]
    start_p = [
        jnp.where(lane_chunk < chunks - 1, pltpu.roll(f, lanes - 1, 1), 0.0) for f in heads
    ]

    def keep(ref, tok, value):
        for half in range(2):
            ref[half, pl.ds(pl.multiple_of(8 * tok, 8), 8), :] = value[
                :, half * toks : (half + 1) * toks
            ]

    def forward_body(tok, carry):
        h0, h1, r0, r1 = carry
        xb = row_of(mixed, tok)
        gb = row_of(gmixed, tok)
        h0 = decay[0] * h0 + xb
        h1 = decay[1] * h1 + xb
        keep(part_y, tok, amp[0] * h0 + amp[1] * h1)
        states[pl.ds(pl.multiple_of(16 * tok, 8), 8), :] = h0
        states[pl.ds(pl.multiple_of(16 * tok + 8, 8), 8), :] = h1
        return (h0, h1, r0 + gb * h0, r1 + gb * h1)

    _, _, r0, r1 = lax.fori_loop(
        0, toks, forward_body, (start_h[0], start_h[1], zero, zero), unroll=16
    )

    def backward_body(step_index, carry):
        p0, p1, k0, k1 = carry
        tok = toks - 1 - step_index
        gb = row_of(gmixed, tok)
        q0 = decay[0] * p0
        q1 = decay[1] * p1
        k0 = k0 + states[pl.ds(pl.multiple_of(16 * tok, 8), 8), :] * q0
        k1 = k1 + states[pl.ds(pl.multiple_of(16 * tok + 8, 8), 8), :] * q1
        p0 = q0 + gb
        p1 = q1 + gb
        keep(part_z, tok, amp[0] * p0 + amp[1] * p1)
        return (p0, p1, k0, k1)

    _, _, k0, k1 = lax.fori_loop(
        0, toks, backward_body, (start_p[0], start_p[1], zero, zero), unroll=16
    )

    def folded(ref, first, count):
        halves = []
        for half in range(2):
            total = None
            for sub in range(8):
                term = ref[half, pl.ds(first + sub, count, stride=8), :]
                total = term if total is None else total + term
            halves.append(total)
        return jnp.concatenate(halves, axis=1)

    def gathered(ref, start):
        return folded(ref, 8 * start, block).astype(jnp.bfloat16).astype(f32)

    def put(stream, start, value):
        hat[stream, start : start + block, :] = value

    for start in range(0, toks, block):
        rows = slice(start, start + block)
        conv = gathered(part_y, start)
        back = gathered(part_z, start)
        grads[0, rows, :] = xt[3, PAD + start : PAD + start + block, :] * conv
        grads[1, rows, :] = back * hat[2, rows, :]
        grads[2, rows, :] = back * hat[1, rows, :]
        mixed[rows, :] = hat[0, rows, :] * conv
    for stream in range(3):
        head = pltpu.roll(grads[stream, 0:PAD, :], lanes - 1, 1)
        grads[stream, toks : toks + PAD, :] = jnp.where(lane_chunk < chunks - 1, head, 0.0)
    for stream in range(3):
        tap_sums = [zero for _ in range(TAPS)]
        for start in range(0, toks, block):
            own = grads[stream, start : start + block, :]
            total = None
            for tap in range(TAPS):
                row = prm_ref[stream * TAPS + tap : stream * TAPS + tap + 1, :]
                term = row * grads[stream, start + tap : start + tap + block, :]
                total = term if total is None else total + term
                lo = PAD - tap + start
                prod = own * xt[stream, lo : lo + block, :]
                for sub in range(0, block, 8):
                    tap_sums[tap] = tap_sums[tap] + prod[sub : sub + 8, :]
            put(stream, start, total)
        for tap in range(TAPS):
            index = stream * TAPS + tap
            keep(sums, index, tap_sums[tap])
    for index in range(21, 24):
        keep(sums, index, zero)
    short_rows = folded(sums, 0, 24)
    modal_rows = [root[0] * r0, root[1] * r1] + [
        amp[i] * (0.5 * (r0, r1)[i] - rates[i] * (k0, k1)[i]) for i in range(2)
    ]
    every = jnp.concatenate([short_rows] + modal_rows, axis=0)
    owner = lax.broadcasted_iota(jnp.int32, (8, lanes), 1) // chunks
    pick = (owner == lax.broadcasted_iota(jnp.int32, (8, lanes), 0)).astype(f32)
    totals = (
        lax.dot_general(
            pick,
            every,
            (((1,), (1,)), ((), ())),
            precision=lax.Precision.HIGHEST,
            preferred_element_type=f32,
        )
        * scale
    )
    modal_ref[...] = totals[:, 24:56]

    for stream in range(4):
        for pair in range(2):
            cols = slice(pair * 2 * chunks, (pair + 1) * 2 * chunks)
            tile = (mixed[:, cols] if stream == 0 else hat[stream - 1, :, cols]).T
            first = stream * 4 + 2 * pair
            out_rows[pl.ds(first, chunks, stride=ROWS_OUT), :] = tile[:chunks]
            out_rows[pl.ds(first + 1, chunks, stride=ROWS_OUT), :] = tile[chunks:]
    short = jnp.concatenate([totals[0:4, 0:24], jnp.zeros((4, toks - 24), f32)], axis=1)
    upper = short.astype(jnp.bfloat16).astype(f32)
    for chan in range(4):
        out_rows[pl.ds(16 + chan, chunks, stride=ROWS_OUT), :] = jnp.broadcast_to(
            upper[chan : chan + 1, :], (chunks, toks)
        )
        out_rows[pl.ds(20 + chan, chunks, stride=ROWS_OUT), :] = jnp.broadcast_to(
            (short - upper)[chan : chan + 1, :], (chunks, toks)
        )
    send_ref[...] = out_rows[...].reshape(send_ref.shape).astype(jnp.bfloat16)


def run_pack(query_in, key_in, value_in, grad_out):
    chans, toks = query_in.shape
    owners = chans // 4
    return pl.pallas_call(
        pack_kernel,
        out_shape=jax.ShapeDtypeStruct((owners, ROWS_IN, toks), jnp.bfloat16),
        scratch_shapes=[
            pltpu.VMEM((chans, toks), jnp.float32),
            pltpu.VMEM((owners * ROWS_IN, toks), jnp.float32),
        ],
        compiler_params=pltpu.CompilerParams(vmem_limit_bytes=VMEM_LIMIT),
    )(query_in, key_in, value_in, grad_out)


def run_main(recv, prm):
    chunks, _, toks = recv.shape
    lanes = 4 * chunks
    f32 = jnp.float32
    return pl.pallas_call(
        main_kernel,
        out_shape=(
            jax.ShapeDtypeStruct((chunks, ROWS_OUT, toks), jnp.bfloat16),
            jax.ShapeDtypeStruct((8, 2 * MODES), f32),
        ),
        scratch_shapes=[
            pltpu.VMEM((chunks * ROWS_IN, toks), f32),
            pltpu.VMEM((4, PAD + toks, lanes), f32),
            pltpu.VMEM((3, toks, lanes), f32),
            pltpu.VMEM((toks, lanes), f32),
            pltpu.VMEM((toks, lanes), f32),
            pltpu.VMEM((2, 8 * toks, lanes // 2), f32),
            pltpu.VMEM((2, 8 * toks, lanes // 2), f32),
            pltpu.VMEM((16 * toks, lanes), f32),
            pltpu.VMEM((3, toks + PAD, lanes), f32),
            pltpu.VMEM((2, 8 * 24, lanes // 2), f32),
            pltpu.VMEM((chunks * ROWS_OUT, toks), f32),
        ],
        compiler_params=pltpu.CompilerParams(vmem_limit_bytes=VMEM_LIMIT),
    )(recv, prm)


def run_unpack(recv):
    owners, _, toks = recv.shape
    chans = 4 * owners
    whole = jax.ShapeDtypeStruct((chans, toks), jnp.bfloat16)
    return pl.pallas_call(
        unpack_kernel,
        out_shape=(whole, whole, whole, whole, jax.ShapeDtypeStruct((3 * TAPS, chans), jnp.float32)),
        scratch_shapes=[
            pltpu.VMEM((owners * ROWS_OUT, toks), jnp.float32),
            pltpu.VMEM((chans, toks), jnp.float32),
        ],
        compiler_params=pltpu.CompilerParams(vmem_limit_bytes=VMEM_LIMIT),
    )(recv)


def parameter_rows(weights, residue, log_rate, chunks):
    rows = jnp.concatenate(
        [
            weights.reshape(3 * TAPS, 4),
            jnp.zeros((3, 4), jnp.float32),
            log_rate.T,
            residue.T,
        ],
        axis=0,
    )
    return jnp.repeat(rows, chunks, axis=1)


def local(query_in, key_in, value_in, short_weight, residue, log_rate, grad_out):
    chunks = lax.axis_size("seq")
    chans = query_in.shape[0]
    owned = chans // chunks
    weights = lax.dynamic_slice(
        short_weight, (0, 0, owned * lax.axis_index("seq")), (3, TAPS, owned)
    )
    prm = parameter_rows(weights, residue, log_rate, chunks)
    send = run_pack(query_in, key_in, value_in, grad_out)
    recv = lax.all_to_all(send, "seq", 0, 0, tiled=True)
    back, modal = run_main(recv, prm)
    final = lax.all_to_all(back, "seq", 0, 0, tiled=True)
    output, grad_query, grad_key, grad_value, short = run_unpack(final)
    grad_short = short.reshape(3, TAPS, chans)
    return (
        output,
        grad_query,
        grad_key,
        grad_value,
        grad_short,
        modal[:owned, :MODES],
        modal[:owned, MODES:],
    )


def solution(mesh):
    return jax.shard_map(
        local,
        mesh=mesh,
        in_specs=(
            P("chan", "seq"),
            P("chan", "seq"),
            P("chan", "seq"),
            P(None, None, "chan"),
            P(("chan", "seq"), None),
            P(("chan", "seq"), None),
            P("chan", "seq"),
        ),
        out_specs=(
            P("chan", "seq"),
            P("chan", "seq"),
            P("chan", "seq"),
            P("chan", "seq"),
            P(None, None, "chan"),
            P(("chan", "seq"), None),
            P(("chan", "seq"), None),
        ),
        check_vma=False,
    )
```

time: 785 us -> 90.4 us (0.12)
  the two profiles are of different devices: /device:TPU:63 before, /device:TPU:33 now
where the time goes in v1:
time: 90.4 us; the launch traced here: 89.9 us
  waiting for transfers between devices  51.4 us (57%)
  starting transfers between devices  25 us (28%)
  Pallas kernels  6.75 us (7%)
  local copies, waits for them, and re-layouts  6.01 us (7%)
    all_to_all x1, waiting for transfers between devices, local(): final = lax.all_to_all(back, 'seq', 0, 0, tiled=True)  26 us
    all_to_all x1, waiting for transfers between devices, local(): recv = lax.all_to_all(send, 'seq', 0, 0, tiled=True)  25.4 us
    all_to_all x1, starting transfers between devices, local(): recv = lax.all_to_all(send, 'seq', 0, 0, tiled=True)  20.5 us
    pallas_call x1, Pallas kernels, run_main(): pl.pallas_call(main_kernel, out_shape=(jax.ShapeDtypeStruct((chunks, ROWS...  4.83 us
    all_to_all x1, starting transfers between devices, local(): final = lax.all_to_all(back, 'seq', 0, 0, tiled=True)  4.47 us
    unnamed x14, local copies, waits for them, and re-layouts  4.05 us
  transfers between devices with their start and end apart: 2, of which 2 were waited for; matrix products, arithmetic and copies ran while one was open for 2% of the time, Pallas kernels for 0%

profile of v1, /device:TPU:33, one launch (start us, length us, event | category | flops | bytes accessed | tf_op | source)
XLA Modules:
  0.0 89.9 jit_solution(3190954345122098039)
XLA Ops:
  0.6 0.0 copy-start
  0.6 0.0 copy-start.1
  0.7 0.8 copy-done.1
  1.5 0.0 copy-start.2
  1.5 0.8 copy-done.2
  2.3 0.0 copy-start.3
  2.3 0.8 copy-done.3
  3.2 0.0 copy-start.4
  3.2 0.8 copy-done.4
  4.0 1.0 %shard_map.126 = bf16[64,16,128]{2,1,0:T(8,128)(2,1)} custom-call(bf16[256,128]{1,0:T(8,128)(2,1)S(1)} %copy-done.1, bf16[256,128]{1,0:T(8,128)(2,1)S(1)} %copy-done.2, bf16[256,128]{1,0:T(8,128)(2,1)S(1)} %copy-done.3, bf16[256,128]{1,0:T(8,128)(2,1)S(1)} %copy-done.4), custom_call_target="tpu_custom_call" | custom-call | tf_op jit(solution)/shard_map/pallas_call | solution.py:274
  5.0 20.5 %all-to-all-start = ((bf16[64,16,128]{2,1,0:T(8,128)(2,1)}), bf16[64,16,128]{2,1,0:T(8,128)(2,1)S(1)}, u32[]{:S(2)}, u32[]{:S(2)}) async-start(bf16[64,16,128]{2,1,0:T(8,128)(2,1)} %shard_map.126), calls=%async_computation | async-start | bytes 524288 | tf_op jit(solution)/shard_map/all_to_all | solution.py:349
  25.5 0.0 copy-done
  25.5 0.1 constant_dynamic-slice_fusion
  25.6 0.1 copy.16
  25.7 0.1 reshape.23
  25.8 0.0 copy-start.6
  25.8 0.1 pad.1.clone
  25.9 0.0 copy-start.5
  25.9 0.6 copy-done.6
  26.5 0.1 copy-done.5
  26.6 0.1 pad_maximum_fusion
  26.6 0.1 copy.17
  26.7 0.1 broadcast_in_dim.3
  26.9 0.1 reshape.24.prm_ref
  27.0 25.4 %all-to-all-done.recv_ref = bf16[64,16,128]{2,1,0:T(8,128)(2,1)S(1)} async-done(((bf16[64,16,128]{2,1,0:T(8,128)(2,1)}), bf16[64,16,128]{2,1,0:T(8,128)(2,1)S(1)}, u32[]{:S(2)}, u32[]{:S(2)}) %all-to-all-start) | async-done | bytes 262176 | tf_op jit(solution)/shard_map/all_to_all | solution.py:349
  52.4 4.8 %shard_map.127 = (bf16[64,24,128]{2,1,0:T(8,128)(2,1)}, f32[8,32]{1,0:T(8,128)S(1)}) custom-call(bf16[64,16,128]{2,1,0:T(8,128)(2,1)S(1)} %all-to-all-done.recv_ref, f32[56,256]{1,0:T(8,128)S(1)} %reshape.24.prm_ref), custom_call_target="tpu_custom_call" | custom-call | tf_op jit(solution)/shard_map/pallas_call | solution.py:289
  57.2 4.5 %all-to-all-start.1 = ((bf16[64,24,128]{2,1,0:T(8,128)(2,1)}), bf16[64,24,128]{2,1,0:T(8,128)(2,1)S(1)}, u32[]{:S(2)}, u32[]{:S(2)}) async-start(bf16[64,24,128]{2,1,0:T(8,128)(2,1)} %get-tuple-element.14), calls=%async_computation.1 | async-start | bytes 786432 | tf_op jit(solution)/shard_map/all_to_all | solution.py:351
  61.7 0.7 fusion
  62.4 26.0 %all-to-all-done.1.recv_ref = bf16[64,24,128]{2,1,0:T(8,128)(2,1)S(1)} async-done(((bf16[64,24,128]{2,1,0:T(8,128)(2,1)}), bf16[64,24,128]{2,1,0:T(8,128)(2,1)S(1)}, u32[]{:S(2)}, u32[]{:S(2)}) %all-to-all-start.1) | async-done | bytes 393248 | tf_op jit(solution)/shard_map/all_to_all | solution.py:351
  88.4 0.9 %shard_map.128 = (bf16[256,128]{1,0:T(8,128)(2,1)}, bf16[256,128]{1,0:T(8,128)(2,1)}, bf16[256,128]{1,0:T(8,128)(2,1)}, bf16[256,128]{1,0:T(8,128)(2,1)}, f32[21,256]{1,0:T(8,128)S(1)}) custom-call(bf16[64,24,128]{2,1,0:T(8,128)(2,1)S(1)} %all-to-all-done.1.recv_ref), custom_call_target="tpu_custom_call" | custom-call | tf_op jit(solution)/shard_map/pallas_call | solution.py:316
  89.3 0.6 reshape.25
  (1 shorter events, 0.0 us)
Async XLA Ops:
  0.6 24.9 %copy-start = (f32[3,7,256]{2,1,0:T(8,128)S(1)}, f32[3,7,256]{2,1,0:T(8,128)}, u32[]{:S(2)}) copy-start(f32[3,7,256]{2,1,0:T(8,128)} %param.10) | copy-start | bytes 64516
  0.6 0.8 copy-start.1
  1.5 0.8 copy-start.2
  2.3 0.8 copy-start.3
  3.2 0.8 copy-start.4
  5.0 47.4 %all-to-all-start = ((bf16[64,16,128]{2,1,0:T(8,128)(2,1)}), bf16[64,16,128]{2,1,0:T(8,128)(2,1)S(1)}, u32[]{:S(2)}, u32[]{:S(2)}) async-start(bf16[64,16,128]{2,1,0:T(8,128)(2,1)} %shard_map.126), calls=%async_computation | async-start | bytes 524288 | tf_op jit(solution)/shard_map/all_to_all | solution.py:349
  25.8 0.7 copy-start.6
  25.9 0.7 copy-start.5
  57.2 31.1 %all-to-all-start.1 = ((bf16[64,24,128]{2,1,0:T(8,128)(2,1)}), bf16[64,24,128]{2,1,0:T(8,128)(2,1)S(1)}, u32[]{:S(2)}, u32[]{:S(2)}) async-start(bf16[64,24,128]{2,1,0:T(8,128)(2,1)} %get-tuple-element.14), calls=%async_computation.1 | async-start | bytes 786432 | tf_op jit(solution)/shard_map/all_to_all | solution.py:351

commit v2 on v1

--- a/solution.py
+++ b/solution.py
@@ -11,36 +11,45 @@
 MODES = 16
 PAD = 8
 ROWS_IN = 16
-ROWS_OUT = 24
+ROWS_OUT = 18
 VMEM_LIMIT = 40 * 1024 * 1024
 
 
-def pack_kernel(query_ref, key_ref, value_ref, grad_ref, send_ref, wide, mixed_rows):
+def pack_kernel(query_ref, key_ref, value_ref, grad_ref, send_ref, held, wide, mixed_rows, sems):
     owners = send_ref.shape[0]
-    for stream, ref in enumerate((query_ref, key_ref, value_ref, grad_ref)):
-        wide[...] = ref[...].astype(jnp.float32)
+    copies = [
+        pltpu.make_async_copy(ref, held.at[stream], sems.at[stream])
+        for stream, ref in enumerate((query_ref, key_ref, value_ref, grad_ref))
+    ]
+    for copy in copies:
+        copy.start()
+    for stream, copy in enumerate(copies):
+        copy.wait()
+        wide[stream] = held[stream].astype(jnp.float32)
         for chan in range(4):
             mixed_rows[pl.ds(stream * 4 + chan, owners, stride=ROWS_IN), :] = wide[
-                pl.ds(chan, owners, stride=4), :
+                stream, pl.ds(chan, owners, stride=4), :
             ]
     send_ref[...] = mixed_rows[...].reshape(send_ref.shape).astype(jnp.bfloat16)
 
 
 def unpack_kernel(recv_ref, out_ref, gq_ref, gk_ref, gv_ref, short_ref, rows, wide):
-    owners = recv_ref.shape[0]
-    rows[...] = recv_ref[...].reshape(rows.shape).astype(jnp.float32)
+    owners = recv_ref.shape[0] // ROWS_OUT
+    rows[...] = recv_ref[...].astype(jnp.float32)
     for stream, ref in enumerate((out_ref, gq_ref, gk_ref, gv_ref)):
         for chan in range(4):
-            wide[pl.ds(chan, owners, stride=4), :] = rows[
+            wide[stream, pl.ds(chan, owners, stride=4), :] = rows[
                 pl.ds(stream * 4 + chan, owners, stride=ROWS_OUT), :
             ]
-        ref[...] = wide[...].astype(jnp.bfloat16)
+        ref[...] = wide[stream].astype(jnp.bfloat16)
+    short = (
+        rows[pl.ds(16, owners, stride=ROWS_OUT), :] + rows[pl.ds(17, owners, stride=ROWS_OUT), :]
+    )
     for chan in range(4):
-        wide[pl.ds(chan, owners, stride=4), :] = (
-            rows[pl.ds(16 + chan, owners, stride=ROWS_OUT), :]
-            + rows[pl.ds(20 + chan, owners, stride=ROWS_OUT), :]
-        )
-    short_ref[...] = wide[...].T[: short_ref.shape[0], :]
+        wide[4, pl.ds(chan, owners, stride=4), :] = pltpu.roll(short, (128 - 32 * chan) % 128, 1)
+    turned = wide[4].T
+    for stream in range(3):
+        short_ref[stream] = turned[stream * TAPS : (stream + 1) * TAPS, :]
 
 
 def main_kernel(
@@ -256,16 +265,14 @@
             first = stream * 4 + 2 * pair
             out_rows[pl.ds(first, chunks, stride=ROWS_OUT), :] = tile[:chunks]
             out_rows[pl.ds(first + 1, chunks, stride=ROWS_OUT), :] = tile[chunks:]
-    short = jnp.concatenate([totals[0:4, 0:24], jnp.zeros((4, toks - 24), f32)], axis=1)
-    upper = short.astype(jnp.bfloat16).astype(f32)
-    for chan in range(4):
-        out_rows[pl.ds(16 + chan, chunks, stride=ROWS_OUT), :] = jnp.broadcast_to(
-            upper[chan : chan + 1, :], (chunks, toks)
-        )
-        out_rows[pl.ds(20 + chan, chunks, stride=ROWS_OUT), :] = jnp.broadcast_to(
-            (short - upper)[chan : chan + 1, :], (chunks, toks)
-        )
-    send_ref[...] = out_rows[...].reshape(send_ref.shape).astype(jnp.bfloat16)
+    short = jnp.concatenate([totals[:, 0:24], jnp.zeros((8, toks - 24), f32)], axis=1)
+    line = short[0:1, :]
+    for chan in range(1, 4):
+        line = line + pltpu.roll(short, 32 * chan, 1)[chan : chan + 1, :]
+    upper = line.astype(jnp.bfloat16).astype(f32)
+    out_rows[pl.ds(16, chunks, stride=ROWS_OUT), :] = jnp.broadcast_to(upper, (chunks, toks))
+    out_rows[pl.ds(17, chunks, stride=ROWS_OUT), :] = jnp.broadcast_to(line - upper, (chunks, toks))
+    send_ref[...] = out_rows[...].astype(jnp.bfloat16)
 
 
 def run_pack(query_in, key_in, value_in, grad_out):
@@ -273,10 +280,13 @@
     owners = chans // 4
     return pl.pallas_call(
         pack_kernel,
+        in_specs=[pl.BlockSpec(memory_space=pltpu.HBM)] * 4,
         out_shape=jax.ShapeDtypeStruct((owners, ROWS_IN, toks), jnp.bfloat16),
         scratch_shapes=[
-            pltpu.VMEM((chans, toks), jnp.float32),
+            pltpu.VMEM((4, chans, toks), jnp.bfloat16),
+            pltpu.VMEM((4, chans, toks), jnp.float32),
             pltpu.VMEM((owners * ROWS_IN, toks), jnp.float32),
+            pltpu.SemaphoreType.DMA((4,)),
         ],
         compiler_params=pltpu.CompilerParams(vmem_limit_bytes=VMEM_LIMIT),
     )(query_in, key_in, value_in, grad_out)
@@ -289,7 +299,7 @@
     return pl.pallas_call(
         main_kernel,
         out_shape=(
-            jax.ShapeDtypeStruct((chunks, ROWS_OUT, toks), jnp.bfloat16),
+            jax.ShapeDtypeStruct((chunks * ROWS_OUT, toks), jnp.bfloat16),
             jax.ShapeDtypeStruct((8, 2 * MODES), f32),
         ),
         scratch_shapes=[
@@ -310,15 +320,16 @@
 
 
 def run_unpack(recv):
-    owners, _, toks = recv.shape
+    rows, toks = recv.shape
+    owners = rows // ROWS_OUT
     chans = 4 * owners
     whole = jax.ShapeDtypeStruct((chans, toks), jnp.bfloat16)
     return pl.pallas_call(
         unpack_kernel,
-        out_shape=(whole, whole, whole, whole, jax.ShapeDtypeStruct((3 * TAPS, chans), jnp.float32)),
+        out_shape=(whole,) * 4 + (jax.ShapeDtypeStruct((3, TAPS, chans), jnp.float32),),
         scratch_shapes=[
             pltpu.VMEM((owners * ROWS_OUT, toks), jnp.float32),
-            pltpu.VMEM((chans, toks), jnp.float32),
+            pltpu.VMEM((5, chans, toks), jnp.float32),
         ],
         compiler_params=pltpu.CompilerParams(vmem_limit_bytes=VMEM_LIMIT),
     )(recv)
@@ -348,9 +359,9 @@
     send = run_pack(query_in, key_in, value_in, grad_out)
     recv = lax.all_to_all(send, "seq", 0, 0, tiled=True)
     back, modal = run_main(recv, prm)
-    final = lax.all_to_all(back, "seq", 0, 0, tiled=True)
-    output, grad_query, grad_key, grad_value, short = run_unpack(final)
-    grad_short = short.reshape(3, TAPS, chans)
+    paired = back.reshape(chunks, ROWS_OUT // 2, 2, back.shape[1])
+    final = lax.all_to_all(paired, "seq", 0, 0, tiled=True)
+    output, grad_query, grad_key, grad_value, grad_short = run_unpack(final.reshape(back.shape))
     return (
         output,
         grad_query,

time: 90.4 us -> 85.9 us (0.950)
  waiting for transfers between devices: 51.4 us -> 47.4 us
    all_to_all x1, waiting for transfers between devices: 26 us -> 22 us  [local(): final = lax.all_to_all(paired, 'seq', 0, 0, tiled=True)]
where the time goes in v2:
time: 85.9 us; the launch traced here: 85.5 us
  waiting for transfers between devices  47.4 us (55%)
  starting transfers between devices  25 us (29%)
  Pallas kernels  6.89 us (8%)
  local copies, waits for them, and re-layouts  5.4 us (6%)
    all_to_all x1, waiting for transfers between devices, local(): recv = lax.all_to_all(send, 'seq', 0, 0, tiled=True)  25.4 us
    all_to_all x1, waiting for transfers between devices, local(): final = lax.all_to_all(paired, 'seq', 0, 0, tiled=True)  22 us
    all_to_all x1, starting transfers between devices, local(): recv = lax.all_to_all(send, 'seq', 0, 0, tiled=True)  20.5 us
    pallas_call x1, Pallas kernels, run_main(): pl.pallas_call(main_kernel, out_shape=(jax.ShapeDtypeStruct((chunks * ROW...  4.77 us
    all_to_all x1, starting transfers between devices, local(): final = lax.all_to_all(paired, 'seq', 0, 0, tiled=True)  4.47 us
    unnamed x14, local copies, waits for them, and re-layouts  4.05 us
  transfers between devices with their start and end apart: 2, of which 2 were waited for; matrix products, arithmetic and copies ran while one was open for 2% of the time, Pallas kernels for 0%

profile of v2, /device:TPU:33, one launch (start us, length us, event | category | flops | bytes accessed | tf_op | source)
XLA Modules:
  0.0 85.5 jit_solution(17716531044755241376)
XLA Ops:
  0.6 0.0 copy-start
  0.6 0.0 copy-start.1
  0.7 0.8 copy-done.1
  1.5 0.0 copy-start.2
  1.5 0.8 copy-done.2
  2.3 0.0 copy-start.3
  2.3 0.8 copy-done.3
  3.2 0.0 copy-start.4
  3.2 0.8 copy-done.4
  4.0 1.3 %shard_map.126 = bf16[64,16,128]{2,1,0:T(8,128)(2,1)} custom-call(bf16[256,128]{1,0:T(8,128)(2,1)S(1)} %copy-done.1, bf16[256,128]{1,0:T(8,128)(2,1)S(1)} %copy-done.2, bf16[256,128]{1,0:T(8,128)(2,1)S(1)} %copy-done.3, bf16[256,128]{1,0:T(8,128)(2,1)S(1)} %copy-done.4), custom_call_target="tpu_custom_call" | custom-call | tf_op jit(solution)/shard_map/pallas_call | solution.py:281
  5.3 20.5 %all-to-all-start = ((bf16[64,16,128]{2,1,0:T(8,128)(2,1)}), bf16[64,16,128]{2,1,0:T(8,128)(2,1)S(1)}, u32[]{:S(2)}, u32[]{:S(2)}) async-start(bf16[64,16,128]{2,1,0:T(8,128)(2,1)} %shard_map.126), calls=%async_computation | async-start | bytes 524288 | tf_op jit(solution)/shard_map/all_to_all | solution.py:360
  25.9 0.0 copy-done
  25.9 0.1 constant_dynamic-slice_fusion
  25.9 0.1 copy.16
  26.1 0.1 reshape.26
  26.1 0.0 copy-start.6
  26.1 0.1 pad.1.clone
  26.2 0.0 copy-start.5
  26.2 0.6 copy-done.6
  26.8 0.1 copy-done.5
  26.9 0.1 pad_maximum_fusion
  27.0 0.1 copy.17
  27.1 0.1 broadcast_in_dim.3
  27.2 0.1 reshape.27.prm_ref
  27.3 25.4 %all-to-all-done.recv_ref = bf16[64,16,128]{2,1,0:T(8,128)(2,1)S(1)} async-done(((bf16[64,16,128]{2,1,0:T(8,128)(2,1)}), bf16[64,16,128]{2,1,0:T(8,128)(2,1)S(1)}, u32[]{:S(2)}, u32[]{:S(2)}) %all-to-all-start) | async-done | bytes 262176 | tf_op jit(solution)/shard_map/all_to_all | solution.py:360
  52.7 4.8 %shard_map.127 = (bf16[1152,128]{1,0:T(8,128)(2,1)}, f32[8,32]{1,0:T(8,128)S(1)}) custom-call(bf16[64,16,128]{2,1,0:T(8,128)(2,1)S(1)} %all-to-all-done.recv_ref, f32[56,256]{1,0:T(8,128)S(1)} %reshape.27.prm_ref), custom_call_target="tpu_custom_call" | custom-call | tf_op jit(solution)/shard_map/pallas_call | solution.py:299
  57.5 4.5 %all-to-all-start.1 = ((bf16[64,9,2,128]{3,2,1,0:T(2,128)(2,1)}), bf16[64,9,2,128]{3,2,1,0:T(2,128)(2,1)S(1)}, u32[]{:S(2)}, u32[]{:S(2)}) async-start(bf16[64,9,2,128]{3,2,1,0:T(2,128)(2,1)} %bitcast.2), calls=%async_computation.1 | async-start | bytes 589824 | tf_op jit(solution)/shard_map/all_to_all | solution.py:363
  62.0 0.7 fusion
  62.6 22.0 %all-to-all-done.1 = bf16[64,9,2,128]{3,2,1,0:T(2,128)(2,1)S(1)} async-done(((bf16[64,9,2,128]{3,2,1,0:T(2,128)(2,1)}), bf16[64,9,2,128]{3,2,1,0:T(2,128)(2,1)S(1)}, u32[]{:S(2)}, u32[]{:S(2)}) %all-to-all-start.1) | async-done | bytes 294944 | tf_op jit(solution)/shard_map/all_to_all | solution.py:363
  84.6 0.8 shard_map.128
  (1 shorter events, 0.0 us)
Async XLA Ops:
  0.6 25.2 %copy-start = (f32[3,7,256]{2,1,0:T(8,128)S(1)}, f32[3,7,256]{2,1,0:T(8,128)}, u32[]{:S(2)}) copy-start(f32[3,7,256]{2,1,0:T(8,128)} %param.10) | copy-start | bytes 64516
  0.6 0.8 copy-start.1
  1.5 0.8 copy-start.2
  2.3 0.8 copy-start.3
  3.2 0.8 copy-start.4
  5.3 47.4 %all-to-all-start = ((bf16[64,16,128]{2,1,0:T(8,128)(2,1)}), bf16[64,16,128]{2,1,0:T(8,128)(2,1)S(1)}, u32[]{:S(2)}, u32[]{:S(2)}) async-start(bf16[64,16,128]{2,1,0:T(8,128)(2,1)} %shard_map.126), calls=%async_computation | async-start | bytes 524288 | tf_op jit(solution)/shard_map/all_to_all | solution.py:360
  26.1 0.7 copy-start.6
  26.2 0.7 copy-start.5
  57.5 27.1 %all-to-all-start.1 = ((bf16[64,9,2,128]{3,2,1,0:T(2,128)(2,1)}), bf16[64,9,2,128]{3,2,1,0:T(2,128)(2,1)S(1)}, u32[]{:S(2)}, u32[]{:S(2)}) async-start(bf16[64,9,2,128]{3,2,1,0:T(2,128)(2,1)} %bitcast.2), calls=%async_computation.1 | async-start | bytes 589824 | tf_op jit(solution)/shard_map/all_to_all | solution.py:363

commit v3 on v2

v3 whole, which is shorter than its diff:
```python
import math

import jax
import jax.numpy as jnp
from jax import lax
from jax.experimental import pallas as pl
from jax.experimental.pallas import tpu as pltpu
from jax.sharding import PartitionSpec as P

TAPS = 7
MODES = 16
PAD = 8
OWNED = 8
ROWS_IN = 4 * OWNED
ROWS_OUT = 40
VMEM_LIMIT = 40 * 1024 * 1024

STATE, DERIV, RSUM, KSUM, EDGE, SHORT, RESPONSE, MESSAGE = 0, 16, 32, 48, 64, 96, 128, 384


def first_row(chan, chans):
    return chan if chan < 4 else chans // 2 + chan - 4


def pack_kernel(query_ref, key_ref, value_ref, grad_ref, send_ref, held, wide, mixed_rows, sems):
    owners = send_ref.shape[0]
    chans = query_ref.shape[0]
    copies = [
        pltpu.make_async_copy(ref, held.at[stream], sems.at[stream])
        for stream, ref in enumerate((query_ref, key_ref, value_ref, grad_ref))
    ]
    for copy in copies:
        copy.start()
    for stream, copy in enumerate(copies):
        copy.wait()
        wide[stream] = held[stream].astype(jnp.float32)
        for chan in range(OWNED):
            mixed_rows[pl.ds(stream * OWNED + chan, owners, stride=ROWS_IN), :] = wide[
                stream, pl.ds(first_row(chan, chans), owners, stride=4), :
            ]
    send_ref[...] = mixed_rows[...].reshape(send_ref.shape).astype(jnp.bfloat16)


def unpack_kernel(recv_ref, out_ref, gq_ref, gk_ref, gv_ref, short_ref, rows, wide):
    owners = recv_ref.shape[0]
    chans = out_ref.shape[0]
    rows[...] = recv_ref[...].reshape(rows.shape).astype(jnp.float32)
    for stream, ref in enumerate((out_ref, gq_ref, gk_ref, gv_ref)):
        for chan in range(OWNED):
            wide[stream, pl.ds(first_row(chan, chans), owners, stride=4), :] = rows[
                pl.ds(stream * OWNED + chan, owners, stride=ROWS_OUT), :
            ]
        ref[...] = wide[stream].astype(jnp.bfloat16)
    for group in range(2):
        short = (
            rows[pl.ds(32 + group, owners, stride=ROWS_OUT), :]
            + rows[pl.ds(34 + group, owners, stride=ROWS_OUT), :]
        )
        for chan in range(4):
            wide[4, pl.ds(first_row(4 * group + chan, chans), owners, stride=4), :] = pltpu.roll(
                short, (128 - 32 * chan) % 128, 1
            )
    turned = wide[4].T
    for stream in range(3):
        short_ref[stream] = turned[stream * TAPS : (stream + 1) * TAPS, :]


def lane_ids(chunks, rows):
    lane = lax.broadcasted_iota(jnp.int32, (rows, OWNED * chunks), 1)
    return lane % chunks, lane // chunks


def owner_pick(chunks):
    owner = lane_ids(chunks, OWNED)[1]
    return (owner == lax.broadcasted_iota(jnp.int32, owner.shape, 0)).astype(jnp.float32)


def exact_dot(left, right, dims):
    return lax.dot_general(
        left,
        right,
        (dims, ((), ())),
        precision=lax.Precision.HIGHEST,
        preferred_element_type=jnp.float32,
    )


def modal_rows(prm_ref):
    rates = [jnp.exp(prm_ref[24 + 8 * i : 32 + 8 * i, :]) for i in range(2)]
    resid = [prm_ref[40 + 8 * i : 48 + 8 * i, :] for i in range(2)]
    decay = [jnp.exp(-r) for r in rates]
    root = [jnp.sqrt(2.0 * r) for r in rates]
    amp = [resid[i] * root[i] for i in range(2)]
    return rates, decay, root, amp


def keep(ref, tok, value):
    lanes = ref.shape[2]
    for half in range(2):
        ref[half, pl.ds(pl.multiple_of(8 * tok, 8), 8), :] = value[
            :, half * lanes : (half + 1) * lanes
        ]


def folded(ref, first, count):
    halves = []
    for half in range(2):
        total = None
        for sub in range(8):
            term = ref[half, pl.ds(first + sub, count, stride=8), :]
            total = term if total is None else total + term
        halves.append(total)
    return jnp.concatenate(halves, axis=1)


def tap_row(prm_ref, stream, tap):
    index = stream * TAPS + tap
    return prm_ref[index : index + 1, :]


def rounded(value):
    return value.astype(jnp.bfloat16).astype(jnp.float32)


def first_kernel(
    half_ref,
    recv_ref,
    prm_ref,
    grad_ref,
    hat_ref,
    fwd_ref,
    bwd_ref,
    msg_ref,
    raw,
    xt,
    mixed,
    gmixed,
    base,
    part_y,
    part_z,
    states,
    weighted,
    sums,
    rows,
):
    chunks = recv_ref.shape[0]
    toks = recv_ref.shape[2]
    lanes = OWNED * chunks
    f32 = jnp.float32
    chunk_of, _ = lane_ids(chunks, 8)
    half = half_ref[0]
    late = half.astype(f32)
    early = 1.0 - late
    zero = jnp.zeros((8, lanes), f32)
    block = 32

    raw[...] = recv_ref[...].reshape(raw.shape).astype(f32)
    per_tile = toks // chunks
    for stream in range(4):
        for group in range(OWNED // per_tile):
            tile = jnp.concatenate(
                [
                    raw[
                        pl.ds(stream * OWNED + group * per_tile + c, chunks, stride=ROWS_IN), :
                    ]
                    for c in range(per_tile)
                ],
                axis=0,
            )
            xt[stream, PAD : PAD + toks, group * toks : (group + 1) * toks] = tile.T
    for stream in range(3):
        tail = pltpu.roll(xt[stream, toks : toks + PAD, :], 1, 1)
        xt[stream, 0:PAD, :] = jnp.where(chunk_of >= 1, tail, 0.0)

    fringe = (lax.broadcasted_iota(jnp.int32, (8, lanes), 0) < TAPS - 1) & (chunk_of == 0)
    kept = 1.0 - jnp.where(fringe, late, 0.0)
    for start in range(0, toks, block):
        filtered = []
        for stream in range(3):
            total = None
            for tap in range(TAPS):
                lo = PAD - tap + start
                term = tap_row(prm_ref, stream, tap) * xt[stream, lo : lo + block, :]
                total = term if total is None else total + term
            filtered.append(total)
            hat_ref[stream, start : start + block, :] = total
        grad = xt[3, PAD + start : PAD + start + block, :]
        mixed[start : start + block, :] = rounded(filtered[1] * filtered[2])
        gmixed[start : start + block, :] = rounded(grad * filtered[0])
        grad_ref[start : start + block, :] = grad
        base[0, start : start + block, :] = grad
        base[1, start : start + block, :] = filtered[2]
        base[2, start : start + block, :] = filtered[1]
    mixed[0:8, :] = mixed[0:8, :] * kept
    gmixed[0:8, :] = gmixed[0:8, :] * kept
    for stream in range(3):
        base[stream, 0:8, :] = base[stream, 0:8, :] * kept

    rates, decay, _, amp = modal_rows(prm_ref)

    def row_of(ref, tok):
        return jnp.broadcast_to(ref[pl.ds(tok, 1), :], (8, lanes))

    def local_body(tok, carry):
        e0, e1, f0, f1 = carry
        xb = row_of(mixed, tok)
        gb = row_of(gmixed, toks - 1 - tok)
        return (
            decay[0] * e0 + xb,
            decay[1] * e1 + xb,
            decay[0] * f0 + gb,
            decay[1] * f1 + gb,
        )

    e0, e1, f0, f1 = lax.fori_loop(0, toks, local_body, (zero,) * 4, unroll=16)
    ends = [e0, e1]
    heads = [f0, f1]
    step = 1
    while step < chunks:
        for i in range(2):
            power = jnp.exp(rates[i] * (-1.0 * toks * step))
            moved = jnp.where(chunk_of >= step, pltpu.roll(ends[i], step, 1), 0.0)
            ends[i] = ends[i] + power * moved
            moved = jnp.where(chunk_of < chunks - step, pltpu.roll(heads[i], lanes - step, 1), 0.0)
            heads[i] = heads[i] + power * moved
        step *= 2
    start_h = [jnp.where(chunk_of >= 1, pltpu.roll(e, 1, 1), 0.0) for e in ends]
    start_p = [jnp.where(chunk_of < chunks - 1, pltpu.roll(f, lanes - 1, 1), 0.0) for f in heads]

    def forward_body(tok, carry):
        h0, h1, r0, r1, d0, d1 = carry
        xb = row_of(mixed, tok)
        gb = row_of(gmixed, tok)
        h0 = decay[0] * h0 + xb
        h1 = decay[1] * h1 + xb
        keep(part_y, tok, amp[0] * h0 + amp[1] * h1)
        states[pl.ds(pl.multiple_of(16 * tok, 8), 8), :] = h0
        states[pl.ds(pl.multiple_of(16 * tok + 8, 8), 8), :] = h1
        return (
            h0,
            h1,
            r0 + gb * h0,
            r1 + gb * h1,
            decay[0] * d0 + h0,
            decay[1] * d1 + h1,
        )

    _, _, r0, r1, d0, d1 = lax.fori_loop(
        0, toks, forward_body, (start_h[0], start_h[1]) + (zero,) * 4, unroll=16
    )

    def backward_body(step_index, carry):
        p0, p1, k0, k1, c0, c1 = carry
        tok = toks - 1 - step_index
        gb = row_of(gmixed, tok)
        q0 = decay[0] * p0
        q1 = decay[1] * p1
        k0 = k0 + states[pl.ds(pl.multiple_of(16 * tok, 8), 8), :] * q0
        k1 = k1 + states[pl.ds(pl.multiple_of(16 * tok + 8, 8), 8), :] * q1
        p0 = q0 + gb
        p1 = q1 + gb
        keep(part_z, tok, amp[0] * p0 + amp[1] * p1)
        return (p0, p1, k0, k1, decay[0] * c0 + p0, decay[1] * c1 + p1)

    _, _, k0, k1, c0, c1 = lax.fori_loop(
        0, toks, backward_body, (start_p[0], start_p[1]) + (zero,) * 4, unroll=16
    )

    for start in range(0, toks, block):
        fwd_ref[start : start + block, :] = folded(part_y, 8 * start, block)
        bwd_ref[start : start + block, :] = folded(part_z, 8 * start, block)

    for stream in range(3):
        tap_sums = [zero for _ in range(TAPS)]
        for start in range(0, toks, block):
            conv = (fwd_ref if stream == 0 else bwd_ref)[start : start + block, :]
            own = conv * base[stream, start : start + block, :]
            for tap in range(TAPS):
                lo = PAD - tap + start
                prod = own * xt[stream, lo : lo + block, :]
                for sub in range(0, block, 8):
                    tap_sums[tap] = tap_sums[tap] + prod[sub : sub + 8, :]
        for tap in range(TAPS):
            keep(sums, stream * TAPS + tap, tap_sums[tap])
    for index in range(3 * TAPS, 24):
        keep(sums, index, zero)
    rows[SHORT : SHORT + 24, :] = folded(sums, 0, 24)
    rows[SHORT + 24 : RESPONSE, :] = zero

    def fill(slot, stream):
        for tap in range(TAPS):
            for start in range(0, toks, block):
                lo = PAD - tap + start
                weighted[slot + tap, start : start + block, :] = (
                    base[stream, start : start + block, :] * xt[stream, lo : lo + block, :]
                )

    span_c = chunk_of.astype(f32)
    power_early = [jnp.exp(-r * (toks * (chunks - 1.0 - span_c) + 1.0)) for r in rates]
    power_late = [jnp.exp(-r * (toks * span_c - (TAPS - 2.0))) for r in rates]

    def respond(slot, powers, reverse):
        def body(step_index, carry):
            tok = toks - 1 - step_index if reverse else step_index
            out = []
            for tap in range(TAPS):
                wb = row_of(weighted.at[slot + tap], tok)
                for i in range(2):
                    out.append(decay[i] * carry[2 * tap + i] + wb)
            return tuple(out)

        total = lax.fori_loop(0, toks, body, (zero,) * (2 * TAPS), unroll=8)
        for tap in range(TAPS):
            for i in range(2):
                lo = RESPONSE + 16 * (slot + tap) + 8 * i
                rows[lo : lo + 8, :] = total[2 * tap + i] * powers[i]

    @pl.when(half == 0)
    def _():
        fill(0, 1)
        fill(TAPS, 2)
        respond(0, power_early, False)
        respond(TAPS, power_early, False)
        for stream in range(4):
            lo = EDGE + 8 * stream
            rows[lo : lo + 8, :] = jnp.where(
                chunk_of == chunks - 1, xt[stream, toks : toks + PAD, :], 0.0
            )
        for i in range(2):
            weight = jnp.exp(-rates[i] * (toks * (chunks - 1.0 - span_c)))
            rows[STATE + 8 * i : STATE + 8 * i + 8, :] = jnp.where(
                chunk_of == chunks - 1, ends[i], 0.0
            )
            rows[DERIV + 8 * i : DERIV + 8 * i + 8, :] = (d0, d1)[i] * weight

    @pl.when(half != 0)
    def _():
        fill(0, 0)
        respond(0, power_late, True)
        for lo in range(RESPONSE + 16 * TAPS, RESPONSE + 32 * TAPS, 8):
            rows[lo : lo + 8, :] = zero
        for stream in range(4):
            lo = EDGE + 8 * stream
            rows[lo : lo + 8, :] = jnp.where(chunk_of == 0, xt[stream, PAD : 2 * PAD, :], 0.0)
        for i in range(2):
            grow = jnp.exp(rates[i] * (TAPS - 1.0))
            weight = jnp.exp(-rates[i] * (toks * span_c))
            first = jnp.where(chunk_of == 0, heads[i], 0.0)
            rows[STATE + 8 * i : STATE + 8 * i + 8, :] = first * grow
            rows[DERIV + 8 * i : DERIV + 8 * i + 8, :] = (
                (c0, c1)[i] * weight - (TAPS - 1.0) * first
            ) * grow

    for i in range(2):
        rows[RSUM + 8 * i : RSUM + 8 * i + 8, :] = (r0, r1)[i]
        rows[KSUM + 8 * i : KSUM + 8 * i + 8, :] = (k0, k1)[i]
    for lo in range(RESPONSE + 32 * TAPS, MESSAGE, 8):
        rows[lo : lo + 8, :] = zero
    msg_ref[...] = exact_dot(owner_pick(chunks), rows[...], ((1,), (1,)))


def second_kernel(
    half_ref,
    own_ref,
    other_ref,
    prm_ref,
    grad_ref,
    hat_ref,
    fwd_ref,
    bwd_ref,
    send_ref,
    modal_ref,
    edge0,
    edge1,
    edges,
    part,
    outs,
    grads,
    out_rows,
):
    toks, lanes = grad_ref.shape
    chunks = lanes // OWNED
    f32 = jnp.float32
    chunk_of, _ = lane_ids(chunks, 8)
    scale = 1.0 / math.sqrt(2 * chunks * toks)
    half = half_ref[0]
    late = half.astype(f32)
    early = 1.0 - late
    rates, decay, root, amp = modal_rows(prm_ref)
    pick = owner_pick(chunks)
    fringe = TAPS - 1
    zero = jnp.zeros((8, lanes), f32)

    own = own_ref[...]
    other = other_ref[...]
    edge0[...] = exact_dot(own * early + other * late, pick, ((0,), (0,)))
    edge1[...] = exact_dot(own * late + other * early, pick, ((0,), (0,)))

    def pair(ref, first):
        return [ref[first + 8 * i : first + 8 * i + 8, :] for i in range(2)]

    row_id = lax.broadcasted_iota(jnp.int32, (8, lanes), 0)
    live = jnp.where(row_id < fringe, 1.0, 0.0)
    hats = []
    for stream in range(3):
        edges[stream, 0:8, :] = edge0[EDGE + 8 * stream : EDGE + 8 * stream + 8, :]
        edges[stream, 8:16, :] = edge1[EDGE + 8 * stream : EDGE + 8 * stream + 8, :]
        total = None
        for tap in range(TAPS):
            term = tap_row(prm_ref, stream, tap) * edges[stream, 8 - tap : 16 - tap, :]
            total = term if total is None else total + term
        hats.append(total)
    grad_edge = edge1[EDGE + 24 : EDGE + 32, :]
    x_edge = rounded(hats[1] * hats[2])
    g_edge = rounded(grad_edge * hats[0])

    state = pair(edge0, STATE)
    passed = []
    y_edge = zero
    for tok in range(fringe):
        xb = jnp.broadcast_to(x_edge[tok : tok + 1, :], (8, lanes))
        state = [decay[i] * state[i] + xb for i in range(2)]
        passed.append(state)
        line = jnp.sum(amp[0] * state[0] + amp[1] * state[1], axis=0, keepdims=True)
        y_edge = jnp.where(row_id == tok, line, y_edge)
    after = state
    back = pair(edge1, STATE)
    r_edge = [zero, zero]
    k_edge = [zero, zero]
    z_edge = zero
    adjoint = back
    for tok in range(fringe - 1, -1, -1):
        gb = jnp.broadcast_to(g_edge[tok : tok + 1, :], (8, lanes))
        moved = [decay[i] * adjoint[i] for i in range(2)]
        k_edge = [k_edge[i] + passed[tok][i] * moved[i] for i in range(2)]
        r_edge = [r_edge[i] + gb * passed[tok][i] for i in range(2)]
        adjoint = [moved[i] + gb for i in range(2)]
        line = jnp.sum(amp[0] * adjoint[0] + amp[1] * adjoint[1], axis=0, keepdims=True)
        z_edge = jnp.where(row_id == tok, line, z_edge)

    span_c = chunk_of.astype(f32)
    carry = []
    for i in range(2):
        into_late = after[i] * jnp.exp(-rates[i] * (toks * span_c - (fringe - 1.0)))
        into_early = adjoint[i] * jnp.exp(-rates[i] * (toks * (chunks - 1.0 - span_c) + 1.0))
        carry.append(amp[i] * (early * into_early + late * into_late))

    def reply_body(step_index, values):
        tok = half * step_index + (1 - half) * (toks - 1 - step_index)
        keep(part, tok, values[0] + values[1])
        return (values[0] * decay[0], values[1] * decay[1])

    lax.fori_loop(0, toks, reply_body, tuple(carry), unroll=16)

    patch = (row_id < fringe) & (chunk_of == 0) & (jnp.broadcast_to(late, (8, lanes)) > 0.5)
    y_edge = rounded(y_edge)
    z_edge = rounded(z_edge)
    for start, count in ((0, 8), (8, 24), (32, 32), (64, 32), (96, 32)):
        span = slice(start, start + count)
        reply = folded(part, 8 * start, count)
        conv = rounded(fwd_ref[span, :] + late * reply)
        turn = rounded(bwd_ref[span, :] + early * reply)
        hat = [hat_ref[stream, span, :] for stream in range(3)]
        if start == 0:
            conv = jnp.where(patch, y_edge, conv)
            turn = jnp.where(patch, z_edge, turn)
            hat = [jnp.where(patch, hats[stream], hat[stream]) for stream in range(3)]
        grads[0, span, :] = grad_ref[span, :] * conv
        grads[1, span, :] = turn * hat[2]
        grads[2, span, :] = turn * hat[1]
        outs[0, span, :] = hat[0] * conv
    edge_grads = (grad_edge * y_edge, z_edge * hats[2], z_edge * hats[1])
    for stream in range(3):
        head = pltpu.roll(grads[stream, 0:PAD, :], lanes - 1, 1)
        grads[stream, toks : toks + PAD, :] = jnp.where(
            chunk_of < chunks - 1, head, early * edge_grads[stream]
        )
    block = 32
    for stream in range(3):
        for start in range(0, toks, block):
            total = None
            for tap in range(TAPS):
                term = (
                    tap_row(prm_ref, stream, tap)
                    * grads[stream, start + tap : start + tap + block, :]
                )
                total = term if total is None else total + term
            outs[1 + stream, start : start + block, :] = total

    single = jnp.where(chunk_of == 0, scale, 0.0)
    forced = [amp[i] * after[i] for i in range(2)]
    turned = [amp[i] * adjoint[i] for i in range(2)]
    short = [
        edge0[SHORT + 8 * i : SHORT + 8 * i + 8, :] + edge1[SHORT + 8 * i : SHORT + 8 * i + 8, :]
        for i in range(3)
    ]
    for stream in range(3):
        live_grad = edge_grads[stream] * live
        for tap in range(TAPS):
            index = stream * TAPS + tap
            term = live_grad * edges[stream, 8 - tap : 16 - tap, :]
            ref, slot = (edge1, tap) if stream == 0 else (edge0, (stream - 1) * TAPS + tap)
            drive = forced if stream == 0 else turned
            for i in range(2):
                lo = RESPONSE + 16 * slot + 8 * i
                term = term + drive[i] * ref[lo : lo + 8, :]
            line = jnp.sum(term, axis=0, keepdims=True)
            short[index // 8] = short[index // 8] + jnp.where(row_id == index % 8, line, 0.0)
    r_all = []
    k_all = []
    for i in range(2):
        first_r, late_r = pair(edge0, RSUM)[i], pair(edge1, RSUM)[i]
        first_k, late_k = pair(edge0, KSUM)[i], pair(edge1, KSUM)[i]
        lag_early, lag_late = pair(edge0, DERIV)[i], pair(edge1, DERIV)[i]
        r_all.append(first_r + late_r + decay[i] * back[i] * after[i] + r_edge[i])
        k_all.append(
            first_k
            + late_k
            + decay[i] * lag_early * adjoint[i]
            + decay[i] * after[i] * (lag_late - back[i])
            + k_edge[i]
        )
    every = jnp.concatenate(
        [value * single for value in short]
        + [root[i] * r_all[i] * single for i in range(2)]
        + [amp[i] * (0.5 * r_all[i] - rates[i] * k_all[i]) * single for i in range(2)],
        axis=0,
    )
    totals = exact_dot(pick, every, ((1,), (1,)))
    modal_ref[...] = totals[:, 24:56]

    per_tile = toks // chunks
    for stream in range(4):
        for group in range(OWNED // per_tile):
            tile = outs[stream, :, group * toks : (group + 1) * toks].T
            for c in range(per_tile):
                out_rows[
                    pl.ds(stream * OWNED + group * per_tile + c, chunks, stride=ROWS_OUT), :
                ] = tile[c * chunks : (c + 1) * chunks]
    wide = jnp.concatenate([totals[:, 0:24], jnp.zeros((8, toks - 24), f32)], axis=1)
    for group in range(2):
        line = wide[4 * group : 4 * group + 1, :]
        for chan in range(1, 4):
            at = 4 * group + chan
            line = line + pltpu.roll(wide, 32 * chan, 1)[at : at + 1, :]
        upper = rounded(line)
        out_rows[pl.ds(32 + group, chunks, stride=ROWS_OUT), :] = jnp.broadcast_to(
            upper, (chunks, toks)
        )
        out_rows[pl.ds(34 + group, chunks, stride=ROWS_OUT), :] = jnp.broadcast_to(
            line - upper, (chunks, toks)
        )
    for spare in range(36, ROWS_OUT):
        out_rows[pl.ds(spare, chunks, stride=ROWS_OUT), :] = jnp.zeros((chunks, toks), f32)
    send_ref[...] = out_rows[...].reshape(send_ref.shape).astype(jnp.bfloat16)


def run_pack(query_in, key_in, value_in, grad_out):
    chans, toks = query_in.shape
    owners = chans // OWNED
    return pl.pallas_call(
        pack_kernel,
        in_specs=[pl.BlockSpec(memory_space=pltpu.HBM)] * 4,
        out_shape=jax.ShapeDtypeStruct((owners, ROWS_IN, toks), jnp.bfloat16),
        scratch_shapes=[
            pltpu.VMEM((4, chans, toks), jnp.bfloat16),
            pltpu.VMEM((4, chans, toks), jnp.float32),
            pltpu.VMEM((owners * ROWS_IN, toks), jnp.float32),
            pltpu.SemaphoreType.DMA((4,)),
        ],
        compiler_params=pltpu.CompilerParams(vmem_limit_bytes=VMEM_LIMIT),
    )(query_in, key_in, value_in, grad_out)


def run_first(half, recv, prm):
    chunks, _, toks = recv.shape
    lanes = OWNED * chunks
    f32 = jnp.float32
    plane = jax.ShapeDtypeStruct((toks, lanes), f32)
    vmem = pl.BlockSpec(memory_space=pltpu.VMEM)
    return pl.pallas_call(
        first_kernel,
        in_specs=[pl.BlockSpec(memory_space=pltpu.SMEM), vmem, vmem],
        out_shape=(
            plane,
            jax.ShapeDtypeStruct((3, toks, lanes), f32),
            plane,
            plane,
            jax.ShapeDtypeStruct((OWNED, MESSAGE), f32),
        ),
        scratch_shapes=[
            pltpu.VMEM((chunks * ROWS_IN, toks), f32),
            pltpu.VMEM((4, PAD + toks, lanes), f32),
            pltpu.VMEM((toks, lanes), f32),
            pltpu.VMEM((toks, lanes), f32),
            pltpu.VMEM((3, toks, lanes), f32),
            pltpu.VMEM((2, 8 * toks, lanes // 2), f32),
            pltpu.VMEM((2, 8 * toks, lanes // 2), f32),
            pltpu.VMEM((16 * toks, lanes), f32),
            pltpu.VMEM((2 * TAPS, toks, lanes), f32),
            pltpu.VMEM((2, 8 * 24, lanes // 2), f32),
            pltpu.VMEM((MESSAGE, lanes), f32),
        ],
        compiler_params=pltpu.CompilerParams(vmem_limit_bytes=VMEM_LIMIT),
    )(half, recv, prm)


def run_second(half, own, other, prm, grad, hat, fwd, bwd):
    toks, lanes = grad.shape
    chunks = lanes // OWNED
    f32 = jnp.float32
    vmem = pl.BlockSpec(memory_space=pltpu.VMEM)
    return pl.pallas_call(
        second_kernel,
        in_specs=[pl.BlockSpec(memory_space=pltpu.SMEM)] + [vmem] * 7,
        out_shape=(
            jax.ShapeDtypeStruct((chunks, ROWS_OUT, toks), jnp.bfloat16),
            jax.ShapeDtypeStruct((OWNED, 2 * MODES), f32),
        ),
        scratch_shapes=[
            pltpu.VMEM((MESSAGE, lanes), f32),
            pltpu.VMEM((MESSAGE, lanes), f32),
            pltpu.VMEM((3, 16, lanes), f32),
            pltpu.VMEM((2, 8 * toks, lanes // 2), f32),
            pltpu.VMEM((4, toks, lanes), f32),
            pltpu.VMEM((3, toks + PAD, lanes), f32),
            pltpu.VMEM((chunks * ROWS_OUT, toks), f32),
        ],
        compiler_params=pltpu.CompilerParams(vmem_limit_bytes=VMEM_LIMIT),
    )(half, own, other, prm, grad, hat, fwd, bwd)


def run_unpack(recv):
    owners, _, toks = recv.shape
    chans = OWNED * owners
    whole = jax.ShapeDtypeStruct((chans, toks), jnp.bfloat16)
    return pl.pallas_call(
        unpack_kernel,
        out_shape=(whole,) * 4 + (jax.ShapeDtypeStruct((3, TAPS, chans), jnp.float32),),
        scratch_shapes=[
            pltpu.VMEM((owners * ROWS_OUT, toks), jnp.float32),
            pltpu.VMEM((5, chans, toks), jnp.float32),
        ],
        compiler_params=pltpu.CompilerParams(vmem_limit_bytes=VMEM_LIMIT),
    )(recv)


def parameter_rows(weights, residue, log_rate, chunks):
    rows = jnp.concatenate(
        [
            weights.reshape(3 * TAPS, OWNED),
            jnp.zeros((3, OWNED), jnp.float32),
            log_rate.T,
            residue.T,
        ],
        axis=0,
    )
    return jnp.repeat(rows, chunks, axis=1)


def local(query_in, key_in, value_in, short_weight, residue, log_rate, grad_out):
    devices = lax.axis_size("seq")
    chunks = devices // 2
    chans = query_in.shape[0]
    me = lax.axis_index("seq")
    half = me // chunks
    index = me % chunks
    groups = [list(range(chunks)), list(range(chunks, devices))]
    across = [(i, (i + chunks) % devices) for i in range(devices)]

    mine = jnp.concatenate([log_rate, residue], axis=1)
    theirs = lax.ppermute(mine, "seq", across)
    modal_params = jnp.where(
        half == 0, jnp.concatenate([mine, theirs]), jnp.concatenate([theirs, mine])
    )
    weights = jnp.concatenate(
        [
            lax.dynamic_slice(short_weight, (0, 0, 4 * index + at), (3, TAPS, 4))
            for at in (0, chans // 2)
        ],
        axis=2,
    )
    prm = parameter_rows(weights, modal_params[:, MODES:], modal_params[:, :MODES], chunks)
    which = half.reshape(1).astype(jnp.int32)

    send = run_pack(query_in, key_in, value_in, grad_out)
    recv = lax.all_to_all(send, "seq", 0, 0, tiled=True, axis_index_groups=groups)
    grad, hat, fwd, bwd, message = run_first(which, recv, prm)
    other = lax.ppermute(message, "seq", across)
    back, modal = run_second(which, message, other, prm, grad, hat, fwd, bwd)
    final = lax.all_to_all(back, "seq", 0, 0, tiled=True, axis_index_groups=groups)
    output, grad_query, grad_key, grad_value, grad_short = run_unpack(final)
    own_modal = lax.dynamic_slice(modal, (4 * half, 0), (4, 2 * MODES))
    return (
        output,
        grad_query,
        grad_key,
        grad_value,
        grad_short,
        own_modal[:, :MODES],
        own_modal[:, MODES:],
    )


def solution(mesh):
    return jax.shard_map(
        local,
        mesh=mesh,
        in_specs=(
            P("chan", "seq"),
            P("chan", "seq"),
            P("chan", "seq"),
            P(None, None, "chan"),
            P(("chan", "seq"), None),
            P(("chan", "seq"), None),
            P("chan", "seq"),
        ),
        out_specs=(
            P("chan", "seq"),
            P("chan", "seq"),
            P("chan", "seq"),
            P("chan", "seq"),
            P(None, None, "chan"),
            P(("chan", "seq"), None),
            P(("chan", "seq"), None),
        ),
        check_vma=False,
    )
```

time: 85.9 us -> 78 us (0.908)
  the two profiles are of different devices: /device:TPU:33 before, /device:TPU:1 now
where the time goes in v3:
time: 78 us; the launch traced here: 77.3 us
  starting transfers between devices  31.2 us (40%)
  waiting for transfers between devices  27.1 us (35%)
  Pallas kernels  11.6 us (15%)
  local copies, waits for them, and re-layouts  5.74 us (7%)
  other arithmetic  1.01 us (1%)
    ppermute x1, starting transfers between devices, local(): theirs = lax.ppermute(mine, 'seq', across)  16.3 us
    ppermute x1, waiting for transfers between devices, local(): other = lax.ppermute(message, 'seq', across)  11.2 us
    all_to_all x1, waiting for transfers between devices, local(): lax.all_to_all(back, 'seq', 0, 0, tiled=True, axis_index_groups=groups)  8.98 us
    all_to_all x1, starting transfers between devices, local(): lax.all_to_all(send, 'seq', 0, 0, tiled=True, axis_index_groups=groups)  8.05 us
    all_to_all x1, waiting for transfers between devices, local(): lax.all_to_all(send, 'seq', 0, 0, tiled=True, axis_index_groups=groups)  6.89 us
    pallas_call x1, Pallas kernels, run_first(): pl.pallas_call(first_kernel, in_specs=[pl.BlockSpec(memory_space=pltpu.SM...  6.48 us
    all_to_all x1, starting transfers between devices, local(): lax.all_to_all(back, 'seq', 0, 0, tiled=True, axis_index_groups=groups)  4.92 us
    unnamed x14, local copies, waits for them, and re-layouts  4.67 us
  transfers between devices with their start and end apart: 4, of which 3 were waited for; matrix products, arithmetic and copies ran while one was open for 2% of the time, Pallas kernels for 2%

profile of v3, /device:TPU:1, one launch (start us, length us, event | category | flops | bytes accessed | tf_op | source)
XLA Modules:
  0.0 77.3 jit_solution(9609821447459607196)
XLA Ops:
  0.6 0.8 %pad_maximum_fusion.2 = f32[4,32]{1,0:T(4,128)S(1)} fusion(f32[4,16]{1,0:T(4,128)} %param.11, f32[4,16]{1,0:T(4,128)} %param.12), kind=kLoop, calls=%fused_computation.5 | loop fusion | flops 128 | bytes 1024 | tf_op jit(solution)/shard_map/concatenate | solution.py:671
  1.4 16.3 %collective-permute-start = (f32[4,32]{1,0:T(4,128)S(1)}, f32[4,32]{1,0:T(4,128)S(1)}, u32[]{:S(2)}, u32[]{:S(2)}) collective-permute-start(f32[4,32]{1,0:T(4,128)S(1)} %pad_maximum_fusion.2), channel_id=1, source_target_pairs={{0,256},{8,264},{16,272},{24,280},{32,288},{40,296},{48,304},{56,3... | collective-permute-start | bytes 1544 | tf_op jit(solution)/shard_map/ppermute | solution.py:672
  17.7 0.0 copy-start
  17.7 0.8 %copy-done = bf16[256,128]{1,0:T(8,128)(2,1)S(1)} copy-done((bf16[256,128]{1,0:T(8,128)(2,1)S(1)}, bf16[256,128]{1,0:T(8,128)(2,1)}, u32[]{:S(2)}) %copy-start) | copy-done | bytes 65560
  18.5 0.0 copy-start.1
  18.5 0.8 %copy-done.1 = bf16[256,128]{1,0:T(8,128)(2,1)S(1)} copy-done((bf16[256,128]{1,0:T(8,128)(2,1)S(1)}, bf16[256,128]{1,0:T(8,128)(2,1)}, u32[]{:S(2)}) %copy-start.1) | copy-done | bytes 65560
  19.4 0.0 copy-start.2
  19.4 0.8 %copy-done.2 = bf16[256,128]{1,0:T(8,128)(2,1)S(1)} copy-done((bf16[256,128]{1,0:T(8,128)(2,1)S(1)}, bf16[256,128]{1,0:T(8,128)(2,1)}, u32[]{:S(2)}) %copy-start.2) | copy-done | bytes 65560
  20.2 0.0 copy-start.3
  20.2 0.8 %copy-done.3 = bf16[256,128]{1,0:T(8,128)(2,1)S(1)} copy-done((bf16[256,128]{1,0:T(8,128)(2,1)S(1)}, bf16[256,128]{1,0:T(8,128)(2,1)}, u32[]{:S(2)}) %copy-start.3) | copy-done | bytes 65560
  21.0 1.6 %shard_map.126 = bf16[32,32,128]{2,1,0:T(8,128)(2,1)} custom-call(bf16[256,128]{1,0:T(8,128)(2,1)S(1)} %copy-done, bf16[256,128]{1,0:T(8,128)(2,1)S(1)} %copy-done.1, bf16[256,128]{1,0:T(8,128)(2,1)S(1)} %copy-done.2, bf16[256,128]{1,0:T(8,128)(2,1)S(1)} %copy-done.3), custom_call_target="tpu_custom_call" | custom-call | tf_op jit(solution)/shard_map/pallas_call | solution.py:561
  22.6 8.1 %all-to-all-start = ((bf16[32,32,128]{2,1,0:T(8,128)(2,1)}), bf16[32,32,128]{2,1,0:T(8,128)(2,1)S(1)}, u32[]{:S(2)}, u32[]{:S(2)}) async-start(bf16[32,32,128]{2,1,0:T(8,128)(2,1)} %shard_map.126), calls=%async_computation | async-start | bytes 524288 | tf_op jit(solution)/shard_map/all_to_all | solution.py:687
  30.7 0.0 copy-start.4
  30.7 0.7 copy-done.4
  31.4 0.1 constant_dynamic-slice_fusion.2
  31.5 0.1 pad_maximum_fusion
  31.6 0.1 copy.19
  31.6 0.0 copy-start.6
  31.6 0.0 copy-start.5
  31.6 0.1 pad.1.clone
  31.7 0.0 collective-permute-done
  31.7 0.6 copy-done.6
  32.3 0.0 copy-done.5
  32.3 0.1 maximum_select_fusion
  32.4 0.1 slice_bitcast_fusion.1
  32.5 0.1 pad_maximum_fusion.1
  32.6 0.1 copy.17.prm_ref
  32.7 6.9 %all-to-all-done.recv_ref = bf16[32,32,128]{2,1,0:T(8,128)(2,1)S(1)} async-done(((bf16[32,32,128]{2,1,0:T(8,128)(2,1)}), bf16[32,32,128]{2,1,0:T(8,128)(2,1)S(1)}, u32[]{:S(2)}, u32[]{:S(2)}) %all-to-all-start) | async-done | bytes 262176 | tf_op jit(solution)/shard_map/all_to_all | solution.py:687
  39.6 6.5 %shard_map.127 = (f32[128,256]{1,0:T(8,128)S(1)}, f32[3,128,256]{2,1,0:T(8,128)S(1)}, f32[128,256]{1,0:T(8,128)S(1)}, f32[128,256]{1,0:T(8,128)S(1)}, f32[8,384]{1,0:T(8,128)S(1)}) custom-call(s32[1]{0:T(128)} %bitcast.half_ref, bf16[32,32,128]{2,1,0:T(8,128)(2,1)S(1)} %all-to-all-done.recv_ref, f32[56,256]{1,0:T(8,128)S(1)} %copy.17.prm_ref), custom_call_target="tpu_custom_call" | custom-call | tf_op jit(solution)/shard_map/pallas_call | solution.py:581
  46.0 1.9 %collective-permute-start.1 = (f32[8,384]{1,0:T(8,128)S(1)}, f32[8,384]{1,0:T(8,128)S(1)}, u32[]{:S(2)}, u32[]{:S(2)}) collective-permute-start(f32[8,384]{1,0:T(8,128)S(1)} %get-tuple-element.19.own_ref), channel_id=1, source_target_pairs={{0,256},{8,264},{16,272},{24,280},{32,288},{40,296},{48,304},{56,3... | collective-permute-start | bytes 36872 | tf_op jit(solution)/shard_map/ppermute | solution.py:689
  48.0 11.2 %collective-permute-done.1.other_ref = f32[8,384]{1,0:T(8,128)S(1)} collective-permute-done((f32[8,384]{1,0:T(8,128)S(1)}, f32[8,384]{1,0:T(8,128)S(1)}, u32[]{:S(2)}, u32[]{:S(2)}) %collective-permute-start.1) | collective-permute-done | bytes 12320 | tf_op jit(solution)/shard_map/ppermute | solution.py:689
  59.2 2.7 %shard_map.128 = (bf16[32,40,128]{2,1,0:T(8,128)(2,1)}, f32[8,32]{1,0:T(8,128)S(1)}) custom-call(s32[1]{0:T(128)} %bitcast.half_ref, f32[8,384]{1,0:T(8,128)S(1)} %get-tuple-element.19.own_ref, f32[8,384]{1,0:T(8,128)S(1)} %collective-permute-done.1.other_ref, f32[56,256]{1,0:T(8,128)S(1)} %copy.17.prm_ref, f32[128,256]{1,0:T(8,128)S(1)} %get-tuple-element.20.grad_ref, ...), custom_call_target="tpu_custom_call" | custom-call | tf_op jit(solution)/shard_map/pallas_call | solution.py:613
  61.9 4.9 %all-to-all-start.1 = ((bf16[32,40,128]{2,1,0:T(8,128)(2,1)}), bf16[32,40,128]{2,1,0:T(8,128)(2,1)S(1)}, u32[]{:S(2)}, u32[]{:S(2)}) async-start(bf16[32,40,128]{2,1,0:T(8,128)(2,1)} %get-tuple-element.24), calls=%async_computation.1 | async-start | bytes 655360 | tf_op jit(solution)/shard_map/all_to_all | solution.py:691
  66.8 0.7 fusion
  67.5 9.0 %all-to-all-done.1.recv_ref = bf16[32,40,128]{2,1,0:T(8,128)(2,1)S(1)} async-done(((bf16[32,40,128]{2,1,0:T(8,128)(2,1)}), bf16[32,40,128]{2,1,0:T(8,128)(2,1)S(1)}, u32[]{:S(2)}, u32[]{:S(2)}) %all-to-all-start.1) | async-done | bytes 327712 | tf_op jit(solution)/shard_map/all_to_all | solution.py:691
  76.5 0.9 %shard_map.129 = (bf16[256,128]{1,0:T(8,128)(2,1)}, bf16[256,128]{1,0:T(8,128)(2,1)}, bf16[256,128]{1,0:T(8,128)(2,1)}, bf16[256,128]{1,0:T(8,128)(2,1)}, f32[3,7,256]{2,1,0:T(8,128)}) custom-call(bf16[32,40,128]{2,1,0:T(8,128)(2,1)S(1)} %all-to-all-done.1.recv_ref), custom_call_target="tpu_custom_call" | custom-call | tf_op jit(solution)/shard_map/pallas_call | solution.py:637
  (4 shorter events, 0.0 us)
Async XLA Ops:
  1.4 30.3 %collective-permute-start = (f32[4,32]{1,0:T(4,128)S(1)}, f32[4,32]{1,0:T(4,128)S(1)}, u32[]{:S(2)}, u32[]{:S(2)}) collective-permute-start(f32[4,32]{1,0:T(4,128)S(1)} %pad_maximum_fusion.2), channel_id=1, source_target_pairs={{0,256},{8,264},{16,272},{24,280},{32,288},{40,296},{48,304},{56,3... | collective-permute-start | bytes 1544 | tf_op jit(solution)/shard_map/ppermute | solution.py:672
  17.7 0.8 %copy-start = (bf16[256,128]{1,0:T(8,128)(2,1)S(1)}, bf16[256,128]{1,0:T(8,128)(2,1)}, u32[]{:S(2)}) copy-start(bf16[256,128]{1,0:T(8,128)(2,1)} %query_ref.1) | copy-start | bytes 196612
  18.5 0.8 %copy-start.1 = (bf16[256,128]{1,0:T(8,128)(2,1)S(1)}, bf16[256,128]{1,0:T(8,128)(2,1)}, u32[]{:S(2)}) copy-start(bf16[256,128]{1,0:T(8,128)(2,1)} %key_ref.1) | copy-start | bytes 196612
  19.4 0.8 %copy-start.2 = (bf16[256,128]{1,0:T(8,128)(2,1)S(1)}, bf16[256,128]{1,0:T(8,128)(2,1)}, u32[]{:S(2)}) copy-start(bf16[256,128]{1,0:T(8,128)(2,1)} %value_ref.1) | copy-start | bytes 196612
  20.2 0.8 %copy-start.3 = (bf16[256,128]{1,0:T(8,128)(2,1)S(1)}, bf16[256,128]{1,0:T(8,128)(2,1)}, u32[]{:S(2)}) copy-start(bf16[256,128]{1,0:T(8,128)(2,1)} %grad_ref.1) | copy-start | bytes 196612
  22.6 17.0 %all-to-all-start = ((bf16[32,32,128]{2,1,0:T(8,128)(2,1)}), bf16[32,32,128]{2,1,0:T(8,128)(2,1)S(1)}, u32[]{:S(2)}, u32[]{:S(2)}) async-start(bf16[32,32,128]{2,1,0:T(8,128)(2,1)} %shard_map.126), calls=%async_computation | async-start | bytes 524288 | tf_op jit(solution)/shard_map/all_to_all | solution.py:687
  30.7 0.7 copy-start.4
  31.6 0.7 copy-start.6
  31.6 0.7 copy-start.5
  46.0 13.2 %collective-permute-start.1 = (f32[8,384]{1,0:T(8,128)S(1)}, f32[8,384]{1,0:T(8,128)S(1)}, u32[]{:S(2)}, u32[]{:S(2)}) collective-permute-start(f32[8,384]{1,0:T(8,128)S(1)} %get-tuple-element.19.own_ref), channel_id=1, source_target_pairs={{0,256},{8,264},{16,272},{24,280},{32,288},{40,296},{48,304},{56,3... | collective-permute-start | bytes 36872 | tf_op jit(solution)/shard_map/ppermute | solution.py:689
  61.9 14.6 %all-to-all-start.1 = ((bf16[32,40,128]{2,1,0:T(8,128)(2,1)}), bf16[32,40,128]{2,1,0:T(8,128)(2,1)S(1)}, u32[]{:S(2)}, u32[]{:S(2)}) async-start(bf16[32,40,128]{2,1,0:T(8,128)(2,1)} %get-tuple-element.24), calls=%async_computation.1 | async-start | bytes 655360 | tf_op jit(solution)/shard_map/all_to_all | solution.py:691

commit v4 on v3

--- a/solution.py
+++ b/solution.py
@@ -569,7 +569,22 @@
             pltpu.SemaphoreType.DMA((4,)),
         ],
         compiler_params=pltpu.CompilerParams(vmem_limit_bytes=VMEM_LIMIT),
-    )(query_in, key_in, value_in, grad_out)
+    )(*[pltpu.with_memory_space_constraint(x, pltpu.HBM) for x in (query_in, key_in, value_in, grad_out)])
+
+
+def modal_kernel(rate_ref, residue_ref, after_ref, both_ref):
+    both_ref[:, :MODES] = rate_ref[...]
+    both_ref[:, MODES:] = residue_ref[...]
+
+
+def run_modal(log_rate, residue, after):
+    vmem = pl.BlockSpec(memory_space=pltpu.VMEM)
+    return pl.pallas_call(
+        modal_kernel,
+        in_specs=[vmem, vmem, pl.BlockSpec(memory_space=pltpu.HBM)],
+        out_shape=jax.ShapeDtypeStruct((log_rate.shape[0], 2 * MODES), jnp.float32),
+        cost_estimate=pl.CostEstimate(flops=10**10, bytes_accessed=10**8, transcendentals=0),
+    )(log_rate, residue, pltpu.with_memory_space_constraint(after, pltpu.HBM))
 
 
 def run_first(half, recv, prm):
@@ -668,7 +683,8 @@
     groups = [list(range(chunks)), list(range(chunks, devices))]
     across = [(i, (i + chunks) % devices) for i in range(devices)]
 
-    mine = jnp.concatenate([log_rate, residue], axis=1)
+    send = run_pack(query_in, key_in, value_in, grad_out)
+    mine = run_modal(log_rate, residue, send)
     theirs = lax.ppermute(mine, "seq", across)
     modal_params = jnp.where(
         half == 0, jnp.concatenate([mine, theirs]), jnp.concatenate([theirs, mine])
@@ -683,7 +699,6 @@
     prm = parameter_rows(weights, modal_params[:, MODES:], modal_params[:, :MODES], chunks)
     which = half.reshape(1).astype(jnp.int32)
 
-    send = run_pack(query_in, key_in, value_in, grad_out)
     recv = lax.all_to_all(send, "seq", 0, 0, tiled=True, axis_index_groups=groups)
     grad, hat, fwd, bwd, message = run_first(which, recv, prm)
     other = lax.ppermute(message, "seq", across)

time: 78 us -> 72.3 us (0.927)
  waiting for transfers between devices: 27.1 us -> 11.9 us
  starting transfers between devices: 31.2 us -> 44.5 us
  local copies, waits for them, and re-layouts: 5.74 us -> 1.07 us
  Pallas kernels: 11.6 us -> 13.4 us
  other arithmetic: 1.01 us -> 0.16 us
    ppermute x1, starting transfers between devices: 1.95 us -> 10.9 us  [local(): other = lax.ppermute(message, 'seq', across)]
    ppermute x1, waiting for transfers between devices: 11.2 us -> 2.24 us  [local(): other = lax.ppermute(message, 'seq', across)]
    all_to_all x1, waiting for transfers between devices: 6.89 us -> 0.01 us  [local(): lax.all_to_all(send, 'seq', 0, 0, tiled=True, axis_index_groups=groups)]
    unnamed x14 -> x4, local copies, waits for them, and re-layouts: 4.67 us -> 0.01 us
    all_to_all x1, starting transfers between devices: 4.92 us -> 9.41 us  [local(): lax.all_to_all(back, 'seq', 0, 0, tiled=True, axis_index_groups=groups)]
    ppermute x1, starting transfers between devices: 16.3 us -> 13.8 us  [local(): theirs = lax.ppermute(mine, 'seq', across)]
    all_to_all x1, starting transfers between devices: 8.05 us -> 10.4 us  [local(): lax.all_to_all(send, 'seq', 0, 0, tiled=True, axis_index_groups=groups)]
    pallas_call x0 -> x1, Pallas kernels: none -> 1.35 us  [run_modal(): pl.pallas_call(modal_kernel, in_specs=[vmem, vmem, pl.BlockSpec(memory_sp...]
where the time goes in v4:
time: 72.3 us; the launch traced here: 71.8 us
  starting transfers between devices  44.5 us (62%)
  Pallas kernels  13.4 us (19%)
  waiting for transfers between devices  11.9 us (16%)
  local copies, waits for them, and re-layouts  1.07 us (1%)
  between operations  0.75 us (1%)
    ppermute x1, starting transfers between devices, local(): theirs = lax.ppermute(mine, 'seq', across)  13.8 us
    ppermute x1, starting transfers between devices, local(): other = lax.ppermute(message, 'seq', across)  10.9 us
    all_to_all x1, starting transfers between devices, local(): lax.all_to_all(send, 'seq', 0, 0, tiled=True, axis_index_groups=groups)  10.4 us
    all_to_all x1, starting transfers between devices, local(): lax.all_to_all(back, 'seq', 0, 0, tiled=True, axis_index_groups=groups)  9.41 us
    all_to_all x1, waiting for transfers between devices, local(): lax.all_to_all(back, 'seq', 0, 0, tiled=True, axis_index_groups=groups)  8.87 us
    pallas_call x1, Pallas kernels, run_first(): pl.pallas_call(first_kernel, in_specs=[pl.BlockSpec(memory_space=pltpu.SM...  6.48 us
    pallas_call x1, Pallas kernels, run_second(): pl.pallas_call(second_kernel, in_specs=[pl.BlockSpec(memory_space=pltpu.S...  2.66 us
    ppermute x1, waiting for transfers between devices, local(): other = lax.ppermute(message, 'seq', across)  2.24 us
  transfers between devices with their start and end apart: 4, of which 3 were waited for; matrix products, arithmetic and copies ran while one was open for 2% of the time, Pallas kernels for 2%

profile of v4, /device:TPU:1, one launch (start us, length us, event | category | flops | bytes accessed | tf_op | source)
XLA Modules:
  0.0 71.8 jit_solution(5850771900847944101)
XLA Ops:
  0.6 2.1 %shard_map.126.after_ref = bf16[32,32,128]{2,1,0:T(8,128)(2,1)} custom-call(bf16[256,128]{1,0:T(8,128)(2,1)} %query_ref.1, bf16[256,128]{1,0:T(8,128)(2,1)} %key_ref.1, bf16[256,128]{1,0:T(8,128)(2,1)} %value_ref.1, bf16[256,128]{1,0:T(8,128)(2,1)} %grad_ref.1), custom_call_target="tpu_custom_call" | custom-call | tf_op jit(solution)/shard_map/pallas_call | solution.py:561
  2.7 10.4 %all-to-all-start = ((bf16[32,32,128]{2,1,0:T(8,128)(2,1)}), bf16[32,32,128]{2,1,0:T(8,128)(2,1)S(1)}, u32[]{:S(2)}, u32[]{:S(2)}) async-start(bf16[32,32,128]{2,1,0:T(8,128)(2,1)} %shard_map.126.after_ref), calls=%async_computation | async-start | bytes 524288 | tf_op jit(solution)/shard_map/all_to_all | solution.py:702
  13.1 1.3 %shard_map.127 = f32[4,32]{1,0:T(4,128)} custom-call(f32[4,16]{1,0:T(4,128)} %rate_ref.1, f32[4,16]{1,0:T(4,128)} %residue_ref.1, bf16[32,32,128]{2,1,0:T(8,128)(2,1)} %shard_map.126.after_ref), custom_call_target="tpu_custom_call" | custom-call | flops 10000000000 | bytes 100000000 | tf_op jit(solution)/shard_map/pallas_call | solution.py:582
  14.5 0.0 copy-start
  14.5 13.8 %collective-permute-start = (f32[4,32]{1,0:T(4,128)}, f32[4,32]{1,0:T(4,128)S(1)}, u32[]{:S(2)}, u32[]{:S(2)}) collective-permute-start(f32[4,32]{1,0:T(4,128)} %shard_map.127), channel_id=1, source_target_pairs={{0,256},{8,264},{16,272},{24,280},{32,288},{40,296},{48,304},{56,3... | collective-permute-start | bytes 1544 | tf_op jit(solution)/shard_map/ppermute | solution.py:688
  28.3 0.0 copy-done
  28.3 0.1 constant_dynamic-slice_fusion.2
  28.4 0.1 pad_maximum_fusion
  28.4 0.1 copy.19
  28.5 0.0 copy-start.1
  28.5 0.1 pad.1.clone
  28.6 0.8 %collective-permute-done = f32[4,32]{1,0:T(4,128)S(1)} collective-permute-done((f32[4,32]{1,0:T(4,128)}, f32[4,32]{1,0:T(4,128)S(1)}, u32[]{:S(2)}, u32[]{:S(2)}) %collective-permute-start) | collective-permute-done | bytes 544 | tf_op jit(solution)/shard_map/ppermute | solution.py:688
  29.4 0.0 copy-done.1
  29.4 0.1 slice_bitcast_fusion.1
  29.5 0.1 pad_maximum_fusion.1
  29.6 0.1 copy.17.prm_ref
  29.7 0.0 all-to-all-done.recv_ref
  29.7 6.5 %shard_map.128 = (f32[128,256]{1,0:T(8,128)S(1)}, f32[3,128,256]{2,1,0:T(8,128)S(1)}, f32[128,256]{1,0:T(8,128)S(1)}, f32[128,256]{1,0:T(8,128)S(1)}, f32[8,384]{1,0:T(8,128)S(1)}) custom-call(s32[1]{0:T(128)} %bitcast.half_ref, bf16[32,32,128]{2,1,0:T(8,128)(2,1)S(1)} %all-to-all-done.recv_ref, f32[56,256]{1,0:T(8,128)S(1)} %copy.17.prm_ref), custom_call_target="tpu_custom_call" | custom-call | tf_op jit(solution)/shard_map/pallas_call | solution.py:596
  36.2 10.9 %collective-permute-start.1 = (f32[8,384]{1,0:T(8,128)S(1)}, f32[8,384]{1,0:T(8,128)S(1)}, u32[]{:S(2)}, u32[]{:S(2)}) collective-permute-start(f32[8,384]{1,0:T(8,128)S(1)} %get-tuple-element.19.own_ref), channel_id=1, source_target_pairs={{0,256},{8,264},{16,272},{24,280},{32,288},{40,296},{48,304},{56,3... | collective-permute-start | bytes 36872 | tf_op jit(solution)/shard_map/ppermute | solution.py:704
  47.1 2.2 %collective-permute-done.1.other_ref = f32[8,384]{1,0:T(8,128)S(1)} collective-permute-done((f32[8,384]{1,0:T(8,128)S(1)}, f32[8,384]{1,0:T(8,128)S(1)}, u32[]{:S(2)}, u32[]{:S(2)}) %collective-permute-start.1) | collective-permute-done | bytes 12320 | tf_op jit(solution)/shard_map/ppermute | solution.py:704
  49.3 2.7 %shard_map.129 = (bf16[32,40,128]{2,1,0:T(8,128)(2,1)}, f32[8,32]{1,0:T(8,128)S(1)}) custom-call(s32[1]{0:T(128)} %bitcast.half_ref, f32[8,384]{1,0:T(8,128)S(1)} %get-tuple-element.19.own_ref, f32[8,384]{1,0:T(8,128)S(1)} %collective-permute-done.1.other_ref, f32[56,256]{1,0:T(8,128)S(1)} %copy.17.prm_ref, f32[128,256]{1,0:T(8,128)S(1)} %get-tuple-element.20.grad_ref, ...), custom_call_target="tpu_custom_call" | custom-call | tf_op jit(solution)/shard_map/pallas_call | solution.py:628
  52.0 9.4 %all-to-all-start.1 = ((bf16[32,40,128]{2,1,0:T(8,128)(2,1)}), bf16[32,40,128]{2,1,0:T(8,128)(2,1)S(1)}, u32[]{:S(2)}, u32[]{:S(2)}) async-start(bf16[32,40,128]{2,1,0:T(8,128)(2,1)} %get-tuple-element.24), calls=%async_computation.1 | async-start | bytes 655360 | tf_op jit(solution)/shard_map/all_to_all | solution.py:706
  61.4 0.7 fusion
  62.1 8.9 %all-to-all-done.1.recv_ref = bf16[32,40,128]{2,1,0:T(8,128)(2,1)S(1)} async-done(((bf16[32,40,128]{2,1,0:T(8,128)(2,1)}), bf16[32,40,128]{2,1,0:T(8,128)(2,1)S(1)}, u32[]{:S(2)}, u32[]{:S(2)}) %all-to-all-start.1) | async-done | bytes 327712 | tf_op jit(solution)/shard_map/all_to_all | solution.py:706
  71.0 0.9 %shard_map.130 = (bf16[256,128]{1,0:T(8,128)(2,1)}, bf16[256,128]{1,0:T(8,128)(2,1)}, bf16[256,128]{1,0:T(8,128)(2,1)}, bf16[256,128]{1,0:T(8,128)(2,1)}, f32[3,7,256]{2,1,0:T(8,128)}) custom-call(bf16[32,40,128]{2,1,0:T(8,128)(2,1)S(1)} %all-to-all-done.1.recv_ref), custom_call_target="tpu_custom_call" | custom-call | tf_op jit(solution)/shard_map/pallas_call | solution.py:652
  (5 shorter events, 0.0 us)
Async XLA Ops:
  2.7 27.0 %all-to-all-start = ((bf16[32,32,128]{2,1,0:T(8,128)(2,1)}), bf16[32,32,128]{2,1,0:T(8,128)(2,1)S(1)}, u32[]{:S(2)}, u32[]{:S(2)}) async-start(bf16[32,32,128]{2,1,0:T(8,128)(2,1)} %shard_map.126.after_ref), calls=%async_computation | async-start | bytes 524288 | tf_op jit(solution)/shard_map/all_to_all | solution.py:702
  14.5 13.8 %copy-start = (f32[3,7,256]{2,1,0:T(8,128)S(1)}, f32[3,7,256]{2,1,0:T(8,128)}, u32[]{:S(2)}) copy-start(f32[3,7,256]{2,1,0:T(8,128)} %param.10) | copy-start | bytes 64516
  14.5 14.9 %collective-permute-start = (f32[4,32]{1,0:T(4,128)}, f32[4,32]{1,0:T(4,128)S(1)}, u32[]{:S(2)}, u32[]{:S(2)}) collective-permute-start(f32[4,32]{1,0:T(4,128)} %shard_map.127), channel_id=1, source_target_pairs={{0,256},{8,264},{16,272},{24,280},{32,288},{40,296},{48,304},{56,3... | collective-permute-start | bytes 1544 | tf_op jit(solution)/shard_map/ppermute | solution.py:688
  28.5 0.9 %copy-start.1 = (f32[4,32]{1,0:T(4,128)S(1)}, f32[4,32]{1,0:T(4,128)}, u32[]{:S(2)}) copy-start(f32[4,32]{1,0:T(4,128)} %shard_map.127) | copy-start | bytes 1540
  36.2 13.2 %collective-permute-start.1 = (f32[8,384]{1,0:T(8,128)S(1)}, f32[8,384]{1,0:T(8,128)S(1)}, u32[]{:S(2)}, u32[]{:S(2)}) collective-permute-start(f32[8,384]{1,0:T(8,128)S(1)} %get-tuple-element.19.own_ref), channel_id=1, source_target_pairs={{0,256},{8,264},{16,272},{24,280},{32,288},{40,296},{48,304},{56,3... | collective-permute-start | bytes 36872 | tf_op jit(solution)/shard_map/ppermute | solution.py:704
  52.0 19.0 %all-to-all-start.1 = ((bf16[32,40,128]{2,1,0:T(8,128)(2,1)}), bf16[32,40,128]{2,1,0:T(8,128)(2,1)S(1)}, u32[]{:S(2)}, u32[]{:S(2)}) async-start(bf16[32,40,128]{2,1,0:T(8,128)(2,1)} %get-tuple-element.24), calls=%async_computation.1 | async-start | bytes 655360 | tf_op jit(solution)/shard_map/all_to_all | solution.py:706

commit v5 on v3

--- a/solution.py
+++ b/solution.py
@@ -15,7 +15,8 @@
 ROWS_OUT = 40
 VMEM_LIMIT = 40 * 1024 * 1024
 
-STATE, DERIV, RSUM, KSUM, EDGE, SHORT, RESPONSE, MESSAGE = 0, 16, 32, 48, 64, 96, 128, 384
+STATE, DERIV, RSUM, KSUM, EDGE, SHORT, COMPACT = 0, 16, 32, 48, 64, 96, 128
+MESSAGE = OWNED + 16
 
 
 def first_row(chan, chans):
@@ -75,14 +76,40 @@
     return (owner == lax.broadcasted_iota(jnp.int32, owner.shape, 0)).astype(jnp.float32)
 
 
-def exact_dot(left, right, dims):
+def three_parts(value):
+    upper = rounded(value)
+    middle = rounded(value - upper)
+    return [upper, middle, value - upper - middle]
+
+
+def lane_sums(value, chunks):
+    shape = (value.shape[1], 128)
+    owner = lax.broadcasted_iota(jnp.int32, shape, 0) // chunks
+    pick = (owner == lax.broadcasted_iota(jnp.int32, shape, 1)).astype(jnp.float32)
+    pick = pick.astype(jnp.bfloat16)
+    total = None
+    for part in reversed(three_parts(value)):
+        term = jnp.dot(part.astype(jnp.bfloat16), pick, preferred_element_type=jnp.float32)
+        total = term if total is None else total + term
+    return total
+
+
+def lane_spread(value, chunks):
+    pick = owner_pick(chunks)
     return lax.dot_general(
-        left,
-        right,
-        (dims, ((), ())),
-        precision=lax.Precision.HIGHEST,
+        jnp.concatenate(three_parts(value), axis=0).astype(jnp.bfloat16),
+        jnp.concatenate([pick] * 3, axis=0).astype(jnp.bfloat16),
+        (((0,), (0,)), ((), ())),
         preferred_element_type=jnp.float32,
     )
+
+
+def one_line(value, first, count, width):
+    line = value[first : first + 1, :]
+    for chan in range(1, count):
+        at = first + chan
+        line = line + pltpu.roll(value, width * chan, 1)[at : at + 1, :]
+    return line
 
 
 def modal_rows(prm_ref):
@@ -126,6 +153,7 @@
     half_ref,
     recv_ref,
     prm_ref,
+    rate_ref,
     grad_ref,
     hat_ref,
     fwd_ref,
@@ -139,7 +167,8 @@
     part_y,
     part_z,
     states,
-    weighted,
+    upper_w,
+    lower_w,
     sums,
     rows,
 ):
@@ -285,42 +314,48 @@
     for index in range(3 * TAPS, 24):
         keep(sums, index, zero)
     rows[SHORT : SHORT + 24, :] = folded(sums, 0, 24)
-    rows[SHORT + 24 : RESPONSE, :] = zero
-
-    def fill(slot, stream):
+    rows[SHORT + 24 : COMPACT, :] = zero
+
+    bf16 = jnp.bfloat16
+    rate_line = jnp.exp(rate_ref[...])
+    rate_line = jnp.concatenate([rate_line, jnp.zeros((OWNED, toks - MODES), f32)], axis=1)
+    rate_line = one_line(rate_line, 0, OWNED, MODES)
+    row_lane = lax.broadcasted_iota(jnp.int32, (lanes, toks), 0)
+    col_owner = lax.broadcasted_iota(jnp.int32, (lanes, toks), 1) // MODES
+    row_chunk = (row_lane % chunks).astype(f32)
+    spread = late * (toks * row_chunk - (TAPS - 2.0)) + early * (
+        toks * (chunks - 1.0 - row_chunk) + 1.0
+    )
+    across = jnp.where(row_lane // chunks == col_owner, jnp.exp(-rate_line * spread), 0.0)
+    across_hi = across.astype(bf16)
+    across_lo = (across - across_hi.astype(f32)).astype(bf16)
+    row_tok = lax.broadcasted_iota(jnp.int32, (toks, toks), 0).astype(f32)
+    along = jnp.exp(-rate_line * (late * row_tok + early * (toks - 1.0 - row_tok)))
+
+    def respond(slot, stream):
         for tap in range(TAPS):
             for start in range(0, toks, block):
+                span = slice(start, start + block)
                 lo = PAD - tap + start
-                weighted[slot + tap, start : start + block, :] = (
-                    base[stream, start : start + block, :] * xt[stream, lo : lo + block, :]
-                )
+                value = base[stream, span, :] * xt[stream, lo : lo + block, :]
+                upper = value.astype(bf16)
+                upper_w[tap, span, :] = upper
+                lower_w[tap, span, :] = (value - upper.astype(f32)).astype(bf16)
+            total = (
+                jnp.dot(upper_w[tap], across_lo, preferred_element_type=f32)
+                + jnp.dot(lower_w[tap], across_hi, preferred_element_type=f32)
+                + jnp.dot(upper_w[tap], across_hi, preferred_element_type=f32)
+            )
+            at = OWNED + slot + tap
+            msg_ref[at : at + 1, :] = jnp.sum(total * along, axis=0, keepdims=True)
 
     span_c = chunk_of.astype(f32)
-    power_early = [jnp.exp(-r * (toks * (chunks - 1.0 - span_c) + 1.0)) for r in rates]
-    power_late = [jnp.exp(-r * (toks * span_c - (TAPS - 2.0))) for r in rates]
-
-    def respond(slot, powers, reverse):
-        def body(step_index, carry):
-            tok = toks - 1 - step_index if reverse else step_index
-            out = []
-            for tap in range(TAPS):
-                wb = row_of(weighted.at[slot + tap], tok)
-                for i in range(2):
-                    out.append(decay[i] * carry[2 * tap + i] + wb)
-            return tuple(out)
-
-        total = lax.fori_loop(0, toks, body, (zero,) * (2 * TAPS), unroll=8)
-        for tap in range(TAPS):
-            for i in range(2):
-                lo = RESPONSE + 16 * (slot + tap) + 8 * i
-                rows[lo : lo + 8, :] = total[2 * tap + i] * powers[i]
+    msg_ref[OWNED:MESSAGE, :] = jnp.zeros((MESSAGE - OWNED, toks), f32)
 
     @pl.when(half == 0)
     def _():
-        fill(0, 1)
-        fill(TAPS, 2)
-        respond(0, power_early, False)
-        respond(TAPS, power_early, False)
+        respond(0, 1)
+        respond(TAPS, 2)
         for stream in range(4):
             lo = EDGE + 8 * stream
             rows[lo : lo + 8, :] = jnp.where(
@@ -335,10 +370,7 @@
 
     @pl.when(half != 0)
     def _():
-        fill(0, 0)
-        respond(0, power_late, True)
-        for lo in range(RESPONSE + 16 * TAPS, RESPONSE + 32 * TAPS, 8):
-            rows[lo : lo + 8, :] = zero
+        respond(0, 0)
         for stream in range(4):
             lo = EDGE + 8 * stream
             rows[lo : lo + 8, :] = jnp.where(chunk_of == 0, xt[stream, PAD : 2 * PAD, :], 0.0)
@@ -354,9 +386,7 @@
     for i in range(2):
         rows[RSUM + 8 * i : RSUM + 8 * i + 8, :] = (r0, r1)[i]
         rows[KSUM + 8 * i : KSUM + 8 * i + 8, :] = (k0, k1)[i]
-    for lo in range(RESPONSE + 32 * TAPS, MESSAGE, 8):
-        rows[lo : lo + 8, :] = zero
-    msg_ref[...] = exact_dot(owner_pick(chunks), rows[...], ((1,), (1,)))
+    msg_ref[0:OWNED, :] = lane_sums(rows[...], chunks).T[:OWNED, :]
 
 
 def second_kernel(
@@ -374,6 +404,7 @@
     edge1,
     edges,
     part,
+    driven,
     outs,
     grads,
     out_rows,
@@ -387,14 +418,15 @@
     late = half.astype(f32)
     early = 1.0 - late
     rates, decay, root, amp = modal_rows(prm_ref)
-    pick = owner_pick(chunks)
     fringe = TAPS - 1
     zero = jnp.zeros((8, lanes), f32)
 
     own = own_ref[...]
     other = other_ref[...]
-    edge0[...] = exact_dot(own * early + other * late, pick, ((0,), (0,)))
-    edge1[...] = exact_dot(own * late + other * early, pick, ((0,), (0,)))
+    message0 = own * early + other * late
+    message1 = own * late + other * early
+    edge0[...] = lane_spread(message0[0:OWNED, :], chunks)
+    edge1[...] = lane_spread(message1[0:OWNED, :], chunks)
 
     def pair(ref, first):
         return [ref[first + 8 * i : first + 8 * i + 8, :] for i in range(2)]
@@ -445,19 +477,37 @@
         into_early = adjoint[i] * jnp.exp(-rates[i] * (toks * (chunks - 1.0 - span_c) + 1.0))
         carry.append(amp[i] * (early * into_early + late * into_late))
 
-    def reply_body(step_index, values):
-        tok = half * step_index + (1 - half) * (toks - 1 - step_index)
-        keep(part, tok, values[0] + values[1])
-        return (values[0] * decay[0], values[1] * decay[1])
-
-    lax.fori_loop(0, toks, reply_body, tuple(carry), unroll=16)
+    sub = row_id.astype(f32)[:, :128]
+    sub = late * sub + early * (7.0 - sub)
+    stride8 = [jnp.exp(-8.0 * r) for r in rates]
+    blocks = toks // 8
+    for cut in range(lanes // 128):
+        cols = slice(cut * 128, (cut + 1) * 128)
+        modes = []
+        factors = []
+        for i in range(2):
+            for m in range(8):
+                rate = jnp.broadcast_to(rates[i][m : m + 1, cols], (8, 128))
+                lead = jnp.broadcast_to(carry[i][m : m + 1, cols], (8, 128))
+                modes.append(lead * jnp.exp(-rate * sub))
+                factors.append(jnp.broadcast_to(stride8[i][m : m + 1, cols], (8, 128)))
+
+        def reply_body(step_index, values, cols=cols, factors=factors):
+            at = half * step_index + (1 - half) * (blocks - 1 - step_index)
+            total = list(values)
+            while len(total) > 1:
+                total = [total[k] + total[k + 1] for k in range(0, len(total), 2)]
+            part[pl.ds(pl.multiple_of(8 * at, 8), 8), cols] = total[0]
+            return tuple(v * f for v, f in zip(values, factors))
+
+        lax.fori_loop(0, blocks, reply_body, tuple(modes), unroll=4)
 
     patch = (row_id < fringe) & (chunk_of == 0) & (jnp.broadcast_to(late, (8, lanes)) > 0.5)
     y_edge = rounded(y_edge)
     z_edge = rounded(z_edge)
     for start, count in ((0, 8), (8, 24), (32, 32), (64, 32), (96, 32)):
         span = slice(start, start + count)
-        reply = folded(part, 8 * start, count)
+        reply = part[span, :]
         conv = rounded(fwd_ref[span, :] + late * reply)
         turn = rounded(bwd_ref[span, :] + early * reply)
         hat = [hat_ref[stream, span, :] for stream in range(3)]
@@ -488,8 +538,20 @@
             outs[1 + stream, start : start + block, :] = total
 
     single = jnp.where(chunk_of == 0, scale, 0.0)
-    forced = [amp[i] * after[i] for i in range(2)]
-    turned = [amp[i] * adjoint[i] for i in range(2)]
+    drives = jnp.concatenate(
+        [amp[i] * after[i] * single for i in range(2)]
+        + [amp[i] * adjoint[i] * single for i in range(2)]
+        + [jnp.zeros((toks - 4 * 8, lanes), f32)],
+        axis=0,
+    )
+    drives = lane_sums(drives, chunks).T[:OWNED, :]
+    in_first = lax.broadcasted_iota(jnp.int32, (OWNED, toks), 1) < MODES
+    forced = one_line(jnp.where(in_first, drives, 0.0), 0, OWNED, MODES)
+    turned = pltpu.roll(drives, toks - MODES, 1)
+    turned = one_line(jnp.where(in_first, turned, 0.0), 0, OWNED, MODES)
+    driven[0:TAPS, :] = message1[OWNED : OWNED + TAPS, :] * forced
+    driven[TAPS : 3 * TAPS, :] = message0[OWNED : OWNED + 2 * TAPS, :] * turned
+    driven[3 * TAPS : 24, :] = jnp.zeros((24 - 3 * TAPS, toks), f32)
     short = [
         edge0[SHORT + 8 * i : SHORT + 8 * i + 8, :] + edge1[SHORT + 8 * i : SHORT + 8 * i + 8, :]
         for i in range(3)
@@ -499,11 +561,6 @@
         for tap in range(TAPS):
             index = stream * TAPS + tap
             term = live_grad * edges[stream, 8 - tap : 16 - tap, :]
-            ref, slot = (edge1, tap) if stream == 0 else (edge0, (stream - 1) * TAPS + tap)
-            drive = forced if stream == 0 else turned
-            for i in range(2):
-                lo = RESPONSE + 16 * slot + 8 * i
-                term = term + drive[i] * ref[lo : lo + 8, :]
             line = jnp.sum(term, axis=0, keepdims=True)
             short[index // 8] = short[index // 8] + jnp.where(row_id == index % 8, line, 0.0)
     r_all = []
@@ -520,13 +577,18 @@
             + decay[i] * after[i] * (lag_late - back[i])
             + k_edge[i]
         )
-    every = jnp.concatenate(
+    columns = jnp.concatenate(
         [value * single for value in short]
         + [root[i] * r_all[i] * single for i in range(2)]
         + [amp[i] * (0.5 * r_all[i] - rates[i] * k_all[i]) * single for i in range(2)],
         axis=0,
     )
-    totals = exact_dot(pick, every, ((1,), (1,)))
+    columns = lane_sums(columns, chunks)
+    replies = lane_sums(driven[...], MODES)
+    columns = jnp.concatenate(
+        [columns[0:24, :] + replies, columns[24:56, :], jnp.zeros((128 - 56, 128), f32)], axis=0
+    )
+    totals = columns.T[:OWNED, :]
     modal_ref[...] = totals[:, 24:56]
 
     per_tile = toks // chunks
@@ -539,10 +601,7 @@
                 ] = tile[c * chunks : (c + 1) * chunks]
     wide = jnp.concatenate([totals[:, 0:24], jnp.zeros((8, toks - 24), f32)], axis=1)
     for group in range(2):
-        line = wide[4 * group : 4 * group + 1, :]
-        for chan in range(1, 4):
-            at = 4 * group + chan
-            line = line + pltpu.roll(wide, 32 * chan, 1)[at : at + 1, :]
+        line = one_line(wide, 4 * group, 4, 32)
         upper = rounded(line)
         out_rows[pl.ds(32 + group, chunks, stride=ROWS_OUT), :] = jnp.broadcast_to(
             upper, (chunks, toks)
@@ -569,10 +628,25 @@
             pltpu.SemaphoreType.DMA((4,)),
         ],
         compiler_params=pltpu.CompilerParams(vmem_limit_bytes=VMEM_LIMIT),
-    )(query_in, key_in, value_in, grad_out)
-
-
-def run_first(half, recv, prm):
+    )(*[pltpu.with_memory_space_constraint(x, pltpu.HBM) for x in (query_in, key_in, value_in, grad_out)])
+
+
+def modal_kernel(both_ref, after_ref, out_ref):
+    out_ref[...] = both_ref[...]
+
+
+def run_modal(both, after):
+    vmem = pl.BlockSpec(memory_space=pltpu.VMEM)
+    return pl.pallas_call(
+        modal_kernel,
+        in_specs=[vmem, pl.BlockSpec(memory_space=pltpu.HBM)],
+        out_specs=vmem,
+        out_shape=jax.ShapeDtypeStruct(both.shape, jnp.float32),
+        cost_estimate=pl.CostEstimate(flops=2 * 10**10, bytes_accessed=1024, transcendentals=0),
+    )(both, pltpu.with_memory_space_constraint(after, pltpu.HBM))
+
+
+def run_first(half, recv, prm, log_rate):
     chunks, _, toks = recv.shape
     lanes = OWNED * chunks
     f32 = jnp.float32
@@ -580,13 +654,13 @@
     vmem = pl.BlockSpec(memory_space=pltpu.VMEM)
     return pl.pallas_call(
         first_kernel,
-        in_specs=[pl.BlockSpec(memory_space=pltpu.SMEM), vmem, vmem],
+        in_specs=[pl.BlockSpec(memory_space=pltpu.SMEM), vmem, vmem, vmem],
         out_shape=(
             plane,
             jax.ShapeDtypeStruct((3, toks, lanes), f32),
             plane,
             plane,
-            jax.ShapeDtypeStruct((OWNED, MESSAGE), f32),
+            jax.ShapeDtypeStruct((MESSAGE, toks), f32),
         ),
         scratch_shapes=[
             pltpu.VMEM((chunks * ROWS_IN, toks), f32),
@@ -597,12 +671,13 @@
             pltpu.VMEM((2, 8 * toks, lanes // 2), f32),
             pltpu.VMEM((2, 8 * toks, lanes // 2), f32),
             pltpu.VMEM((16 * toks, lanes), f32),
-            pltpu.VMEM((2 * TAPS, toks, lanes), f32),
+            pltpu.VMEM((TAPS, toks, lanes), jnp.bfloat16),
+            pltpu.VMEM((TAPS, toks, lanes), jnp.bfloat16),
             pltpu.VMEM((2, 8 * 24, lanes // 2), f32),
-            pltpu.VMEM((MESSAGE, lanes), f32),
+            pltpu.VMEM((COMPACT, lanes), f32),
         ],
         compiler_params=pltpu.CompilerParams(vmem_limit_bytes=VMEM_LIMIT),
-    )(half, recv, prm)
+    )(half, recv, prm, log_rate)
 
 
 def run_second(half, own, other, prm, grad, hat, fwd, bwd):
@@ -618,10 +693,11 @@
             jax.ShapeDtypeStruct((OWNED, 2 * MODES), f32),
         ),
         scratch_shapes=[
-            pltpu.VMEM((MESSAGE, lanes), f32),
-            pltpu.VMEM((MESSAGE, lanes), f32),
+            pltpu.VMEM((COMPACT, lanes), f32),
+            pltpu.VMEM((COMPACT, lanes), f32),
             pltpu.VMEM((3, 16, lanes), f32),
-            pltpu.VMEM((2, 8 * toks, lanes // 2), f32),
+            pltpu.VMEM((toks, lanes), f32),
+            pltpu.VMEM((24, toks), f32),
             pltpu.VMEM((4, toks, lanes), f32),
             pltpu.VMEM((3, toks + PAD, lanes), f32),
             pltpu.VMEM((chunks * ROWS_OUT, toks), f32),
@@ -668,7 +744,8 @@
     groups = [list(range(chunks)), list(range(chunks, devices))]
     across = [(i, (i + chunks) % devices) for i in range(devices)]
 
-    mine = jnp.concatenate([log_rate, residue], axis=1)
+    send = run_pack(query_in, key_in, value_in, grad_out)
+    mine = run_modal(jnp.concatenate([log_rate, residue], axis=1), send)
     theirs = lax.ppermute(mine, "seq", across)
     modal_params = jnp.where(
         half == 0, jnp.concatenate([mine, theirs]), jnp.concatenate([theirs, mine])
@@ -683,9 +760,8 @@
     prm = parameter_rows(weights, modal_params[:, MODES:], modal_params[:, :MODES], chunks)
     which = half.reshape(1).astype(jnp.int32)
 
-    send = run_pack(query_in, key_in, value_in, grad_out)
     recv = lax.all_to_all(send, "seq", 0, 0, tiled=True, axis_index_groups=groups)
-    grad, hat, fwd, bwd, message = run_first(which, recv, prm)
+    grad, hat, fwd, bwd, message = run_first(which, recv, prm, modal_params[:, :MODES])
     other = lax.ppermute(message, "seq", across)
     back, modal = run_second(which, message, other, prm, grad, hat, fwd, bwd)
     final = lax.all_to_all(back, "seq", 0, 0, tiled=True, axis_index_groups=groups)

time: 78 us -> 71 us (0.910)
  waiting for transfers between devices: 27.1 us -> 11.2 us
  starting transfers between devices: 31.2 us -> 45.1 us
  local copies, waits for them, and re-layouts: 5.74 us -> 1.09 us
    ppermute x1, waiting for transfers between devices: 11.2 us -> 1.56 us  [local(): other = lax.ppermute(message, 'seq', across)]
    ppermute x1, starting transfers between devices: 1.95 us -> 11.6 us  [local(): other = lax.ppermute(message, 'seq', across)]
    all_to_all x1, waiting for transfers between devices: 6.89 us -> 0.01 us  [local(): lax.all_to_all(send, 'seq', 0, 0, tiled=True, axis_index_groups=groups)]
    unnamed x14 -> x8, local copies, waits for them, and re-layouts: 4.67 us -> 0.02 us
    all_to_all x1, starting transfers between devices: 4.92 us -> 9.4 us  [local(): lax.all_to_all(back, 'seq', 0, 0, tiled=True, axis_index_groups=groups)]
    ppermute x1, starting transfers between devices: 16.3 us -> 13.8 us  [local(): theirs = lax.ppermute(mine, 'seq', across)]
    all_to_all x1, starting transfers between devices: 8.05 us -> 10.4 us  [local(): lax.all_to_all(send, 'seq', 0, 0, tiled=True, axis_index_groups=groups)]
    pallas_call x1, Pallas kernels: 6.48 us -> 5.07 us  [run_first(): pl.pallas_call(first_kernel, in_specs=[pl.BlockSpec(memory_space=pltpu.SM...]
  transfers between devices with their start and end apart: 4 -> 4, of which waited for: 3 -> 3; matrix products, arithmetic and copies ran while one was open for 2% -> 3% of each run, Pallas kernels for 2% -> 2%
where the time goes in v5:
time: 71 us; the launch traced here: 70.5 us
  starting transfers between devices  45.1 us (64%)
  Pallas kernels  11.5 us (16%)
  waiting for transfers between devices  11.2 us (16%)
  local copies, waits for them, and re-layouts  1.09 us (2%)
  other arithmetic  0.82 us (1%)
  between operations  0.78 us (1%)
    ppermute x1, starting transfers between devices, local(): theirs = lax.ppermute(mine, 'seq', across)  13.8 us
    ppermute x1, starting transfers between devices, local(): other = lax.ppermute(message, 'seq', across)  11.6 us
    all_to_all x1, starting transfers between devices, local(): lax.all_to_all(send, 'seq', 0, 0, tiled=True, axis_index_groups=groups)  10.4 us
    all_to_all x1, starting transfers between devices, local(): lax.all_to_all(back, 'seq', 0, 0, tiled=True, axis_index_groups=groups)  9.4 us
    all_to_all x1, waiting for transfers between devices, local(): lax.all_to_all(back, 'seq', 0, 0, tiled=True, axis_index_groups=groups)  8.87 us
    pallas_call x1, Pallas kernels, run_first(): pl.pallas_call(first_kernel, in_specs=[pl.BlockSpec(memory_space=pltpu.SM...  5.07 us
    pallas_call x1, Pallas kernels, run_second(): pl.pallas_call(second_kernel, in_specs=[pl.BlockSpec(memory_space=pltpu.S...  2.2 us
    pallas_call x1, Pallas kernels, run_pack(): pl.pallas_call(pack_kernel, in_specs=[pl.BlockSpec(memory_space=pltpu.HBM...  2.08 us
  transfers between devices with their start and end apart: 4, of which 3 were waited for; matrix products, arithmetic and copies ran while one was open for 3% of the time, Pallas kernels for 2%

profile of v5, /device:TPU:1, one launch (start us, length us, event | category | flops | bytes accessed | tf_op | source)
XLA Modules:
  0.0 70.5 jit_solution(9135778615703238187)
XLA Ops:
  0.6 2.1 %shard_map.126.after_ref = bf16[32,32,128]{2,1,0:T(8,128)(2,1)} custom-call(bf16[256,128]{1,0:T(8,128)(2,1)} %query_ref.1, bf16[256,128]{1,0:T(8,128)(2,1)} %key_ref.1, bf16[256,128]{1,0:T(8,128)(2,1)} %value_ref.1, bf16[256,128]{1,0:T(8,128)(2,1)} %grad_ref.1), custom_call_target="tpu_custom_call" | custom-call | tf_op jit(solution)/shard_map/pallas_call | solution.py:620
  2.7 0.0 copy-start.1
  2.7 0.0 copy-start.2
  2.7 10.4 %all-to-all-start = ((bf16[32,32,128]{2,1,0:T(8,128)(2,1)}), bf16[32,32,128]{2,1,0:T(8,128)(2,1)S(1)}, u32[]{:S(2)}, u32[]{:S(2)}) async-start(bf16[32,32,128]{2,1,0:T(8,128)(2,1)} %shard_map.126.after_ref), calls=%async_computation | async-start | bytes 524288 | tf_op jit(solution)/shard_map/all_to_all | solution.py:763
  13.2 0.0 copy-done.1
  13.2 0.0 copy-done.2
  13.2 0.7 pad_maximum_fusion.2.both_ref
  13.8 1.3 %shard_map.127 = f32[4,32]{1,0:T(4,128)} custom-call(f32[4,32]{1,0:T(4,128)} %pad_maximum_fusion.2.both_ref, bf16[32,32,128]{2,1,0:T(8,128)(2,1)} %shard_map.126.after_ref), custom_call_target="tpu_custom_call" | custom-call | flops 20000000000 | bytes 1024 | tf_op jit(solution)/shard_map/pallas_call | solution.py:640
  15.1 0.0 copy-start
  15.1 13.8 %collective-permute-start = (f32[4,32]{1,0:T(4,128)}, f32[4,32]{1,0:T(4,128)S(1)}, u32[]{:S(2)}, u32[]{:S(2)}) collective-permute-start(f32[4,32]{1,0:T(4,128)} %shard_map.127), channel_id=1, source_target_pairs={{0,256},{8,264},{16,272},{24,280},{32,288},{40,296},{48,304},{56,3... | collective-permute-start | bytes 1544 | tf_op jit(solution)/shard_map/ppermute | solution.py:749
  28.9 0.0 copy-done
  28.9 0.1 constant_dynamic-slice_fusion.2
  29.0 0.1 pad_maximum_fusion
  29.1 0.1 copy.19
  29.1 0.0 copy-start.3
  29.1 0.1 pad.1.clone
  29.2 0.8 %collective-permute-done = f32[4,32]{1,0:T(4,128)S(1)} collective-permute-done((f32[4,32]{1,0:T(4,128)}, f32[4,32]{1,0:T(4,128)S(1)}, u32[]{:S(2)}, u32[]{:S(2)}) %collective-permute-start) | collective-permute-done | bytes 544 | tf_op jit(solution)/shard_map/ppermute | solution.py:749
  30.0 0.0 copy-done.3
  30.0 0.1 fusion
  30.1 0.1 pad_maximum_fusion.1
  30.2 0.1 copy.17.prm_ref
  30.3 0.0 all-to-all-done.recv_ref
  30.3 5.1 %shard_map.128 = (f32[128,256]{1,0:T(8,128)S(1)}, f32[3,128,256]{2,1,0:T(8,128)S(1)}, f32[128,256]{1,0:T(8,128)S(1)}, f32[128,256]{1,0:T(8,128)S(1)}, f32[24,128]{1,0:T(8,128)S(1)}) custom-call(s32[1]{0:T(128)} %bitcast.half_ref, bf16[32,32,128]{2,1,0:T(8,128)(2,1)S(1)} %all-to-all-done.recv_ref, f32[56,256]{1,0:T(8,128)S(1)} %copy.17.prm_ref, ...), custom_call_target="tpu_custom_call" | custom-call | tf_op jit(solution)/shard_map/pallas_call | solution.py:655
  35.4 11.6 %collective-permute-start.1 = (f32[24,128]{1,0:T(8,128)S(1)}, f32[24,128]{1,0:T(8,128)S(1)}, u32[]{:S(2)}, u32[]{:S(2)}) collective-permute-start(f32[24,128]{1,0:T(8,128)S(1)} %get-tuple-element.19.own_ref), channel_id=1, source_target_pairs={{0,256},{8,264},{16,272},{24,280},{32,288},{40,296},{48,304},{56,3... | collective-permute-start | bytes 36872 | tf_op jit(solution)/shard_map/ppermute | solution.py:765
  47.0 1.6 %collective-permute-done.1.other_ref = f32[24,128]{1,0:T(8,128)S(1)} collective-permute-done((f32[24,128]{1,0:T(8,128)S(1)}, f32[24,128]{1,0:T(8,128)S(1)}, u32[]{:S(2)}, u32[]{:S(2)}) %collective-permute-start.1) | collective-permute-done | bytes 12320 | tf_op jit(solution)/shard_map/ppermute | solution.py:765
  48.5 2.2 %shard_map.129 = (bf16[32,40,128]{2,1,0:T(8,128)(2,1)}, f32[8,32]{1,0:T(8,128)S(1)}) custom-call(s32[1]{0:T(128)} %bitcast.half_ref, f32[24,128]{1,0:T(8,128)S(1)} %get-tuple-element.19.own_ref, f32[24,128]{1,0:T(8,128)S(1)} %collective-permute-done.1.other_ref, f32[56,256]{1,0:T(8,128)S(1)} %copy.17.prm_ref, f32[128,256]{1,0:T(8,128)S(1)} %get-tuple-element.20.grad_ref, ...), custom_call_target="tpu_custom_call" | custom-call | tf_op jit(solution)/shard_map/pallas_call | solution.py:688
  50.7 9.4 %all-to-all-start.1 = ((bf16[32,40,128]{2,1,0:T(8,128)(2,1)}), bf16[32,40,128]{2,1,0:T(8,128)(2,1)S(1)}, u32[]{:S(2)}, u32[]{:S(2)}) async-start(bf16[32,40,128]{2,1,0:T(8,128)(2,1)} %get-tuple-element.24), calls=%async_computation.1 | async-start | bytes 655360 | tf_op jit(solution)/shard_map/all_to_all | solution.py:767
  60.1 0.7 fusion.1
  60.8 8.9 %all-to-all-done.1.recv_ref = bf16[32,40,128]{2,1,0:T(8,128)(2,1)S(1)} async-done(((bf16[32,40,128]{2,1,0:T(8,128)(2,1)}), bf16[32,40,128]{2,1,0:T(8,128)(2,1)S(1)}, u32[]{:S(2)}, u32[]{:S(2)}) %all-to-all-start.1) | async-done | bytes 327712 | tf_op jit(solution)/shard_map/all_to_all | solution.py:767
  69.7 0.9 %shard_map.130 = (bf16[256,128]{1,0:T(8,128)(2,1)}, bf16[256,128]{1,0:T(8,128)(2,1)}, bf16[256,128]{1,0:T(8,128)(2,1)}, bf16[256,128]{1,0:T(8,128)(2,1)}, f32[3,7,256]{2,1,0:T(8,128)}) custom-call(bf16[32,40,128]{2,1,0:T(8,128)(2,1)S(1)} %all-to-all-done.1.recv_ref), custom_call_target="tpu_custom_call" | custom-call | tf_op jit(solution)/shard_map/pallas_call | solution.py:713
  (5 shorter events, 0.0 us)
Async XLA Ops:
  2.7 10.4 %copy-start.1 = (f32[4,16]{1,0:T(4,128)S(1)}, f32[4,16]{1,0:T(4,128)}, u32[]{:S(2)}) copy-start(f32[4,16]{1,0:T(4,128)} %param.11) | copy-start | bytes 772
  2.7 10.4 %copy-start.2 = (f32[4,16]{1,0:T(4,128)S(1)}, f32[4,16]{1,0:T(4,128)}, u32[]{:S(2)}) copy-start(f32[4,16]{1,0:T(4,128)} %param.12) | copy-start | bytes 772
  2.7 27.6 %all-to-all-start = ((bf16[32,32,128]{2,1,0:T(8,128)(2,1)}), bf16[32,32,128]{2,1,0:T(8,128)(2,1)S(1)}, u32[]{:S(2)}, u32[]{:S(2)}) async-start(bf16[32,32,128]{2,1,0:T(8,128)(2,1)} %shard_map.126.after_ref), calls=%async_computation | async-start | bytes 524288 | tf_op jit(solution)/shard_map/all_to_all | solution.py:763
  15.1 13.8 %copy-start = (f32[3,7,256]{2,1,0:T(8,128)S(1)}, f32[3,7,256]{2,1,0:T(8,128)}, u32[]{:S(2)}) copy-start(f32[3,7,256]{2,1,0:T(8,128)} %param.10) | copy-start | bytes 64516
  15.1 14.9 %collective-permute-start = (f32[4,32]{1,0:T(4,128)}, f32[4,32]{1,0:T(4,128)S(1)}, u32[]{:S(2)}, u32[]{:S(2)}) collective-permute-start(f32[4,32]{1,0:T(4,128)} %shard_map.127), channel_id=1, source_target_pairs={{0,256},{8,264},{16,272},{24,280},{32,288},{40,296},{48,304},{56,3... | collective-permute-start | bytes 1544 | tf_op jit(solution)/shard_map/ppermute | solution.py:749
  29.1 0.9 %copy-start.3 = (f32[4,32]{1,0:T(4,128)S(1)}, f32[4,32]{1,0:T(4,128)}, u32[]{:S(2)}) copy-start(f32[4,32]{1,0:T(4,128)} %shard_map.127) | copy-start | bytes 1540
  35.4 13.2 %collective-permute-start.1 = (f32[24,128]{1,0:T(8,128)S(1)}, f32[24,128]{1,0:T(8,128)S(1)}, u32[]{:S(2)}, u32[]{:S(2)}) collective-permute-start(f32[24,128]{1,0:T(8,128)S(1)} %get-tuple-element.19.own_ref), channel_id=1, source_target_pairs={{0,256},{8,264},{16,272},{24,280},{32,288},{40,296},{48,304},{56,3... | collective-permute-start | bytes 36872 | tf_op jit(solution)/shard_map/ppermute | solution.py:765
  50.7 18.9 %all-to-all-start.1 = ((bf16[32,40,128]{2,1,0:T(8,128)(2,1)}), bf16[32,40,128]{2,1,0:T(8,128)(2,1)S(1)}, u32[]{:S(2)}, u32[]{:S(2)}) async-start(bf16[32,40,128]{2,1,0:T(8,128)(2,1)} %get-tuple-element.24), calls=%async_computation.1 | async-start | bytes 655360 | tf_op jit(solution)/shard_map/all_to_all | solution.py:767

commit v6 on v5

--- a/solution.py
+++ b/solution.py
@@ -13,7 +13,7 @@
 OWNED = 8
 ROWS_IN = 4 * OWNED
 ROWS_OUT = 40
-VMEM_LIMIT = 40 * 1024 * 1024
+VMEM_LIMIT = 16 * 1024 * 1024
 
 STATE, DERIV, RSUM, KSUM, EDGE, SHORT, COMPACT = 0, 16, 32, 48, 64, 96, 128
 MESSAGE = OWNED + 16
@@ -112,9 +112,9 @@
     return line
 
 
-def modal_rows(prm_ref):
-    rates = [jnp.exp(prm_ref[24 + 8 * i : 32 + 8 * i, :]) for i in range(2)]
-    resid = [prm_ref[40 + 8 * i : 48 + 8 * i, :] for i in range(2)]
+def modal_rows(modal_ref):
+    rates = [jnp.exp(modal_ref[8 * i : 8 * i + 8, :]) for i in range(2)]
+    resid = [modal_ref[16 + 8 * i : 24 + 8 * i, :] for i in range(2)]
     decay = [jnp.exp(-r) for r in rates]
     root = [jnp.sqrt(2.0 * r) for r in rates]
     amp = [resid[i] * root[i] for i in range(2)]
@@ -140,37 +140,27 @@
     return jnp.concatenate(halves, axis=1)
 
 
-def tap_row(prm_ref, stream, tap):
+def tap_row(taps_ref, stream, tap):
     index = stream * TAPS + tap
-    return prm_ref[index : index + 1, :]
+    return taps_ref[index : index + 1, :]
 
 
 def rounded(value):
     return value.astype(jnp.bfloat16).astype(jnp.float32)
 
 
-def first_kernel(
+def filter_kernel(
     half_ref,
     recv_ref,
-    prm_ref,
-    rate_ref,
-    grad_ref,
+    taps_ref,
+    xt,
     hat_ref,
-    fwd_ref,
-    bwd_ref,
-    msg_ref,
-    raw,
-    xt,
     mixed,
     gmixed,
     base,
-    part_y,
-    part_z,
-    states,
     upper_w,
     lower_w,
-    sums,
-    rows,
+    raw,
 ):
     chunks = recv_ref.shape[0]
     toks = recv_ref.shape[2]
@@ -179,8 +169,6 @@
     chunk_of, _ = lane_ids(chunks, 8)
     half = half_ref[0]
     late = half.astype(f32)
-    early = 1.0 - late
-    zero = jnp.zeros((8, lanes), f32)
     block = 32
 
     raw[...] = recv_ref[...].reshape(raw.shape).astype(f32)
@@ -209,14 +197,13 @@
             total = None
             for tap in range(TAPS):
                 lo = PAD - tap + start
-                term = tap_row(prm_ref, stream, tap) * xt[stream, lo : lo + block, :]
+                term = tap_row(taps_ref, stream, tap) * xt[stream, lo : lo + block, :]
                 total = term if total is None else total + term
             filtered.append(total)
             hat_ref[stream, start : start + block, :] = total
         grad = xt[3, PAD + start : PAD + start + block, :]
         mixed[start : start + block, :] = rounded(filtered[1] * filtered[2])
         gmixed[start : start + block, :] = rounded(grad * filtered[0])
-        grad_ref[start : start + block, :] = grad
         base[0, start : start + block, :] = grad
         base[1, start : start + block, :] = filtered[2]
         base[2, start : start + block, :] = filtered[1]
@@ -225,7 +212,56 @@
     for stream in range(3):
         base[stream, 0:8, :] = base[stream, 0:8, :] * kept
 
-    rates, decay, _, amp = modal_rows(prm_ref)
+    def weigh(slot, stream):
+        for tap in range(TAPS):
+            for start in range(0, toks, block):
+                span = slice(start, start + block)
+                lo = PAD - tap + start
+                value = base[stream, span, :] * xt[stream, lo : lo + block, :]
+                upper = value.astype(jnp.bfloat16)
+                upper_w[slot + tap, span, :] = upper
+                lower_w[slot + tap, span, :] = (value - upper.astype(f32)).astype(jnp.bfloat16)
+
+    @pl.when(half == 0)
+    def _():
+        weigh(0, 1)
+        weigh(TAPS, 2)
+
+    @pl.when(half != 0)
+    def _():
+        weigh(0, 0)
+
+
+def first_kernel(
+    half_ref,
+    modal_ref,
+    rate_ref,
+    xt,
+    mixed,
+    gmixed,
+    base,
+    upper_w,
+    lower_w,
+    fwd_ref,
+    bwd_ref,
+    msg_ref,
+    part_y,
+    part_z,
+    states,
+    sums,
+    rows,
+):
+    toks, lanes = mixed.shape
+    chunks = lanes // OWNED
+    f32 = jnp.float32
+    chunk_of, _ = lane_ids(chunks, 8)
+    half = half_ref[0]
+    late = half.astype(f32)
+    early = 1.0 - late
+    zero = jnp.zeros((8, lanes), f32)
+    block = 32
+
+    rates, decay, _, amp = modal_rows(modal_ref)
 
     def row_of(ref, tok):
         return jnp.broadcast_to(ref[pl.ds(tok, 1), :], (8, lanes))
@@ -332,21 +368,14 @@
     row_tok = lax.broadcasted_iota(jnp.int32, (toks, toks), 0).astype(f32)
     along = jnp.exp(-rate_line * (late * row_tok + early * (toks - 1.0 - row_tok)))
 
-    def respond(slot, stream):
-        for tap in range(TAPS):
-            for start in range(0, toks, block):
-                span = slice(start, start + block)
-                lo = PAD - tap + start
-                value = base[stream, span, :] * xt[stream, lo : lo + block, :]
-                upper = value.astype(bf16)
-                upper_w[tap, span, :] = upper
-                lower_w[tap, span, :] = (value - upper.astype(f32)).astype(bf16)
+    def respond(slot):
+        for tap in range(slot, slot + TAPS):
             total = (
                 jnp.dot(upper_w[tap], across_lo, preferred_element_type=f32)
                 + jnp.dot(lower_w[tap], across_hi, preferred_element_type=f32)
                 + jnp.dot(upper_w[tap], across_hi, preferred_element_type=f32)
             )
-            at = OWNED + slot + tap
+            at = OWNED + tap
             msg_ref[at : at + 1, :] = jnp.sum(total * along, axis=0, keepdims=True)
 
     span_c = chunk_of.astype(f32)
@@ -354,8 +383,8 @@
 
     @pl.when(half == 0)
     def _():
-        respond(0, 1)
-        respond(TAPS, 2)
+        respond(0)
+        respond(TAPS)
         for stream in range(4):
             lo = EDGE + 8 * stream
             rows[lo : lo + 8, :] = jnp.where(
@@ -370,7 +399,7 @@
 
     @pl.when(half != 0)
     def _():
-        respond(0, 0)
+        respond(0)
         for stream in range(4):
             lo = EDGE + 8 * stream
             rows[lo : lo + 8, :] = jnp.where(chunk_of == 0, xt[stream, PAD : 2 * PAD, :], 0.0)
@@ -393,13 +422,14 @@
     half_ref,
     own_ref,
     other_ref,
-    prm_ref,
-    grad_ref,
+    taps_ref,
+    modal_ref,
+    xt,
     hat_ref,
     fwd_ref,
     bwd_ref,
     send_ref,
-    modal_ref,
+    sums_ref,
     edge0,
     edge1,
     edges,
@@ -409,7 +439,7 @@
     grads,
     out_rows,
 ):
-    toks, lanes = grad_ref.shape
+    toks, lanes = fwd_ref.shape
     chunks = lanes // OWNED
     f32 = jnp.float32
     chunk_of, _ = lane_ids(chunks, 8)
@@ -417,7 +447,7 @@
     half = half_ref[0]
     late = half.astype(f32)
     early = 1.0 - late
-    rates, decay, root, amp = modal_rows(prm_ref)
+    rates, decay, root, amp = modal_rows(modal_ref)
     fringe = TAPS - 1
     zero = jnp.zeros((8, lanes), f32)
 
@@ -439,7 +469,7 @@
         edges[stream, 8:16, :] = edge1[EDGE + 8 * stream : EDGE + 8 * stream + 8, :]
         total = None
         for tap in range(TAPS):
-            term = tap_row(prm_ref, stream, tap) * edges[stream, 8 - tap : 16 - tap, :]
+            term = tap_row(taps_ref, stream, tap) * edges[stream, 8 - tap : 16 - tap, :]
             total = term if total is None else total + term
         hats.append(total)
     grad_edge = edge1[EDGE + 24 : EDGE + 32, :]
@@ -515,7 +545,7 @@
             conv = jnp.where(patch, y_edge, conv)
             turn = jnp.where(patch, z_edge, turn)
             hat = [jnp.where(patch, hats[stream], hat[stream]) for stream in range(3)]
-        grads[0, span, :] = grad_ref[span, :] * conv
+        grads[0, span, :] = xt[3, PAD + start : PAD + start + count, :] * conv
         grads[1, span, :] = turn * hat[2]
         grads[2, span, :] = turn * hat[1]
         outs[0, span, :] = hat[0] * conv
@@ -531,7 +561,7 @@
             total = None
             for tap in range(TAPS):
                 term = (
-                    tap_row(prm_ref, stream, tap)
+                    tap_row(taps_ref, stream, tap)
                     * grads[stream, start + tap : start + tap + block, :]
                 )
                 total = term if total is None else total + term
@@ -589,7 +619,7 @@
         [columns[0:24, :] + replies, columns[24:56, :], jnp.zeros((128 - 56, 128), f32)], axis=0
     )
     totals = columns.T[:OWNED, :]
-    modal_ref[...] = totals[:, 24:56]
+    sums_ref[...] = totals[:, 24:56]
 
     per_tile = toks // chunks
     for stream in range(4):
@@ -643,54 +673,66 @@
         out_specs=vmem,
         out_shape=jax.ShapeDtypeStruct(both.shape, jnp.float32),
         cost_estimate=pl.CostEstimate(flops=2 * 10**10, bytes_accessed=1024, transcendentals=0),
+        compiler_params=pltpu.CompilerParams(vmem_limit_bytes=1024 * 1024),
     )(both, pltpu.with_memory_space_constraint(after, pltpu.HBM))
 
 
-def run_first(half, recv, prm, log_rate):
+def plane(*shape, dtype=jnp.float32):
+    return jax.ShapeDtypeStruct(shape, dtype)
+
+
+def run_filter(half, recv, taps):
     chunks, _, toks = recv.shape
     lanes = OWNED * chunks
+    vmem = pl.BlockSpec(memory_space=pltpu.VMEM)
+    return pl.pallas_call(
+        filter_kernel,
+        in_specs=[pl.BlockSpec(memory_space=pltpu.SMEM), vmem, vmem],
+        out_shape=(
+            plane(4, PAD + toks, lanes),
+            plane(3, toks, lanes),
+            plane(toks, lanes),
+            plane(toks, lanes),
+            plane(3, toks, lanes),
+            plane(2 * TAPS, toks, lanes, dtype=jnp.bfloat16),
+            plane(2 * TAPS, toks, lanes, dtype=jnp.bfloat16),
+        ),
+        scratch_shapes=[pltpu.VMEM((chunks * ROWS_IN, toks), jnp.float32)],
+        cost_estimate=pl.CostEstimate(flops=2 * 10**10, bytes_accessed=1024, transcendentals=0),
+        compiler_params=pltpu.CompilerParams(vmem_limit_bytes=VMEM_LIMIT),
+    )(half, recv, taps)
+
+
+def run_first(half, modal, log_rate, xt, mixed, gmixed, base, upper_w, lower_w):
+    toks, lanes = mixed.shape
     f32 = jnp.float32
-    plane = jax.ShapeDtypeStruct((toks, lanes), f32)
     vmem = pl.BlockSpec(memory_space=pltpu.VMEM)
     return pl.pallas_call(
         first_kernel,
-        in_specs=[pl.BlockSpec(memory_space=pltpu.SMEM), vmem, vmem, vmem],
-        out_shape=(
-            plane,
-            jax.ShapeDtypeStruct((3, toks, lanes), f32),
-            plane,
-            plane,
-            jax.ShapeDtypeStruct((MESSAGE, toks), f32),
-        ),
+        in_specs=[pl.BlockSpec(memory_space=pltpu.SMEM)] + [vmem] * 8,
+        out_shape=(plane(toks, lanes), plane(toks, lanes), plane(MESSAGE, toks)),
         scratch_shapes=[
-            pltpu.VMEM((chunks * ROWS_IN, toks), f32),
-            pltpu.VMEM((4, PAD + toks, lanes), f32),
-            pltpu.VMEM((toks, lanes), f32),
-            pltpu.VMEM((toks, lanes), f32),
-            pltpu.VMEM((3, toks, lanes), f32),
             pltpu.VMEM((2, 8 * toks, lanes // 2), f32),
             pltpu.VMEM((2, 8 * toks, lanes // 2), f32),
             pltpu.VMEM((16 * toks, lanes), f32),
-            pltpu.VMEM((TAPS, toks, lanes), jnp.bfloat16),
-            pltpu.VMEM((TAPS, toks, lanes), jnp.bfloat16),
             pltpu.VMEM((2, 8 * 24, lanes // 2), f32),
             pltpu.VMEM((COMPACT, lanes), f32),
         ],
         compiler_params=pltpu.CompilerParams(vmem_limit_bytes=VMEM_LIMIT),
-    )(half, recv, prm, log_rate)
-
-
-def run_second(half, own, other, prm, grad, hat, fwd, bwd):
-    toks, lanes = grad.shape
+    )(half, modal, log_rate, xt, mixed, gmixed, base, upper_w, lower_w)
+
+
+def run_second(half, own, other, taps, modal, xt, hat, fwd, bwd):
+    toks, lanes = fwd.shape
     chunks = lanes // OWNED
     f32 = jnp.float32
     vmem = pl.BlockSpec(memory_space=pltpu.VMEM)
     return pl.pallas_call(
         second_kernel,
-        in_specs=[pl.BlockSpec(memory_space=pltpu.SMEM)] + [vmem] * 7,
+        in_specs=[pl.BlockSpec(memory_space=pltpu.SMEM)] + [vmem] * 8,
         out_shape=(
-            jax.ShapeDtypeStruct((chunks, ROWS_OUT, toks), jnp.bfloat16),
-            jax.ShapeDtypeStruct((OWNED, 2 * MODES), f32),
+            plane(chunks, ROWS_OUT, toks, dtype=jnp.bfloat16),
+            plane(OWNED, 2 * MODES),
         ),
         scratch_shapes=[
             pltpu.VMEM((COMPACT, lanes), f32),
@@ -703,7 +745,7 @@
             pltpu.VMEM((chunks * ROWS_OUT, toks), f32),
         ],
         compiler_params=pltpu.CompilerParams(vmem_limit_bytes=VMEM_LIMIT),
-    )(half, own, other, prm, grad, hat, fwd, bwd)
+    )(half, own, other, taps, modal, xt, hat, fwd, bwd)
 
 
 def run_unpack(recv):
@@ -721,15 +763,9 @@
     )(recv)
 
 
-def parameter_rows(weights, residue, log_rate, chunks):
+def tap_rows(weights, chunks):
     rows = jnp.concatenate(
-        [
-            weights.reshape(3 * TAPS, OWNED),
-            jnp.zeros((3, OWNED), jnp.float32),
-            log_rate.T,
-            residue.T,
-        ],
-        axis=0,
+        [weights.reshape(3 * TAPS, OWNED), jnp.zeros((3, OWNED), jnp.float32)], axis=0
     )
     return jnp.repeat(rows, chunks, axis=1)
 
@@ -747,9 +783,6 @@
     send = run_pack(query_in, key_in, value_in, grad_out)
     mine = run_modal(jnp.concatenate([log_rate, residue], axis=1), send)
     theirs = lax.ppermute(mine, "seq", across)
-    modal_params = jnp.where(
-        half == 0, jnp.concatenate([mine, theirs]), jnp.concatenate([theirs, mine])
-    )
     weights = jnp.concatenate(
         [
             lax.dynamic_slice(short_weight, (0, 0, 4 * index + at), (3, TAPS, 4))
@@ -757,16 +790,22 @@
         ],
         axis=2,
     )
-    prm = parameter_rows(weights, modal_params[:, MODES:], modal_params[:, :MODES], chunks)
+    taps = tap_rows(weights, chunks)
     which = half.reshape(1).astype(jnp.int32)
 
     recv = lax.all_to_all(send, "seq", 0, 0, tiled=True, axis_index_groups=groups)
-    grad, hat, fwd, bwd, message = run_first(which, recv, prm, modal_params[:, :MODES])
+    xt, hat, *inner = run_filter(which, recv, taps)
+    theirs, inner = lax.optimization_barrier((theirs, inner))
+    modal_params = jnp.where(
+        half == 0, jnp.concatenate([mine, theirs]), jnp.concatenate([theirs, mine])
+    )
+    modal = jnp.repeat(modal_params.T, chunks, axis=1)
+    fwd, bwd, message = run_first(which, modal, modal_params[:, :MODES], xt, *inner)
     other = lax.ppermute(message, "seq", across)
-    back, modal = run_second(which, message, other, prm, grad, hat, fwd, bwd)
+    back, sums = run_second(which, message, other, taps, modal, xt, hat, fwd, bwd)
     final = lax.all_to_all(back, "seq", 0, 0, tiled=True, axis_index_groups=groups)
     output, grad_query, grad_key, grad_value, grad_short = run_unpack(final)
-    own_modal = lax.dynamic_slice(modal, (4 * half, 0), (4, 2 * MODES))
+    own_modal = lax.dynamic_slice(sums, (4 * half, 0), (4, 2 * MODES))
     return (
         output,
         grad_query,

time: 71 us -> 71.8 us (1.011)
  local copies, waits for them, and re-layouts: 1.09 us -> 5.03 us
  starting transfers between devices: 45.1 us -> 41.9 us
  waiting for transfers between devices: 11.2 us -> 12.9 us
  Pallas kernels: 11.5 us -> 10.4 us
    unnamed x8 -> x14, local copies, waits for them, and re-layouts: 0.02 us -> 3.84 us
    ppermute x1, starting transfers between devices: 11.6 us -> 9.08 us  [local(): other = lax.ppermute(message, 'seq', across)]
    ppermute x1, waiting for transfers between devices: 1.56 us -> 4.05 us  [local(): other = lax.ppermute(message, 'seq', across)]
    pallas_call x1, Pallas kernels: 1.26 us -> 0.01 us  [run_modal(): pl.pallas_call(modal_kernel, in_specs=[vmem, pl.BlockSpec(memory_space=pl...]
    pallas_call x0 -> x1, Pallas kernels: none -> 1.13 us  [run_filter(): pl.pallas_call(filter_kernel, in_specs=[pl.BlockSpec(memory_space=pltpu.S...]
    pallas_call x1, Pallas kernels: 5.07 us -> 4.14 us  [run_first(): pl.pallas_call(first_kernel, in_specs=[pl.BlockSpec(memory_space=pltpu.SM...]
    ppermute x1, waiting for transfers between devices: 0.81 us -> 0.01 us  [local(): theirs = lax.ppermute(mine, 'seq', across)]
  transfers between devices with their start and end apart: 4 -> 4, of which waited for: 3 -> 2; matrix products, arithmetic and copies ran while one was open for 3% -> 2% of each run, Pallas kernels for 2% -> 2%
where the time goes in v6:
time: 71.8 us; the launch traced here: 71.3 us
  starting transfers between devices  41.9 us (58%)
  waiting for transfers between devices  12.9 us (18%)
  Pallas kernels  10.4 us (14%)
  local copies, waits for them, and re-layouts  5.03 us (7%)
  between operations  0.84 us (1%)
    ppermute x1, starting transfers between devices, local(): theirs = lax.ppermute(mine, 'seq', across)  13.6 us
    all_to_all x1, starting transfers between devices, local(): lax.all_to_all(send, 'seq', 0, 0, tiled=True, axis_index_groups=groups)  10.4 us
    ppermute x1, starting transfers between devices, local(): other = lax.ppermute(message, 'seq', across)  9.08 us
    all_to_all x1, waiting for transfers between devices, local(): lax.all_to_all(back, 'seq', 0, 0, tiled=True, axis_index_groups=groups)  8.87 us
    all_to_all x1, starting transfers between devices, local(): lax.all_to_all(back, 'seq', 0, 0, tiled=True, axis_index_groups=groups)  8.81 us
    pallas_call x1, Pallas kernels, run_first(): pl.pallas_call(first_kernel, in_specs=[pl.BlockSpec(memory_space=pltpu.SM...  4.14 us
    ppermute x1, waiting for transfers between devices, local(): other = lax.ppermute(message, 'seq', across)  4.05 us
    unnamed x14, local copies, waits for them, and re-layouts  3.84 us
  transfers between devices with their start and end apart: 4, of which 2 were waited for; matrix products, arithmetic and copies ran while one was open for 2% of the time, Pallas kernels for 2%

profile of v6, /device:TPU:1, one launch (start us, length us, event | category | flops | bytes accessed | tf_op | source)
XLA Modules:
  0.0 71.3 jit_solution(16383992813607976157)
XLA Ops:
  0.6 2.1 %shard_map.126.after_ref = bf16[32,32,128]{2,1,0:T(8,128)(2,1)} custom-call(bf16[256,128]{1,0:T(8,128)(2,1)} %query_ref.1, bf16[256,128]{1,0:T(8,128)(2,1)} %key_ref.1, bf16[256,128]{1,0:T(8,128)(2,1)} %value_ref.1, bf16[256,128]{1,0:T(8,128)(2,1)} %grad_ref.1), custom_call_target="tpu_custom_call" | custom-call | tf_op jit(solution)/shard_map/pallas_call | solution.py:650
  2.7 0.0 copy-start.5
  2.7 0.0 copy-start.6
  2.8 10.4 %all-to-all-start = ((bf16[32,32,128]{2,1,0:T(8,128)(2,1)}), bf16[32,32,128]{2,1,0:T(8,128)(2,1)S(1)}, u32[]{:S(2)}, u32[]{:S(2)}) async-start(bf16[32,32,128]{2,1,0:T(8,128)(2,1)} %shard_map.126.after_ref), calls=%async_computation | async-start | bytes 524288 | tf_op jit(solution)/shard_map/all_to_all | solution.py:796
  13.2 0.0 copy-done.5
  13.2 0.0 copy-done.6
  13.2 0.1 pad_maximum_fusion.1.both_ref
  13.3 13.6 %collective-permute-start = (f32[4,32]{1,0:T(4,128)S(1)}, f32[4,32]{1,0:T(4,128)S(1)}, u32[]{:S(2)}, u32[]{:S(2)}) collective-permute-start(f32[4,32]{1,0:T(4,128)S(1)} %shard_map.127), channel_id=1, source_target_pairs={{0,256},{8,264},{16,272},{24,280},{32,288},{40,296},{48,304},{56,3... | collective-permute-start | bytes 1544 | tf_op jit(solution)/shard_map/ppermute | solution.py:785
  26.9 0.0 copy-start.4
  26.9 0.7 copy-done.4
  27.6 0.1 constant_dynamic-slice_fusion.2
  27.7 0.1 pad_maximum_fusion
  27.8 0.1 broadcast_in_dim.6
  27.9 0.1 reshape.28.taps_ref
  28.0 0.0 all-to-all-done.recv_ref
  28.0 1.1 %shard_map.128 = (f32[4,136,256]{2,1,0:T(8,128)S(1)}, f32[3,128,256]{2,1,0:T(8,128)S(1)}, f32[128,256]{1,0:T(8,128)S(1)}, f32[128,256]{1,0:T(8,128)S(1)}, f32[3,...) custom-call(s32[1]{0:T(128)} %bitcast.half_ref, ...), custom_call_target="tpu_custom_call" | custom-call | flops 20000000000 | bytes 1024 | tf_op jit(solution)/shard_map/pallas_call | solution.py:688
  29.2 0.0 copy-start
  29.2 0.7 copy-done
  29.8 0.0 copy-start.2
  29.8 0.7 copy-done.2
  30.5 0.0 collective-permute-done
  30.5 0.1 copy.17
  30.6 0.1 broadcast_in_dim.7
  30.7 0.1 reshape.29.modal_ref
  30.8 0.0 copy-start.1
  30.8 0.9 %copy-done.1 = f32[128,256]{1,0:T(8,128)S(1)} copy-done((f32[128,256]{1,0:T(8,128)S(1)}, f32[128,256]{1,0:T(8,128)}, u32[]{:S(2)}) %copy-start.1) | copy-done | bytes 131096
  31.7 0.0 copy-start.3
  31.7 0.9 %copy-done.3 = f32[128,256]{1,0:T(8,128)S(1)} copy-done((f32[128,256]{1,0:T(8,128)S(1)}, f32[128,256]{1,0:T(8,128)}, u32[]{:S(2)}) %copy-start.3) | copy-done | bytes 131096
  32.6 4.1 %shard_map.129 = (f32[128,256]{1,0:T(8,128)S(1)}, f32[128,256]{1,0:T(8,128)S(1)}, f32[24,128]{1,0:T(8,128)S(1)}) custom-call(s32[1]{0:T(128)} %bitcast.half_ref, f32[32,256]{1,0:T(8,128)S(1)} %reshape.29.modal_ref, f32[8,16]{1,0:T(8,128)S(1)} %bitcast.4, f32[4,136,256]{2,1,0:T(8,128)S(1)} %get-tuple-element.36.xt, f32[128,256]{1,0:T(8,128)S(1)} %copy-done.1, ...), custom_call_target="tpu_custom_call" | custom-call | tf_op jit(solution)/shard_map/pallas_call | solution.py:710
  36.7 9.1 %collective-permute-start.1 = (f32[24,128]{1,0:T(8,128)S(1)}, f32[24,128]{1,0:T(8,128)S(1)}, u32[]{:S(2)}, u32[]{:S(2)}) collective-permute-start(f32[24,128]{1,0:T(8,128)S(1)} %get-tuple-element.42.own_ref), channel_id=1, source_target_pairs={{0,256},{8,264},{16,272},{24,280},{32,288},{40,296},{48,304},{56,3... | collective-permute-start | bytes 36872 | tf_op jit(solution)/shard_map/ppermute | solution.py:804
  45.8 4.0 %collective-permute-done.1.other_ref = f32[24,128]{1,0:T(8,128)S(1)} collective-permute-done((f32[24,128]{1,0:T(8,128)S(1)}, f32[24,128]{1,0:T(8,128)S(1)}, u32[]{:S(2)}, u32[]{:S(2)}) %collective-permute-start.1) | collective-permute-done | bytes 12320 | tf_op jit(solution)/shard_map/ppermute | solution.py:804
  49.9 2.2 %shard_map.130 = (bf16[32,40,128]{2,1,0:T(8,128)(2,1)}, f32[8,32]{1,0:T(8,128)S(1)}) custom-call(s32[1]{0:T(128)} %bitcast.half_ref, f32[24,128]{1,0:T(8,128)S(1)} %get-tuple-element.42.own_ref, f32[24,128]{1,0:T(8,128)S(1)} %collective-permute-done.1.other_ref, f32[24,256]{1,0:T(8,128)S(1)} %reshape.28.taps_ref, f32[32,256]{1,0:T(8,128)S(1)} %reshape.29.modal_ref, ...), custom_call_target="tpu_custom_call" | custom-call | tf_op jit(solution)/shard_map/pallas_call | solution.py:730
  52.1 8.8 %all-to-all-start.1 = ((bf16[32,40,128]{2,1,0:T(8,128)(2,1)}), bf16[32,40,128]{2,1,0:T(8,128)(2,1)S(1)}, u32[]{:S(2)}, u32[]{:S(2)}) async-start(bf16[32,40,128]{2,1,0:T(8,128)(2,1)} %get-tuple-element.46), calls=%async_computation.1 | async-start | bytes 655360 | tf_op jit(solution)/shard_map/all_to_all | solution.py:806
  60.9 0.7 fusion
  61.6 8.9 %all-to-all-done.1.recv_ref = bf16[32,40,128]{2,1,0:T(8,128)(2,1)S(1)} async-done(((bf16[32,40,128]{2,1,0:T(8,128)(2,1)}), bf16[32,40,128]{2,1,0:T(8,128)(2,1)S(1)}, u32[]{:S(2)}, u32[]{:S(2)}) %all-to-all-start.1) | async-done | bytes 327712 | tf_op jit(solution)/shard_map/all_to_all | solution.py:806
  70.4 0.9 %shard_map.131 = (bf16[256,128]{1,0:T(8,128)(2,1)}, bf16[256,128]{1,0:T(8,128)(2,1)}, bf16[256,128]{1,0:T(8,128)(2,1)}, bf16[256,128]{1,0:T(8,128)(2,1)}, f32[3,7,256]{2,1,0:T(8,128)}) custom-call(bf16[32,40,128]{2,1,0:T(8,128)(2,1)S(1)} %all-to-all-done.1.recv_ref), custom_call_target="tpu_custom_call" | custom-call | tf_op jit(solution)/shard_map/pallas_call | solution.py:755
  (5 shorter events, 0.0 us)
Async XLA Ops:
  2.7 10.4 %copy-start.5 = (f32[4,16]{1,0:T(4,128)S(1)}, f32[4,16]{1,0:T(4,128)}, u32[]{:S(2)}) copy-start(f32[4,16]{1,0:T(4,128)} %param.11) | copy-start | bytes 772
  2.7 10.4 %copy-start.6 = (f32[4,16]{1,0:T(4,128)S(1)}, f32[4,16]{1,0:T(4,128)}, u32[]{:S(2)}) copy-start(f32[4,16]{1,0:T(4,128)} %param.12) | copy-start | bytes 772
  2.8 25.3 %all-to-all-start = ((bf16[32,32,128]{2,1,0:T(8,128)(2,1)}), bf16[32,32,128]{2,1,0:T(8,128)(2,1)S(1)}, u32[]{:S(2)}, u32[]{:S(2)}) async-start(bf16[32,32,128]{2,1,0:T(8,128)(2,1)} %shard_map.126.after_ref), calls=%async_computation | async-start | bytes 524288 | tf_op jit(solution)/shard_map/all_to_all | solution.py:796
  13.3 17.2 %collective-permute-start = (f32[4,32]{1,0:T(4,128)S(1)}, f32[4,32]{1,0:T(4,128)S(1)}, u32[]{:S(2)}, u32[]{:S(2)}) collective-permute-start(f32[4,32]{1,0:T(4,128)S(1)} %shard_map.127), channel_id=1, source_target_pairs={{0,256},{8,264},{16,272},{24,280},{32,288},{40,296},{48,304},{56,3... | collective-permute-start | bytes 1544 | tf_op jit(solution)/shard_map/ppermute | solution.py:785
  26.9 0.7 %copy-start.4 = (f32[3,7,256]{2,1,0:T(8,128)S(1)}, f32[3,7,256]{2,1,0:T(8,128)}, u32[]{:S(2)}) copy-start(f32[3,7,256]{2,1,0:T(8,128)} %param.10) | copy-start | bytes 64516
  29.2 0.7 copy-start
  29.8 0.7 copy-start.2
  30.8 0.9 %copy-start.1 = (f32[128,256]{1,0:T(8,128)S(1)}, f32[128,256]{1,0:T(8,128)}, u32[]{:S(2)}) copy-start(f32[128,256]{1,0:T(8,128)} %copy-done) | copy-start | bytes 393220
  31.7 0.9 %copy-start.3 = (f32[128,256]{1,0:T(8,128)S(1)}, f32[128,256]{1,0:T(8,128)}, u32[]{:S(2)}) copy-start(f32[128,256]{1,0:T(8,128)} %copy-done.2) | copy-start | bytes 393220
  36.7 13.2 %collective-permute-start.1 = (f32[24,128]{1,0:T(8,128)S(1)}, f32[24,128]{1,0:T(8,128)S(1)}, u32[]{:S(2)}, u32[]{:S(2)}) collective-permute-start(f32[24,128]{1,0:T(8,128)S(1)} %get-tuple-element.42.own_ref), channel_id=1, source_target_pairs={{0,256},{8,264},{16,272},{24,280},{32,288},{40,296},{48,304},{56,3... | collective-permute-start | bytes 36872 | tf_op jit(solution)/shard_map/ppermute | solution.py:804
  52.1 18.4 %all-to-all-start.1 = ((bf16[32,40,128]{2,1,0:T(8,128)(2,1)}), bf16[32,40,128]{2,1,0:T(8,128)(2,1)S(1)}, u32[]{:S(2)}, u32[]{:S(2)}) async-start(bf16[32,40,128]{2,1,0:T(8,128)(2,1)} %get-tuple-element.46), calls=%async_computation.1 | async-start | bytes 655360 | tf_op jit(solution)/shard_map/all_to_all | solution.py:806

commit v7 on v6

--- a/solution.py
+++ b/solution.py
@@ -155,13 +155,10 @@
     taps_ref,
     xt,
     hat_ref,
-    mixed,
-    gmixed,
     base,
-    upper_w,
-    lower_w,
     raw,
 ):
+    mixed, gmixed = base.at[3], base.at[4]
     chunks = recv_ref.shape[0]
     toks = recv_ref.shape[2]
     lanes = OWNED * chunks
@@ -212,46 +209,26 @@
     for stream in range(3):
         base[stream, 0:8, :] = base[stream, 0:8, :] * kept
 
-    def weigh(slot, stream):
-        for tap in range(TAPS):
-            for start in range(0, toks, block):
-                span = slice(start, start + block)
-                lo = PAD - tap + start
-                value = base[stream, span, :] * xt[stream, lo : lo + block, :]
-                upper = value.astype(jnp.bfloat16)
-                upper_w[slot + tap, span, :] = upper
-                lower_w[slot + tap, span, :] = (value - upper.astype(f32)).astype(jnp.bfloat16)
-
-    @pl.when(half == 0)
-    def _():
-        weigh(0, 1)
-        weigh(TAPS, 2)
-
-    @pl.when(half != 0)
-    def _():
-        weigh(0, 0)
-
 
 def first_kernel(
     half_ref,
     modal_ref,
     rate_ref,
     xt,
-    mixed,
-    gmixed,
     base,
-    upper_w,
-    lower_w,
-    fwd_ref,
-    bwd_ref,
+    conv_ref,
     msg_ref,
     part_y,
     part_z,
     states,
+    upper_w,
+    lower_w,
     sums,
     rows,
 ):
-    toks, lanes = mixed.shape
+    _, toks, lanes = base.shape
+    mixed, gmixed = base.at[3], base.at[4]
+    fwd_ref, bwd_ref = conv_ref.at[0], conv_ref.at[1]
     chunks = lanes // OWNED
     f32 = jnp.float32
     chunk_of, _ = lane_ids(chunks, 8)
@@ -368,14 +345,21 @@
     row_tok = lax.broadcasted_iota(jnp.int32, (toks, toks), 0).astype(f32)
     along = jnp.exp(-rate_line * (late * row_tok + early * (toks - 1.0 - row_tok)))
 
-    def respond(slot):
-        for tap in range(slot, slot + TAPS):
+    def respond(slot, stream):
+        for tap in range(TAPS):
+            for start in range(0, toks, block):
+                span = slice(start, start + block)
+                lo = PAD - tap + start
+                value = base[stream, span, :] * xt[stream, lo : lo + block, :]
+                upper = value.astype(bf16)
+                upper_w[tap, span, :] = upper
+                lower_w[tap, span, :] = (value - upper.astype(f32)).astype(bf16)
             total = (
                 jnp.dot(upper_w[tap], across_lo, preferred_element_type=f32)
                 + jnp.dot(lower_w[tap], across_hi, preferred_element_type=f32)
                 + jnp.dot(upper_w[tap], across_hi, preferred_element_type=f32)
             )
-            at = OWNED + tap
+            at = OWNED + slot + tap
             msg_ref[at : at + 1, :] = jnp.sum(total * along, axis=0, keepdims=True)
 
     span_c = chunk_of.astype(f32)
@@ -383,8 +367,8 @@
 
     @pl.when(half == 0)
     def _():
-        respond(0)
-        respond(TAPS)
+        respond(0, 1)
+        respond(TAPS, 2)
         for stream in range(4):
             lo = EDGE + 8 * stream
             rows[lo : lo + 8, :] = jnp.where(
@@ -399,7 +383,7 @@
 
     @pl.when(half != 0)
     def _():
-        respond(0)
+        respond(0, 0)
         for stream in range(4):
             lo = EDGE + 8 * stream
             rows[lo : lo + 8, :] = jnp.where(chunk_of == 0, xt[stream, PAD : 2 * PAD, :], 0.0)
@@ -426,8 +410,7 @@
     modal_ref,
     xt,
     hat_ref,
-    fwd_ref,
-    bwd_ref,
+    conv_ref,
     send_ref,
     sums_ref,
     edge0,
@@ -439,7 +422,8 @@
     grads,
     out_rows,
 ):
-    toks, lanes = fwd_ref.shape
+    _, toks, lanes = conv_ref.shape
+    fwd_ref, bwd_ref = conv_ref.at[0], conv_ref.at[1]
     chunks = lanes // OWNED
     f32 = jnp.float32
     chunk_of, _ = lane_ids(chunks, 8)
@@ -691,11 +675,7 @@
         out_shape=(
             plane(4, PAD + toks, lanes),
             plane(3, toks, lanes),
-            plane(toks, lanes),
-            plane(toks, lanes),
-            plane(3, toks, lanes),
-            plane(2 * TAPS, toks, lanes, dtype=jnp.bfloat16),
-            plane(2 * TAPS, toks, lanes, dtype=jnp.bfloat16),
+            plane(5, toks, lanes),
         ),
         scratch_shapes=[pltpu.VMEM((chunks * ROWS_IN, toks), jnp.float32)],
         cost_estimate=pl.CostEstimate(flops=2 * 10**10, bytes_accessed=1024, transcendentals=0),
@@ -703,33 +683,35 @@
     )(half, recv, taps)
 
 
-def run_first(half, modal, log_rate, xt, mixed, gmixed, base, upper_w, lower_w):
-    toks, lanes = mixed.shape
+def run_first(half, modal, log_rate, xt, base):
+    _, toks, lanes = base.shape
     f32 = jnp.float32
     vmem = pl.BlockSpec(memory_space=pltpu.VMEM)
     return pl.pallas_call(
         first_kernel,
-        in_specs=[pl.BlockSpec(memory_space=pltpu.SMEM)] + [vmem] * 8,
-        out_shape=(plane(toks, lanes), plane(toks, lanes), plane(MESSAGE, toks)),
+        in_specs=[pl.BlockSpec(memory_space=pltpu.SMEM)] + [vmem] * 4,
+        out_shape=(plane(2, toks, lanes), plane(MESSAGE, toks)),
         scratch_shapes=[
             pltpu.VMEM((2, 8 * toks, lanes // 2), f32),
             pltpu.VMEM((2, 8 * toks, lanes // 2), f32),
             pltpu.VMEM((16 * toks, lanes), f32),
+            pltpu.VMEM((TAPS, toks, lanes), jnp.bfloat16),
+            pltpu.VMEM((TAPS, toks, lanes), jnp.bfloat16),
             pltpu.VMEM((2, 8 * 24, lanes // 2), f32),
             pltpu.VMEM((COMPACT, lanes), f32),
         ],
         compiler_params=pltpu.CompilerParams(vmem_limit_bytes=VMEM_LIMIT),
-    )(half, modal, log_rate, xt, mixed, gmixed, base, upper_w, lower_w)
-
-
-def run_second(half, own, other, taps, modal, xt, hat, fwd, bwd):
-    toks, lanes = fwd.shape
+    )(half, modal, log_rate, xt, base)
+
+
+def run_second(half, own, other, taps, modal, xt, hat, conv):
+    _, toks, lanes = conv.shape
     chunks = lanes // OWNED
     f32 = jnp.float32
     vmem = pl.BlockSpec(memory_space=pltpu.VMEM)
     return pl.pallas_call(
         second_kernel,
-        in_specs=[pl.BlockSpec(memory_space=pltpu.SMEM)] + [vmem] * 8,
+        in_specs=[pl.BlockSpec(memory_space=pltpu.SMEM)] + [vmem] * 7,
         out_shape=(
             plane(chunks, ROWS_OUT, toks, dtype=jnp.bfloat16),
             plane(OWNED, 2 * MODES),
@@ -745,7 +727,7 @@
             pltpu.VMEM((chunks * ROWS_OUT, toks), f32),
         ],
         compiler_params=pltpu.CompilerParams(vmem_limit_bytes=VMEM_LIMIT),
-    )(half, own, other, taps, modal, xt, hat, fwd, bwd)
+    )(half, own, other, taps, modal, xt, hat, conv)
 
 
 def run_unpack(recv):
@@ -800,9 +782,9 @@
         half == 0, jnp.concatenate([mine, theirs]), jnp.concatenate([theirs, mine])
     )
     modal = jnp.repeat(modal_params.T, chunks, axis=1)
-    fwd, bwd, message = run_first(which, modal, modal_params[:, :MODES], xt, *inner)
+    conv, message = run_first(which, modal, modal_params[:, :MODES], xt, *inner)
     other = lax.ppermute(message, "seq", across)
-    back, sums = run_second(which, message, other, taps, modal, xt, hat, fwd, bwd)
+    back, sums = run_second(which, message, other, taps, modal, xt, hat, conv)
     final = lax.all_to_all(back, "seq", 0, 0, tiled=True, axis_index_groups=groups)
     output, grad_query, grad_key, grad_value, grad_short = run_unpack(final)
     own_modal = lax.dynamic_slice(sums, (4 * half, 0), (4, 2 * MODES))

time: 71.8 us -> 68.4 us (0.953)
  local copies, waits for them, and re-layouts: 5.03 us -> 1.91 us
  starting transfers between devices: 41.9 us -> 43.5 us
  waiting for transfers between devices: 12.9 us -> 11.4 us
    unnamed x14 -> x6, local copies, waits for them, and re-layouts: 3.84 us -> 0.72 us
    ppermute x1, starting transfers between devices: 9.08 us -> 10.7 us  [local(): other = lax.ppermute(message, 'seq', across)]
    ppermute x1, waiting for transfers between devices: 4.05 us -> 2.48 us  [local(): other = lax.ppermute(message, 'seq', across)]
  transfers between devices with their start and end apart: 4 -> 4, of which waited for: 2 -> 2; matrix products, arithmetic and copies ran while one was open for 2% -> 2% of each run, Pallas kernels for 2% -> 1%
where the time goes in v7:
time: 68.4 us; the launch traced here: 67.9 us
  starting transfers between devices  43.5 us (64%)
  waiting for transfers between devices  11.4 us (17%)
  Pallas kernels  10.2 us (15%)
  local copies, waits for them, and re-layouts  1.91 us (3%)
  between operations  0.83 us (1%)
    ppermute x1, starting transfers between devices, local(): theirs = lax.ppermute(mine, 'seq', across)  13.6 us
    ppermute x1, starting transfers between devices, local(): other = lax.ppermute(message, 'seq', across)  10.7 us
    all_to_all x1, starting transfers between devices, local(): lax.all_to_all(send, 'seq', 0, 0, tiled=True, axis_index_groups=groups)  10.4 us
    all_to_all x1, waiting for transfers between devices, local(): lax.all_to_all(back, 'seq', 0, 0, tiled=True, axis_index_groups=groups)  8.87 us
    all_to_all x1, starting transfers between devices, local(): lax.all_to_all(back, 'seq', 0, 0, tiled=True, axis_index_groups=groups)  8.81 us
    pallas_call x1, Pallas kernels, run_first(): pl.pallas_call(first_kernel, in_specs=[pl.BlockSpec(memory_space=pltpu.SM...  4.3 us
    ppermute x1, waiting for transfers between devices, local(): other = lax.ppermute(message, 'seq', across)  2.48 us
    pallas_call x1, Pallas kernels, run_second(): pl.pallas_call(second_kernel, in_specs=[pl.BlockSpec(memory_space=pltpu.S...  2.19 us
  transfers between devices with their start and end apart: 4, of which 2 were waited for; matrix products, arithmetic and copies ran while one was open for 2% of the time, Pallas kernels for 1%

profile of v7, /device:TPU:1, one launch (start us, length us, event | category | flops | bytes accessed | tf_op | source)
XLA Modules:
  0.0 67.9 jit_solution(11088542029903330993)
XLA Ops:
  0.6 2.1 %shard_map.126.after_ref = bf16[32,32,128]{2,1,0:T(8,128)(2,1)} custom-call(bf16[256,128]{1,0:T(8,128)(2,1)} %query_ref.1, bf16[256,128]{1,0:T(8,128)(2,1)} %key_ref.1, bf16[256,128]{1,0:T(8,128)(2,1)} %value_ref.1, bf16[256,128]{1,0:T(8,128)(2,1)} %grad_ref.1), custom_call_target="tpu_custom_call" | custom-call | tf_op jit(solution)/shard_map/pallas_call | solution.py:634
  2.7 0.0 copy-start.1
  2.7 0.0 copy-start.2
  2.7 10.4 %all-to-all-start = ((bf16[32,32,128]{2,1,0:T(8,128)(2,1)}), bf16[32,32,128]{2,1,0:T(8,128)(2,1)S(1)}, u32[]{:S(2)}, u32[]{:S(2)}) async-start(bf16[32,32,128]{2,1,0:T(8,128)(2,1)} %shard_map.126.after_ref), calls=%async_computation | async-start | bytes 524288 | tf_op jit(solution)/shard_map/all_to_all | solution.py:778
  13.2 0.0 copy-done.1
  13.2 0.0 copy-done.2
  13.2 0.1 pad_maximum_fusion.1.both_ref
  13.3 13.6 %collective-permute-start = (f32[4,32]{1,0:T(4,128)S(1)}, f32[4,32]{1,0:T(4,128)S(1)}, u32[]{:S(2)}, u32[]{:S(2)}) collective-permute-start(f32[4,32]{1,0:T(4,128)S(1)} %shard_map.127), channel_id=1, source_target_pairs={{0,256},{8,264},{16,272},{24,280},{32,288},{40,296},{48,304},{56,3... | collective-permute-start | bytes 1544 | tf_op jit(solution)/shard_map/ppermute | solution.py:767
  26.9 0.0 copy-start
  26.9 0.7 %copy-done = f32[3,7,256]{2,1,0:T(8,128)S(1)} copy-done((f32[3,7,256]{2,1,0:T(8,128)S(1)}, f32[3,7,256]{2,1,0:T(8,128)}, u32[]{:S(2)}) %copy-start) | copy-done | bytes 21528
  27.6 0.1 constant_dynamic-slice_fusion.2
  27.7 0.1 pad_maximum_fusion
  27.8 0.1 broadcast_in_dim.6
  27.9 0.1 reshape.28.taps_ref
  28.0 0.0 all-to-all-done.recv_ref
  28.0 0.7 %shard_map.128 = (f32[4,136,256]{2,1,0:T(8,128)S(1)}, f32[3,128,256]{2,1,0:T(8,128)S(1)}, f32[5,128,256]{2,1,0:T(8,128)S(1)}) custom-call(s32[1]{0:T(128)} %bitcast.half_ref, bf16[32,32,128]{2,1,0:T(8,128)(2,1)S(1)} %all-to-all-done.recv_ref, f32[24,256]{1,0:T(8,128)S(1)} %reshape.28.taps_ref), custom_call_target="tpu_custom_call" | custom-call | flops 20000000000 | bytes 1024 | tf_op jit(solution)/shard_map/pallas_call | solution.py:672
  28.8 0.0 collective-permute-done
  28.8 0.1 copy.17
  28.9 0.1 broadcast_in_dim.7
  29.0 0.1 reshape.29.modal_ref
  29.1 4.3 %shard_map.129 = (f32[2,128,256]{2,1,0:T(8,128)S(1)}, f32[24,128]{1,0:T(8,128)S(1)}) custom-call(s32[1]{0:T(128)} %bitcast.half_ref, f32[32,256]{1,0:T(8,128)S(1)} %reshape.29.modal_ref, f32[8,16]{1,0:T(8,128)S(1)} %bitcast.4, f32[4,136,256]{2,1,0:T(8,128)S(1)} %get-tuple-element.23.xt, f32[5,128,256]{2,1,0:T(8,128)S(1)} %get-tuple-element.24.base), custom_call_target="tpu_custom_call" | custom-call | tf_op jit(solution)/shard_map/pallas_call | solution.py:690
  33.4 10.7 %collective-permute-start.1 = (f32[24,128]{1,0:T(8,128)S(1)}, f32[24,128]{1,0:T(8,128)S(1)}, u32[]{:S(2)}, u32[]{:S(2)}) collective-permute-start(f32[24,128]{1,0:T(8,128)S(1)} %get-tuple-element.25.own_ref), channel_id=1, source_target_pairs={{0,256},{8,264},{16,272},{24,280},{32,288},{40,296},{48,304},{56,3... | collective-permute-start | bytes 36872 | tf_op jit(solution)/shard_map/ppermute | solution.py:786
  44.0 2.5 %collective-permute-done.1.other_ref = f32[24,128]{1,0:T(8,128)S(1)} collective-permute-done((f32[24,128]{1,0:T(8,128)S(1)}, f32[24,128]{1,0:T(8,128)S(1)}, u32[]{:S(2)}, u32[]{:S(2)}) %collective-permute-start.1) | collective-permute-done | bytes 12320 | tf_op jit(solution)/shard_map/ppermute | solution.py:786
  46.5 2.2 %shard_map.130 = (bf16[32,40,128]{2,1,0:T(8,128)(2,1)}, f32[8,32]{1,0:T(8,128)S(1)}) custom-call(s32[1]{0:T(128)} %bitcast.half_ref, f32[24,128]{1,0:T(8,128)S(1)} %get-tuple-element.25.own_ref, f32[24,128]{1,0:T(8,128)S(1)} %collective-permute-done.1.other_ref, f32[24,256]{1,0:T(8,128)S(1)} %reshape.28.taps_ref, f32[32,256]{1,0:T(8,128)S(1)} %reshape.29.modal_ref, ...), custom_call_target="tpu_custom_call" | custom-call | tf_op jit(solution)/shard_map/pallas_call | solution.py:712
  48.7 8.8 %all-to-all-start.1 = ((bf16[32,40,128]{2,1,0:T(8,128)(2,1)}), bf16[32,40,128]{2,1,0:T(8,128)(2,1)S(1)}, u32[]{:S(2)}, u32[]{:S(2)}) async-start(bf16[32,40,128]{2,1,0:T(8,128)(2,1)} %get-tuple-element.28), calls=%async_computation.1 | async-start | bytes 655360 | tf_op jit(solution)/shard_map/all_to_all | solution.py:788
  57.5 0.7 fusion
  58.2 8.9 %all-to-all-done.1.recv_ref = bf16[32,40,128]{2,1,0:T(8,128)(2,1)S(1)} async-done(((bf16[32,40,128]{2,1,0:T(8,128)(2,1)}), bf16[32,40,128]{2,1,0:T(8,128)(2,1)S(1)}, u32[]{:S(2)}, u32[]{:S(2)}) %all-to-all-start.1) | async-done | bytes 327712 | tf_op jit(solution)/shard_map/all_to_all | solution.py:788
  67.1 0.9 %shard_map.131 = (bf16[256,128]{1,0:T(8,128)(2,1)}, bf16[256,128]{1,0:T(8,128)(2,1)}, bf16[256,128]{1,0:T(8,128)(2,1)}, bf16[256,128]{1,0:T(8,128)(2,1)}, f32[3,7,256]{2,1,0:T(8,128)}) custom-call(bf16[32,40,128]{2,1,0:T(8,128)(2,1)S(1)} %all-to-all-done.1.recv_ref), custom_call_target="tpu_custom_call" | custom-call | tf_op jit(solution)/shard_map/pallas_call | solution.py:737
  (5 shorter events, 0.0 us)
Async XLA Ops:
  2.7 10.4 %copy-start.1 = (f32[4,16]{1,0:T(4,128)S(1)}, f32[4,16]{1,0:T(4,128)}, u32[]{:S(2)}) copy-start(f32[4,16]{1,0:T(4,128)} %param.11) | copy-start | bytes 772
  2.7 10.4 %copy-start.2 = (f32[4,16]{1,0:T(4,128)S(1)}, f32[4,16]{1,0:T(4,128)}, u32[]{:S(2)}) copy-start(f32[4,16]{1,0:T(4,128)} %param.12) | copy-start | bytes 772
  2.7 25.3 %all-to-all-start = ((bf16[32,32,128]{2,1,0:T(8,128)(2,1)}), bf16[32,32,128]{2,1,0:T(8,128)(2,1)S(1)}, u32[]{:S(2)}, u32[]{:S(2)}) async-start(bf16[32,32,128]{2,1,0:T(8,128)(2,1)} %shard_map.126.after_ref), calls=%async_computation | async-start | bytes 524288 | tf_op jit(solution)/shard_map/all_to_all | solution.py:778
  13.3 15.5 %collective-permute-start = (f32[4,32]{1,0:T(4,128)S(1)}, f32[4,32]{1,0:T(4,128)S(1)}, u32[]{:S(2)}, u32[]{:S(2)}) collective-permute-start(f32[4,32]{1,0:T(4,128)S(1)} %shard_map.127), channel_id=1, source_target_pairs={{0,256},{8,264},{16,272},{24,280},{32,288},{40,296},{48,304},{56,3... | collective-permute-start | bytes 1544 | tf_op jit(solution)/shard_map/ppermute | solution.py:767
  26.9 0.7 %copy-start = (f32[3,7,256]{2,1,0:T(8,128)S(1)}, f32[3,7,256]{2,1,0:T(8,128)}, u32[]{:S(2)}) copy-start(f32[3,7,256]{2,1,0:T(8,128)} %param.10) | copy-start | bytes 64516
  33.4 13.2 %collective-permute-start.1 = (f32[24,128]{1,0:T(8,128)S(1)}, f32[24,128]{1,0:T(8,128)S(1)}, u32[]{:S(2)}, u32[]{:S(2)}) collective-permute-start(f32[24,128]{1,0:T(8,128)S(1)} %get-tuple-element.25.own_ref), channel_id=1, source_target_pairs={{0,256},{8,264},{16,272},{24,280},{32,288},{40,296},{48,304},{56,3... | collective-permute-start | bytes 36872 | tf_op jit(solution)/shard_map/ppermute | solution.py:786
  48.7 18.4 %all-to-all-start.1 = ((bf16[32,40,128]{2,1,0:T(8,128)(2,1)}), bf16[32,40,128]{2,1,0:T(8,128)(2,1)S(1)}, u32[]{:S(2)}, u32[]{:S(2)}) async-start(bf16[32,40,128]{2,1,0:T(8,128)(2,1)} %get-tuple-element.28), calls=%async_computation.1 | async-start | bytes 655360 | tf_op jit(solution)/shard_map/all_to_all | solution.py:788

commit v8 on v7

--- a/solution.py
+++ b/solution.py
@@ -12,7 +12,7 @@
 PAD = 8
 OWNED = 8
 ROWS_IN = 4 * OWNED
-ROWS_OUT = 40
+ROWS_OUT = 36
 VMEM_LIMIT = 16 * 1024 * 1024
 
 STATE, DERIV, RSUM, KSUM, EDGE, SHORT, COMPACT = 0, 16, 32, 48, 64, 96, 128
@@ -42,16 +42,22 @@
     send_ref[...] = mixed_rows[...].reshape(send_ref.shape).astype(jnp.bfloat16)
 
 
-def unpack_kernel(recv_ref, out_ref, gq_ref, gk_ref, gv_ref, short_ref, rows, wide):
-    owners = recv_ref.shape[0]
+def unpack_kernel(
+    recv_ref, out_ref, gq_ref, gk_ref, gv_ref, short_ref, rows, wide, staged, sems
+):
+    owners = recv_ref.shape[0] // ROWS_OUT
     chans = out_ref.shape[0]
-    rows[...] = recv_ref[...].reshape(rows.shape).astype(jnp.float32)
+    rows[...] = recv_ref[...].astype(jnp.float32)
+    sends = []
     for stream, ref in enumerate((out_ref, gq_ref, gk_ref, gv_ref)):
         for chan in range(OWNED):
             wide[stream, pl.ds(first_row(chan, chans), owners, stride=4), :] = rows[
                 pl.ds(stream * OWNED + chan, owners, stride=ROWS_OUT), :
             ]
-        ref[...] = wide[stream].astype(jnp.bfloat16)
+        staged[stream] = wide[stream].astype(jnp.bfloat16)
+        send = pltpu.make_async_copy(staged.at[stream], ref, sems.at[stream])
+        send.start()
+        sends.append(send)
     for group in range(2):
         short = (
             rows[pl.ds(32 + group, owners, stride=ROWS_OUT), :]
@@ -64,6 +70,8 @@
     turned = wide[4].T
     for stream in range(3):
         short_ref[stream] = turned[stream * TAPS : (stream + 1) * TAPS, :]
+    for send in sends:
+        send.wait()
 
 
 def lane_ids(chunks, rows):
@@ -623,9 +631,7 @@
         out_rows[pl.ds(34 + group, chunks, stride=ROWS_OUT), :] = jnp.broadcast_to(
             line - upper, (chunks, toks)
         )
-    for spare in range(36, ROWS_OUT):
-        out_rows[pl.ds(spare, chunks, stride=ROWS_OUT), :] = jnp.zeros((chunks, toks), f32)
-    send_ref[...] = out_rows[...].reshape(send_ref.shape).astype(jnp.bfloat16)
+    send_ref[...] = out_rows[...].astype(jnp.bfloat16)
 
 
 def run_pack(query_in, key_in, value_in, grad_out):
@@ -713,7 +719,7 @@
         second_kernel,
         in_specs=[pl.BlockSpec(memory_space=pltpu.SMEM)] + [vmem] * 7,
         out_shape=(
-            plane(chunks, ROWS_OUT, toks, dtype=jnp.bfloat16),
+            plane(chunks * ROWS_OUT, toks, dtype=jnp.bfloat16),
             plane(OWNED, 2 * MODES),
         ),
         scratch_shapes=[
@@ -731,15 +737,20 @@
 
 
 def run_unpack(recv):
-    owners, _, toks = recv.shape
+    rows, toks = recv.shape
+    owners = rows // ROWS_OUT
     chans = OWNED * owners
     whole = jax.ShapeDtypeStruct((chans, toks), jnp.bfloat16)
     return pl.pallas_call(
         unpack_kernel,
+        out_specs=(pl.BlockSpec(memory_space=pltpu.HBM),) * 4
+        + (pl.BlockSpec(memory_space=pltpu.VMEM),),
         out_shape=(whole,) * 4 + (jax.ShapeDtypeStruct((3, TAPS, chans), jnp.float32),),
         scratch_shapes=[
             pltpu.VMEM((owners * ROWS_OUT, toks), jnp.float32),
             pltpu.VMEM((5, chans, toks), jnp.float32),
+            pltpu.VMEM((4, chans, toks), jnp.bfloat16),
+            pltpu.SemaphoreType.DMA((4,)),
         ],
         compiler_params=pltpu.CompilerParams(vmem_limit_bytes=VMEM_LIMIT),
     )(recv)
@@ -785,8 +796,9 @@
     conv, message = run_first(which, modal, modal_params[:, :MODES], xt, *inner)
     other = lax.ppermute(message, "seq", across)
     back, sums = run_second(which, message, other, taps, modal, xt, hat, conv)
-    final = lax.all_to_all(back, "seq", 0, 0, tiled=True, axis_index_groups=groups)
-    output, grad_query, grad_key, grad_value, grad_short = run_unpack(final)
+    paired = back.reshape(chunks, ROWS_OUT // 4, 4, back.shape[1])
+    final = lax.all_to_all(paired, "seq", 0, 0, tiled=True, axis_index_groups=groups)
+    output, grad_query, grad_key, grad_value, grad_short = run_unpack(final.reshape(back.shape))
     own_modal = lax.dynamic_slice(sums, (4 * half, 0), (4, 2 * MODES))
     return (
         output,

time: 68.4 us -> 68.6 us (level)
  no operation moved by 1% of the time
where the time goes in v8:
time: 68.6 us; the launch traced here: 68.2 us
  starting transfers between devices  43.5 us (63%)
  waiting for transfers between devices  11 us (16%)
  Pallas kernels  10.8 us (16%)
  local copies, waits for them, and re-layouts  1.91 us (3%)
  between operations  0.83 us (1%)
    ppermute x1, starting transfers between devices, local(): theirs = lax.ppermute(mine, 'seq', across)  13.6 us
    ppermute x1, starting transfers between devices, local(): other = lax.ppermute(message, 'seq', across)  10.7 us
    all_to_all x1, starting transfers between devices, local(): lax.all_to_all(send, 'seq', 0, 0, tiled=True, axis_index_groups=groups)  10.4 us
    all_to_all x1, starting transfers between devices, local(): lax.all_to_all(paired, 'seq', 0, 0, tiled=True, axis_index_groups=groups)  8.81 us
    all_to_all x1, waiting for transfers between devices, local(): lax.all_to_all(paired, 'seq', 0, 0, tiled=True, axis_index_groups=groups)  8.55 us
    pallas_call x1, Pallas kernels, run_first(): pl.pallas_call(first_kernel, in_specs=[pl.BlockSpec(memory_space=pltpu.SM...  4.3 us
    ppermute x1, waiting for transfers between devices, local(): other = lax.ppermute(message, 'seq', across)  2.48 us
    pallas_call x1, Pallas kernels, run_second(): pl.pallas_call(second_kernel, in_specs=[pl.BlockSpec(memory_space=pltpu.S...  2.17 us
  transfers between devices with their start and end apart: 4, of which 2 were waited for; matrix products, arithmetic and copies ran while one was open for 2% of the time, Pallas kernels for 1%

profile of v8, /device:TPU:1, one launch (start us, length us, event | category | flops | bytes accessed | tf_op | source)
XLA Modules:
  0.0 68.2 jit_solution(12548411355198647980)
XLA Ops:
  0.6 2.1 %shard_map.126.after_ref = bf16[32,32,128]{2,1,0:T(8,128)(2,1)} custom-call(bf16[256,128]{1,0:T(8,128)(2,1)} %query_ref.1, bf16[256,128]{1,0:T(8,128)(2,1)} %key_ref.1, bf16[256,128]{1,0:T(8,128)(2,1)} %value_ref.1, bf16[256,128]{1,0:T(8,128)(2,1)} %grad_ref.1), custom_call_target="tpu_custom_call" | custom-call | tf_op jit(solution)/shard_map/pallas_call | solution.py:640
  2.7 0.0 copy-start.1
  2.7 0.0 copy-start.2
  2.7 10.4 %all-to-all-start = ((bf16[32,32,128]{2,1,0:T(8,128)(2,1)}), bf16[32,32,128]{2,1,0:T(8,128)(2,1)S(1)}, u32[]{:S(2)}, u32[]{:S(2)}) async-start(bf16[32,32,128]{2,1,0:T(8,128)(2,1)} %shard_map.126.after_ref), calls=%async_computation | async-start | bytes 524288 | tf_op jit(solution)/shard_map/all_to_all | solution.py:789
  13.2 0.0 copy-done.1
  13.2 0.0 copy-done.2
  13.2 0.1 pad_maximum_fusion.1.both_ref
  13.3 13.6 %collective-permute-start = (f32[4,32]{1,0:T(4,128)S(1)}, f32[4,32]{1,0:T(4,128)S(1)}, u32[]{:S(2)}, u32[]{:S(2)}) collective-permute-start(f32[4,32]{1,0:T(4,128)S(1)} %shard_map.127), channel_id=1, source_target_pairs={{0,256},{8,264},{16,272},{24,280},{32,288},{40,296},{48,304},{56,3... | collective-permute-start | bytes 1544 | tf_op jit(solution)/shard_map/ppermute | solution.py:778
  26.9 0.0 copy-start
  26.9 0.7 %copy-done = f32[3,7,256]{2,1,0:T(8,128)S(1)} copy-done((f32[3,7,256]{2,1,0:T(8,128)S(1)}, f32[3,7,256]{2,1,0:T(8,128)}, u32[]{:S(2)}) %copy-start) | copy-done | bytes 21528
  27.6 0.1 constant_dynamic-slice_fusion.2
  27.7 0.1 pad_maximum_fusion
  27.8 0.1 broadcast_in_dim.6
  27.9 0.1 reshape.34.taps_ref
  28.0 0.0 all-to-all-done.recv_ref
  28.0 0.7 %shard_map.128 = (f32[4,136,256]{2,1,0:T(8,128)S(1)}, f32[3,128,256]{2,1,0:T(8,128)S(1)}, f32[5,128,256]{2,1,0:T(8,128)S(1)}) custom-call(s32[1]{0:T(128)} %bitcast.half_ref, bf16[32,32,128]{2,1,0:T(8,128)(2,1)S(1)} %all-to-all-done.recv_ref, f32[24,256]{1,0:T(8,128)S(1)} %reshape.34.taps_ref), custom_call_target="tpu_custom_call" | custom-call | flops 20000000000 | bytes 1024 | tf_op jit(solution)/shard_map/pallas_call | solution.py:678
  28.8 0.0 collective-permute-done
  28.8 0.1 copy.17
  28.9 0.1 broadcast_in_dim.7
  29.0 0.1 reshape.35.modal_ref
  29.1 4.3 %shard_map.129 = (f32[2,128,256]{2,1,0:T(8,128)S(1)}, f32[24,128]{1,0:T(8,128)S(1)}) custom-call(s32[1]{0:T(128)} %bitcast.half_ref, f32[32,256]{1,0:T(8,128)S(1)} %reshape.35.modal_ref, f32[8,16]{1,0:T(8,128)S(1)} %bitcast.7, f32[4,136,256]{2,1,0:T(8,128)S(1)} %get-tuple-element.23.xt, f32[5,128,256]{2,1,0:T(8,128)S(1)} %get-tuple-element.24.base), custom_call_target="tpu_custom_call" | custom-call | tf_op jit(solution)/shard_map/pallas_call | solution.py:696
  33.4 10.7 %collective-permute-start.1 = (f32[24,128]{1,0:T(8,128)S(1)}, f32[24,128]{1,0:T(8,128)S(1)}, u32[]{:S(2)}, u32[]{:S(2)}) collective-permute-start(f32[24,128]{1,0:T(8,128)S(1)} %get-tuple-element.25.own_ref), channel_id=1, source_target_pairs={{0,256},{8,264},{16,272},{24,280},{32,288},{40,296},{48,304},{56,3... | collective-permute-start | bytes 36872 | tf_op jit(solution)/shard_map/ppermute | solution.py:797
  44.0 2.5 %collective-permute-done.1.other_ref = f32[24,128]{1,0:T(8,128)S(1)} collective-permute-done((f32[24,128]{1,0:T(8,128)S(1)}, f32[24,128]{1,0:T(8,128)S(1)}, u32[]{:S(2)}, u32[]{:S(2)}) %collective-permute-start.1) | collective-permute-done | bytes 12320 | tf_op jit(solution)/shard_map/ppermute | solution.py:797
  46.5 2.2 %shard_map.130 = (bf16[1152,128]{1,0:T(8,128)(2,1)}, f32[8,32]{1,0:T(8,128)S(1)}) custom-call(s32[1]{0:T(128)} %bitcast.half_ref, f32[24,128]{1,0:T(8,128)S(1)} %get-tuple-element.25.own_ref, f32[24,128]{1,0:T(8,128)S(1)} %collective-permute-done.1.other_ref, f32[24,256]{1,0:T(8,128)S(1)} %reshape.34.taps_ref, f32[32,256]{1,0:T(8,128)S(1)} %reshape.35.modal_ref, ...), custom_call_target="tpu_custom_call" | custom-call | tf_op jit(solution)/shard_map/pallas_call | solution.py:718
  48.7 8.8 %all-to-all-start.1 = ((bf16[32,9,4,128]{3,2,1,0:T(4,128)(2,1)}), bf16[32,9,4,128]{3,2,1,0:T(4,128)(2,1)S(1)}, u32[]{:S(2)}, u32[]{:S(2)}) async-start(bf16[32,9,4,128]{3,2,1,0:T(4,128)(2,1)} %bitcast.2), calls=%async_computation.1 | async-start | bytes 589824 | tf_op jit(solution)/shard_map/all_to_all | solution.py:800
  57.5 0.7 fusion
  58.2 8.5 %all-to-all-done.1 = bf16[32,9,4,128]{3,2,1,0:T(4,128)(2,1)S(1)} async-done(((bf16[32,9,4,128]{3,2,1,0:T(4,128)(2,1)}), bf16[32,9,4,128]{3,2,1,0:T(4,128)(2,1)S(1)}, u32[]{:S(2)}, u32[]{:S(2)}) %all-to-all-start.1) | async-done | bytes 294944 | tf_op jit(solution)/shard_map/all_to_all | solution.py:800
  66.7 1.5 %shard_map.131 = (bf16[256,128]{1,0:T(8,128)(2,1)}, bf16[256,128]{1,0:T(8,128)(2,1)}, bf16[256,128]{1,0:T(8,128)(2,1)}, bf16[256,128]{1,0:T(8,128)(2,1)}, f32[3,7,256]{2,1,0:T(8,128)}) custom-call(bf16[1152,128]{1,0:T(8,128)(2,1)S(1)} %bitcast.5), custom_call_target="tpu_custom_call" | custom-call | tf_op jit(solution)/shard_map/pallas_call | solution.py:744
  (5 shorter events, 0.0 us)
Async XLA Ops:
  2.7 10.4 %copy-start.1 = (f32[4,16]{1,0:T(4,128)S(1)}, f32[4,16]{1,0:T(4,128)}, u32[]{:S(2)}) copy-start(f32[4,16]{1,0:T(4,128)} %param.11) | copy-start | bytes 772
  2.7 10.4 %copy-start.2 = (f32[4,16]{1,0:T(4,128)S(1)}, f32[4,16]{1,0:T(4,128)}, u32[]{:S(2)}) copy-start(f32[4,16]{1,0:T(4,128)} %param.12) | copy-start | bytes 772
  2.7 25.3 %all-to-all-start = ((bf16[32,32,128]{2,1,0:T(8,128)(2,1)}), bf16[32,32,128]{2,1,0:T(8,128)(2,1)S(1)}, u32[]{:S(2)}, u32[]{:S(2)}) async-start(bf16[32,32,128]{2,1,0:T(8,128)(2,1)} %shard_map.126.after_ref), calls=%async_computation | async-start | bytes 524288 | tf_op jit(solution)/shard_map/all_to_all | solution.py:789
  13.3 15.5 %collective-permute-start = (f32[4,32]{1,0:T(4,128)S(1)}, f32[4,32]{1,0:T(4,128)S(1)}, u32[]{:S(2)}, u32[]{:S(2)}) collective-permute-start(f32[4,32]{1,0:T(4,128)S(1)} %shard_map.127), channel_id=1, source_target_pairs={{0,256},{8,264},{16,272},{24,280},{32,288},{40,296},{48,304},{56,3... | collective-permute-start | bytes 1544 | tf_op jit(solution)/shard_map/ppermute | solution.py:778
  26.9 0.7 %copy-start = (f32[3,7,256]{2,1,0:T(8,128)S(1)}, f32[3,7,256]{2,1,0:T(8,128)}, u32[]{:S(2)}) copy-start(f32[3,7,256]{2,1,0:T(8,128)} %param.10) | copy-start | bytes 64516
  33.4 13.2 %collective-permute-start.1 = (f32[24,128]{1,0:T(8,128)S(1)}, f32[24,128]{1,0:T(8,128)S(1)}, u32[]{:S(2)}, u32[]{:S(2)}) collective-permute-start(f32[24,128]{1,0:T(8,128)S(1)} %get-tuple-element.25.own_ref), channel_id=1, source_target_pairs={{0,256},{8,264},{16,272},{24,280},{32,288},{40,296},{48,304},{56,3... | collective-permute-start | bytes 36872 | tf_op jit(solution)/shard_map/ppermute | solution.py:797
  48.7 18.0 %all-to-all-start.1 = ((bf16[32,9,4,128]{3,2,1,0:T(4,128)(2,1)}), bf16[32,9,4,128]{3,2,1,0:T(4,128)(2,1)S(1)}, u32[]{:S(2)}, u32[]{:S(2)}) async-start(bf16[32,9,4,128]{3,2,1,0:T(4,128)(2,1)} %bitcast.2), calls=%async_computation.1 | async-start | bytes 589824 | tf_op jit(solution)/shard_map/all_to_all | solution.py:800

commit v9 on v8

--- a/solution.py
+++ b/solution.py
@@ -42,22 +42,16 @@
     send_ref[...] = mixed_rows[...].reshape(send_ref.shape).astype(jnp.bfloat16)
 
 
-def unpack_kernel(
-    recv_ref, out_ref, gq_ref, gk_ref, gv_ref, short_ref, rows, wide, staged, sems
-):
+def unpack_kernel(recv_ref, out_ref, gq_ref, gk_ref, gv_ref, short_ref, rows, wide):
     owners = recv_ref.shape[0] // ROWS_OUT
     chans = out_ref.shape[0]
     rows[...] = recv_ref[...].astype(jnp.float32)
-    sends = []
     for stream, ref in enumerate((out_ref, gq_ref, gk_ref, gv_ref)):
         for chan in range(OWNED):
             wide[stream, pl.ds(first_row(chan, chans), owners, stride=4), :] = rows[
                 pl.ds(stream * OWNED + chan, owners, stride=ROWS_OUT), :
             ]
-        staged[stream] = wide[stream].astype(jnp.bfloat16)
-        send = pltpu.make_async_copy(staged.at[stream], ref, sems.at[stream])
-        send.start()
-        sends.append(send)
+        ref[...] = wide[stream].astype(jnp.bfloat16)
     for group in range(2):
         short = (
             rows[pl.ds(32 + group, owners, stride=ROWS_OUT), :]
@@ -70,8 +64,6 @@
     turned = wide[4].T
     for stream in range(3):
         short_ref[stream] = turned[stream * TAPS : (stream + 1) * TAPS, :]
-    for send in sends:
-        send.wait()
 
 
 def lane_ids(chunks, rows):
@@ -743,14 +735,10 @@
     whole = jax.ShapeDtypeStruct((chans, toks), jnp.bfloat16)
     return pl.pallas_call(
         unpack_kernel,
-        out_specs=(pl.BlockSpec(memory_space=pltpu.HBM),) * 4
-        + (pl.BlockSpec(memory_space=pltpu.VMEM),),
         out_shape=(whole,) * 4 + (jax.ShapeDtypeStruct((3, TAPS, chans), jnp.float32),),
         scratch_shapes=[
             pltpu.VMEM((owners * ROWS_OUT, toks), jnp.float32),
             pltpu.VMEM((5, chans, toks), jnp.float32),
-            pltpu.VMEM((4, chans, toks), jnp.bfloat16),
-            pltpu.SemaphoreType.DMA((4,)),
         ],
         compiler_params=pltpu.CompilerParams(vmem_limit_bytes=VMEM_LIMIT),
     )(recv)

time: 68.6 us -> 68 us (level)
  Pallas kernels: 10.8 us -> 10.1 us
where the time goes in v9:
time: 68 us; the launch traced here: 67.5 us
  starting transfers between devices  43.5 us (64%)
  waiting for transfers between devices  11 us (16%)
  Pallas kernels  10.1 us (15%)
  local copies, waits for them, and re-layouts  1.91 us (3%)
  between operations  0.83 us (1%)
    ppermute x1, starting transfers between devices, local(): theirs = lax.ppermute(mine, 'seq', across)  13.6 us
    ppermute x1, starting transfers between devices, local(): other = lax.ppermute(message, 'seq', across)  10.7 us
    all_to_all x1, starting transfers between devices, local(): lax.all_to_all(send, 'seq', 0, 0, tiled=True, axis_index_groups=groups)  10.4 us
    all_to_all x1, starting transfers between devices, local(): lax.all_to_all(paired, 'seq', 0, 0, tiled=True, axis_index_groups=groups)  8.81 us
    all_to_all x1, waiting for transfers between devices, local(): lax.all_to_all(paired, 'seq', 0, 0, tiled=True, axis_index_groups=groups)  8.55 us
    pallas_call x1, Pallas kernels, run_first(): pl.pallas_call(first_kernel, in_specs=[pl.BlockSpec(memory_space=pltpu.SM...  4.3 us
    ppermute x1, waiting for transfers between devices, local(): other = lax.ppermute(message, 'seq', across)  2.48 us
    pallas_call x1, Pallas kernels, run_second(): pl.pallas_call(second_kernel, in_specs=[pl.BlockSpec(memory_space=pltpu.S...  2.17 us
  transfers between devices with their start and end apart: 4, of which 2 were waited for; matrix products, arithmetic and copies ran while one was open for 2% of the time, Pallas kernels for 1%

profile of v9, /device:TPU:1, one launch (start us, length us, event | category | flops | bytes accessed | tf_op | source)
XLA Modules:
  0.0 67.5 jit_solution(580158525240175156)
XLA Ops:
  0.6 2.1 %shard_map.126.after_ref = bf16[32,32,128]{2,1,0:T(8,128)(2,1)} custom-call(bf16[256,128]{1,0:T(8,128)(2,1)} %query_ref.1, bf16[256,128]{1,0:T(8,128)(2,1)} %key_ref.1, bf16[256,128]{1,0:T(8,128)(2,1)} %value_ref.1, bf16[256,128]{1,0:T(8,128)(2,1)} %grad_ref.1), custom_call_target="tpu_custom_call" | custom-call | tf_op jit(solution)/shard_map/pallas_call | solution.py:632
  2.7 0.0 copy-start.1
  2.7 0.0 copy-start.2
  2.7 10.4 %all-to-all-start = ((bf16[32,32,128]{2,1,0:T(8,128)(2,1)}), bf16[32,32,128]{2,1,0:T(8,128)(2,1)S(1)}, u32[]{:S(2)}, u32[]{:S(2)}) async-start(bf16[32,32,128]{2,1,0:T(8,128)(2,1)} %shard_map.126.after_ref), calls=%async_computation | async-start | bytes 524288 | tf_op jit(solution)/shard_map/all_to_all | solution.py:777
  13.2 0.0 copy-done.1
  13.2 0.0 copy-done.2
  13.2 0.1 pad_maximum_fusion.1.both_ref
  13.3 13.6 %collective-permute-start = (f32[4,32]{1,0:T(4,128)S(1)}, f32[4,32]{1,0:T(4,128)S(1)}, u32[]{:S(2)}, u32[]{:S(2)}) collective-permute-start(f32[4,32]{1,0:T(4,128)S(1)} %shard_map.127), channel_id=1, source_target_pairs={{0,256},{8,264},{16,272},{24,280},{32,288},{40,296},{48,304},{56,3... | collective-permute-start | bytes 1544 | tf_op jit(solution)/shard_map/ppermute | solution.py:766
  26.9 0.0 copy-start
  26.9 0.7 %copy-done = f32[3,7,256]{2,1,0:T(8,128)S(1)} copy-done((f32[3,7,256]{2,1,0:T(8,128)S(1)}, f32[3,7,256]{2,1,0:T(8,128)}, u32[]{:S(2)}) %copy-start) | copy-done | bytes 21528
  27.6 0.1 constant_dynamic-slice_fusion.2
  27.7 0.1 pad_maximum_fusion
  27.8 0.1 broadcast_in_dim.6
  27.9 0.1 reshape.34.taps_ref
  28.0 0.0 all-to-all-done.recv_ref
  28.0 0.7 %shard_map.128 = (f32[4,136,256]{2,1,0:T(8,128)S(1)}, f32[3,128,256]{2,1,0:T(8,128)S(1)}, f32[5,128,256]{2,1,0:T(8,128)S(1)}) custom-call(s32[1]{0:T(128)} %bitcast.half_ref, bf16[32,32,128]{2,1,0:T(8,128)(2,1)S(1)} %all-to-all-done.recv_ref, f32[24,256]{1,0:T(8,128)S(1)} %reshape.34.taps_ref), custom_call_target="tpu_custom_call" | custom-call | flops 20000000000 | bytes 1024 | tf_op jit(solution)/shard_map/pallas_call | solution.py:670
  28.8 0.0 collective-permute-done
  28.8 0.1 copy.17
  28.9 0.1 broadcast_in_dim.7
  29.0 0.1 reshape.35.modal_ref
  29.1 4.3 %shard_map.129 = (f32[2,128,256]{2,1,0:T(8,128)S(1)}, f32[24,128]{1,0:T(8,128)S(1)}) custom-call(s32[1]{0:T(128)} %bitcast.half_ref, f32[32,256]{1,0:T(8,128)S(1)} %reshape.35.modal_ref, f32[8,16]{1,0:T(8,128)S(1)} %bitcast.7, f32[4,136,256]{2,1,0:T(8,128)S(1)} %get-tuple-element.23.xt, f32[5,128,256]{2,1,0:T(8,128)S(1)} %get-tuple-element.24.base), custom_call_target="tpu_custom_call" | custom-call | tf_op jit(solution)/shard_map/pallas_call | solution.py:688
  33.4 10.7 %collective-permute-start.1 = (f32[24,128]{1,0:T(8,128)S(1)}, f32[24,128]{1,0:T(8,128)S(1)}, u32[]{:S(2)}, u32[]{:S(2)}) collective-permute-start(f32[24,128]{1,0:T(8,128)S(1)} %get-tuple-element.25.own_ref), channel_id=1, source_target_pairs={{0,256},{8,264},{16,272},{24,280},{32,288},{40,296},{48,304},{56,3... | collective-permute-start | bytes 36872 | tf_op jit(solution)/shard_map/ppermute | solution.py:785
  44.0 2.5 %collective-permute-done.1.other_ref = f32[24,128]{1,0:T(8,128)S(1)} collective-permute-done((f32[24,128]{1,0:T(8,128)S(1)}, f32[24,128]{1,0:T(8,128)S(1)}, u32[]{:S(2)}, u32[]{:S(2)}) %collective-permute-start.1) | collective-permute-done | bytes 12320 | tf_op jit(solution)/shard_map/ppermute | solution.py:785
  46.5 2.2 %shard_map.130 = (bf16[1152,128]{1,0:T(8,128)(2,1)}, f32[8,32]{1,0:T(8,128)S(1)}) custom-call(s32[1]{0:T(128)} %bitcast.half_ref, f32[24,128]{1,0:T(8,128)S(1)} %get-tuple-element.25.own_ref, f32[24,128]{1,0:T(8,128)S(1)} %collective-permute-done.1.other_ref, f32[24,256]{1,0:T(8,128)S(1)} %reshape.34.taps_ref, f32[32,256]{1,0:T(8,128)S(1)} %reshape.35.modal_ref, ...), custom_call_target="tpu_custom_call" | custom-call | tf_op jit(solution)/shard_map/pallas_call | solution.py:710
  48.7 8.8 %all-to-all-start.1 = ((bf16[32,9,4,128]{3,2,1,0:T(4,128)(2,1)}), bf16[32,9,4,128]{3,2,1,0:T(4,128)(2,1)S(1)}, u32[]{:S(2)}, u32[]{:S(2)}) async-start(bf16[32,9,4,128]{3,2,1,0:T(4,128)(2,1)} %bitcast.2), calls=%async_computation.1 | async-start | bytes 589824 | tf_op jit(solution)/shard_map/all_to_all | solution.py:788
  57.5 0.7 fusion
  58.2 8.5 %all-to-all-done.1 = bf16[32,9,4,128]{3,2,1,0:T(4,128)(2,1)S(1)} async-done(((bf16[32,9,4,128]{3,2,1,0:T(4,128)(2,1)}), bf16[32,9,4,128]{3,2,1,0:T(4,128)(2,1)S(1)}, u32[]{:S(2)}, u32[]{:S(2)}) %all-to-all-start.1) | async-done | bytes 294944 | tf_op jit(solution)/shard_map/all_to_all | solution.py:788
  66.7 0.8 %shard_map.131 = (bf16[256,128]{1,0:T(8,128)(2,1)}, bf16[256,128]{1,0:T(8,128)(2,1)}, bf16[256,128]{1,0:T(8,128)(2,1)}, bf16[256,128]{1,0:T(8,128)(2,1)}, f32[3,7,256]{2,1,0:T(8,128)}) custom-call(bf16[1152,128]{1,0:T(8,128)(2,1)S(1)} %bitcast.5), custom_call_target="tpu_custom_call" | custom-call | tf_op jit(solution)/shard_map/pallas_call | solution.py:736
  (5 shorter events, 0.0 us)
Async XLA Ops:
  2.7 10.4 %copy-start.1 = (f32[4,16]{1,0:T(4,128)S(1)}, f32[4,16]{1,0:T(4,128)}, u32[]{:S(2)}) copy-start(f32[4,16]{1,0:T(4,128)} %param.11) | copy-start | bytes 772
  2.7 10.4 %copy-start.2 = (f32[4,16]{1,0:T(4,128)S(1)}, f32[4,16]{1,0:T(4,128)}, u32[]{:S(2)}) copy-start(f32[4,16]{1,0:T(4,128)} %param.12) | copy-start | bytes 772
  2.7 25.3 %all-to-all-start = ((bf16[32,32,128]{2,1,0:T(8,128)(2,1)}), bf16[32,32,128]{2,1,0:T(8,128)(2,1)S(1)}, u32[]{:S(2)}, u32[]{:S(2)}) async-start(bf16[32,32,128]{2,1,0:T(8,128)(2,1)} %shard_map.126.after_ref), calls=%async_computation | async-start | bytes 524288 | tf_op jit(solution)/shard_map/all_to_all | solution.py:777
  13.3 15.5 %collective-permute-start = (f32[4,32]{1,0:T(4,128)S(1)}, f32[4,32]{1,0:T(4,128)S(1)}, u32[]{:S(2)}, u32[]{:S(2)}) collective-permute-start(f32[4,32]{1,0:T(4,128)S(1)} %shard_map.127), channel_id=1, source_target_pairs={{0,256},{8,264},{16,272},{24,280},{32,288},{40,296},{48,304},{56,3... | collective-permute-start | bytes 1544 | tf_op jit(solution)/shard_map/ppermute | solution.py:766
  26.9 0.7 %copy-start = (f32[3,7,256]{2,1,0:T(8,128)S(1)}, f32[3,7,256]{2,1,0:T(8,128)}, u32[]{:S(2)}) copy-start(f32[3,7,256]{2,1,0:T(8,128)} %param.10) | copy-start | bytes 64516
  33.4 13.2 %collective-permute-start.1 = (f32[24,128]{1,0:T(8,128)S(1)}, f32[24,128]{1,0:T(8,128)S(1)}, u32[]{:S(2)}, u32[]{:S(2)}) collective-permute-start(f32[24,128]{1,0:T(8,128)S(1)} %get-tuple-element.25.own_ref), channel_id=1, source_target_pairs={{0,256},{8,264},{16,272},{24,280},{32,288},{40,296},{48,304},{56,3... | collective-permute-start | bytes 36872 | tf_op jit(solution)/shard_map/ppermute | solution.py:785
  48.7 18.0 %all-to-all-start.1 = ((bf16[32,9,4,128]{3,2,1,0:T(4,128)(2,1)}), bf16[32,9,4,128]{3,2,1,0:T(4,128)(2,1)S(1)}, u32[]{:S(2)}, u32[]{:S(2)}) async-start(bf16[32,9,4,128]{3,2,1,0:T(4,128)(2,1)} %bitcast.2), calls=%async_computation.1 | async-start | bytes 589824 | tf_op jit(solution)/shard_map/all_to_all | solution.py:788

commit v10 on v9

--- a/solution.py
+++ b/solution.py
@@ -287,9 +287,15 @@
             decay[1] * d1 + h1,
         )
 
-    _, _, r0, r1, d0, d1 = lax.fori_loop(
-        0, toks, forward_body, (start_h[0], start_h[1]) + (zero,) * 4, unroll=16
-    )
+    def forward(lagged):
+        def body(tok, carry):
+            out = forward_body(tok, carry)
+            return out if lagged else out[:4] + carry[4:]
+
+        first = (start_h[0], start_h[1]) + (zero,) * 4
+        return lax.fori_loop(0, toks, body, first, unroll=16)[2:]
+
+    r0, r1, d0, d1 = lax.cond(half == 0, lambda: forward(True), lambda: forward(False))
 
     def backward_body(step_index, carry):
         p0, p1, k0, k1, c0, c1 = carry

time: 68 us -> 68 us (level)
  no operation moved by 1% of the time
where the time goes in v10:
time: 68 us; the launch traced here: 67.5 us
  starting transfers between devices  43.4 us (64%)
  waiting for transfers between devices  11.2 us (16%)
  Pallas kernels  10.1 us (15%)
  local copies, waits for them, and re-layouts  1.91 us (3%)
  between operations  0.83 us (1%)
    ppermute x1, starting transfers between devices, local(): theirs = lax.ppermute(mine, 'seq', across)  13.6 us
    ppermute x1, starting transfers between devices, local(): other = lax.ppermute(message, 'seq', across)  10.5 us
    all_to_all x1, starting transfers between devices, local(): lax.all_to_all(send, 'seq', 0, 0, tiled=True, axis_index_groups=groups)  10.4 us
    all_to_all x1, starting transfers between devices, local(): lax.all_to_all(paired, 'seq', 0, 0, tiled=True, axis_index_groups=groups)  8.81 us
    all_to_all x1, waiting for transfers between devices, local(): lax.all_to_all(paired, 'seq', 0, 0, tiled=True, axis_index_groups=groups)  8.55 us
    pallas_call x1, Pallas kernels, run_first(): pl.pallas_call(first_kernel, in_specs=[pl.BlockSpec(memory_space=pltpu.SM...  4.3 us
    ppermute x1, waiting for transfers between devices, local(): other = lax.ppermute(message, 'seq', across)  2.61 us
    pallas_call x1, Pallas kernels, run_second(): pl.pallas_call(second_kernel, in_specs=[pl.BlockSpec(memory_space=pltpu.S...  2.17 us
  transfers between devices with their start and end apart: 4, of which 2 were waited for; matrix products, arithmetic and copies ran while one was open for 2% of the time, Pallas kernels for 1%

profile of v10, /device:TPU:1, one launch (start us, length us, event | category | flops | bytes accessed | tf_op | source)
XLA Modules:
  0.0 67.5 jit_solution(14230814742278745444)
XLA Ops:
  0.6 2.1 %shard_map.126.after_ref = bf16[32,32,128]{2,1,0:T(8,128)(2,1)} custom-call(bf16[256,128]{1,0:T(8,128)(2,1)} %query_ref.1, bf16[256,128]{1,0:T(8,128)(2,1)} %key_ref.1, bf16[256,128]{1,0:T(8,128)(2,1)} %value_ref.1, bf16[256,128]{1,0:T(8,128)(2,1)} %grad_ref.1), custom_call_target="tpu_custom_call" | custom-call | tf_op jit(solution)/shard_map/pallas_call | solution.py:638
  2.7 0.0 copy-start.1
  2.7 0.0 copy-start.2
  2.7 10.4 %all-to-all-start = ((bf16[32,32,128]{2,1,0:T(8,128)(2,1)}), bf16[32,32,128]{2,1,0:T(8,128)(2,1)S(1)}, u32[]{:S(2)}, u32[]{:S(2)}) async-start(bf16[32,32,128]{2,1,0:T(8,128)(2,1)} %shard_map.126.after_ref), calls=%async_computation | async-start | bytes 524288 | tf_op jit(solution)/shard_map/all_to_all | solution.py:783
  13.2 0.0 copy-done.1
  13.2 0.0 copy-done.2
  13.2 0.1 pad_maximum_fusion.1.both_ref
  13.3 13.6 %collective-permute-start = (f32[4,32]{1,0:T(4,128)S(1)}, f32[4,32]{1,0:T(4,128)S(1)}, u32[]{:S(2)}, u32[]{:S(2)}) collective-permute-start(f32[4,32]{1,0:T(4,128)S(1)} %shard_map.127), channel_id=1, source_target_pairs={{0,256},{8,264},{16,272},{24,280},{32,288},{40,296},{48,304},{56,3... | collective-permute-start | bytes 1544 | tf_op jit(solution)/shard_map/ppermute | solution.py:772
  26.9 0.0 copy-start
  26.9 0.7 %copy-done = f32[3,7,256]{2,1,0:T(8,128)S(1)} copy-done((f32[3,7,256]{2,1,0:T(8,128)S(1)}, f32[3,7,256]{2,1,0:T(8,128)}, u32[]{:S(2)}) %copy-start) | copy-done | bytes 21528
  27.6 0.1 constant_dynamic-slice_fusion.2
  27.7 0.1 pad_maximum_fusion
  27.8 0.1 broadcast_in_dim.6
  27.9 0.1 reshape.34.taps_ref
  28.0 0.0 all-to-all-done.recv_ref
  28.0 0.7 %shard_map.128 = (f32[4,136,256]{2,1,0:T(8,128)S(1)}, f32[3,128,256]{2,1,0:T(8,128)S(1)}, f32[5,128,256]{2,1,0:T(8,128)S(1)}) custom-call(s32[1]{0:T(128)} %bitcast.half_ref, bf16[32,32,128]{2,1,0:T(8,128)(2,1)S(1)} %all-to-all-done.recv_ref, f32[24,256]{1,0:T(8,128)S(1)} %reshape.34.taps_ref), custom_call_target="tpu_custom_call" | custom-call | flops 20000000000 | bytes 1024 | tf_op jit(solution)/shard_map/pallas_call | solution.py:676
  28.8 0.0 collective-permute-done
  28.8 0.1 copy.17
  28.9 0.1 broadcast_in_dim.7
  29.0 0.1 reshape.35.modal_ref
  29.1 4.3 %shard_map.129 = (f32[2,128,256]{2,1,0:T(8,128)S(1)}, f32[24,128]{1,0:T(8,128)S(1)}) custom-call(s32[1]{0:T(128)} %bitcast.half_ref, f32[32,256]{1,0:T(8,128)S(1)} %reshape.35.modal_ref, f32[8,16]{1,0:T(8,128)S(1)} %bitcast.7, f32[4,136,256]{2,1,0:T(8,128)S(1)} %get-tuple-element.23.xt, f32[5,128,256]{2,1,0:T(8,128)S(1)} %get-tuple-element.24.base), custom_call_target="tpu_custom_call" | custom-call | tf_op jit(solution)/shard_map/pallas_call | solution.py:694
  33.4 10.5 %collective-permute-start.1 = (f32[24,128]{1,0:T(8,128)S(1)}, f32[24,128]{1,0:T(8,128)S(1)}, u32[]{:S(2)}, u32[]{:S(2)}) collective-permute-start(f32[24,128]{1,0:T(8,128)S(1)} %get-tuple-element.25.own_ref), channel_id=1, source_target_pairs={{0,256},{8,264},{16,272},{24,280},{32,288},{40,296},{48,304},{56,3... | collective-permute-start | bytes 36872 | tf_op jit(solution)/shard_map/ppermute | solution.py:791
  43.9 2.6 %collective-permute-done.1.other_ref = f32[24,128]{1,0:T(8,128)S(1)} collective-permute-done((f32[24,128]{1,0:T(8,128)S(1)}, f32[24,128]{1,0:T(8,128)S(1)}, u32[]{:S(2)}, u32[]{:S(2)}) %collective-permute-start.1) | collective-permute-done | bytes 12320 | tf_op jit(solution)/shard_map/ppermute | solution.py:791
  46.5 2.2 %shard_map.130 = (bf16[1152,128]{1,0:T(8,128)(2,1)}, f32[8,32]{1,0:T(8,128)S(1)}) custom-call(s32[1]{0:T(128)} %bitcast.half_ref, f32[24,128]{1,0:T(8,128)S(1)} %get-tuple-element.25.own_ref, f32[24,128]{1,0:T(8,128)S(1)} %collective-permute-done.1.other_ref, f32[24,256]{1,0:T(8,128)S(1)} %reshape.34.taps_ref, f32[32,256]{1,0:T(8,128)S(1)} %reshape.35.modal_ref, ...), custom_call_target="tpu_custom_call" | custom-call | tf_op jit(solution)/shard_map/pallas_call | solution.py:716
  48.7 8.8 %all-to-all-start.1 = ((bf16[32,9,4,128]{3,2,1,0:T(4,128)(2,1)}), bf16[32,9,4,128]{3,2,1,0:T(4,128)(2,1)S(1)}, u32[]{:S(2)}, u32[]{:S(2)}) async-start(bf16[32,9,4,128]{3,2,1,0:T(4,128)(2,1)} %bitcast.2), calls=%async_computation.1 | async-start | bytes 589824 | tf_op jit(solution)/shard_map/all_to_all | solution.py:794
  57.5 0.7 fusion
  58.2 8.5 %all-to-all-done.1 = bf16[32,9,4,128]{3,2,1,0:T(4,128)(2,1)S(1)} async-done(((bf16[32,9,4,128]{3,2,1,0:T(4,128)(2,1)}), bf16[32,9,4,128]{3,2,1,0:T(4,128)(2,1)S(1)}, u32[]{:S(2)}, u32[]{:S(2)}) %all-to-all-start.1) | async-done | bytes 294944 | tf_op jit(solution)/shard_map/all_to_all | solution.py:794
  66.7 0.8 %shard_map.131 = (bf16[256,128]{1,0:T(8,128)(2,1)}, bf16[256,128]{1,0:T(8,128)(2,1)}, bf16[256,128]{1,0:T(8,128)(2,1)}, bf16[256,128]{1,0:T(8,128)(2,1)}, f32[3,7,256]{2,1,0:T(8,128)}) custom-call(bf16[1152,128]{1,0:T(8,128)(2,1)S(1)} %bitcast.5), custom_call_target="tpu_custom_call" | custom-call | tf_op jit(solution)/shard_map/pallas_call | solution.py:742
  (5 shorter events, 0.0 us)
Async XLA Ops:
  2.7 10.4 %copy-start.1 = (f32[4,16]{1,0:T(4,128)S(1)}, f32[4,16]{1,0:T(4,128)}, u32[]{:S(2)}) copy-start(f32[4,16]{1,0:T(4,128)} %param.11) | copy-start | bytes 772
  2.7 10.4 %copy-start.2 = (f32[4,16]{1,0:T(4,128)S(1)}, f32[4,16]{1,0:T(4,128)}, u32[]{:S(2)}) copy-start(f32[4,16]{1,0:T(4,128)} %param.12) | copy-start | bytes 772
  2.7 25.3 %all-to-all-start = ((bf16[32,32,128]{2,1,0:T(8,128)(2,1)}), bf16[32,32,128]{2,1,0:T(8,128)(2,1)S(1)}, u32[]{:S(2)}, u32[]{:S(2)}) async-start(bf16[32,32,128]{2,1,0:T(8,128)(2,1)} %shard_map.126.after_ref), calls=%async_computation | async-start | bytes 524288 | tf_op jit(solution)/shard_map/all_to_all | solution.py:783
  13.3 15.5 %collective-permute-start = (f32[4,32]{1,0:T(4,128)S(1)}, f32[4,32]{1,0:T(4,128)S(1)}, u32[]{:S(2)}, u32[]{:S(2)}) collective-permute-start(f32[4,32]{1,0:T(4,128)S(1)} %shard_map.127), channel_id=1, source_target_pairs={{0,256},{8,264},{16,272},{24,280},{32,288},{40,296},{48,304},{56,3... | collective-permute-start | bytes 1544 | tf_op jit(solution)/shard_map/ppermute | solution.py:772
  26.9 0.7 %copy-start = (f32[3,7,256]{2,1,0:T(8,128)S(1)}, f32[3,7,256]{2,1,0:T(8,128)}, u32[]{:S(2)}) copy-start(f32[3,7,256]{2,1,0:T(8,128)} %param.10) | copy-start | bytes 64516
  33.4 13.2 %collective-permute-start.1 = (f32[24,128]{1,0:T(8,128)S(1)}, f32[24,128]{1,0:T(8,128)S(1)}, u32[]{:S(2)}, u32[]{:S(2)}) collective-permute-start(f32[24,128]{1,0:T(8,128)S(1)} %get-tuple-element.25.own_ref), channel_id=1, source_target_pairs={{0,256},{8,264},{16,272},{24,280},{32,288},{40,296},{48,304},{56,3... | collective-permute-start | bytes 36872 | tf_op jit(solution)/shard_map/ppermute | solution.py:791
  48.7 18.0 %all-to-all-start.1 = ((bf16[32,9,4,128]{3,2,1,0:T(4,128)(2,1)}), bf16[32,9,4,128]{3,2,1,0:T(4,128)(2,1)S(1)}, u32[]{:S(2)}, u32[]{:S(2)}) async-start(bf16[32,9,4,128]{3,2,1,0:T(4,128)(2,1)} %bitcast.2), calls=%async_computation.1 | async-start | bytes 589824 | tf_op jit(solution)/shard_map/all_to_all | solution.py:794
